TPU v7x, 32 devices: a whole 2x2x4 slice. The times are simulated.
32 devices in a mesh: fsdp: 8 (over z, core), ctx: 2 (over y), tp: 2 (over x).
Axes of the slice: x: 2, y: 2, z: 4, core: 2. Of those that a mesh axis runs over, the one named last changes fastest.
Arguments:
- inputs: bfloat16 [8, 1056, 1024], P('fsdp', 'ctx'), may hold values from -6 to 6
- lengths: int32 [8, 2], P('fsdp'), may hold values from 1 to 528, 1025 in all within a row
- first_gain: bfloat16 [1024], P('fsdp'), may hold values from 0.25 to 1.75
- first_shift: bfloat16 [1024], P('fsdp'), may hold values from -3 to 3
- qkv_weight: bfloat16 [1024, 3, 1024], P('fsdp', None, 'tp'), may hold values from -8 to 8
- qkv_bias: bfloat16 [2, 16, 64], P(None, 'tp', 'fsdp'), may hold values from -3 to 3
- proj_weight: bfloat16 [1024, 1024], P('tp', 'fsdp'), may hold values from -1.5 to 1.5
- proj_bias: bfloat16 [1024], P('fsdp'), may hold values from -3 to 3
- attn_scale: bfloat16 [1024], P('fsdp'), may hold values from 0.5 to 1.5
- second_gain: bfloat16 [1024], P('fsdp'), may hold values from 0.25 to 1.75
- second_shift: bfloat16 [1024], P('fsdp'), may hold values from -3 to 3
- up_weight: bfloat16 [1024, 4096], P('fsdp', 'tp'), may hold values from -0.1875 to 0.1875
- up_bias: bfloat16 [64, 64], P('tp', 'fsdp'), may hold values from -3 to 3
- down_weight: bfloat16 [4096, 1024], P('tp', 'fsdp'), may hold values from -0.09375 to 0.09375
- down_bias: bfloat16 [1024], P('fsdp'), may hold values from -3 to 3
- mlp_scale: bfloat16 [1024], P('fsdp'), may hold values from 0.5 to 1.5
- cotangent: float32 [8, 1056, 1024], P('fsdp', 'ctx'), may hold values from -6 to 6
Outputs:
- output: bfloat16 [8, 1056, 1024], P('fsdp', 'ctx')
- input_grad: bfloat16 [8, 1056, 1024], P('fsdp', 'ctx')
- first_gain_grad: float32 [1024], P('fsdp')
- first_shift_grad: float32 [1024], P('fsdp')
- qkv_weight_grad: float32 [1024, 3, 1024], P('fsdp', None, 'tp')
- qkv_bias_grad: float32 [2, 16, 64], P(None, 'tp', 'fsdp')
- proj_weight_grad: float32 [1024, 1024], P('tp', 'fsdp')
- proj_bias_grad: float32 [1024], P('fsdp')
- attn_scale_grad: float32 [1024], P('fsdp')
- second_gain_grad: float32 [1024], P('fsdp')
- second_shift_grad: float32 [1024], P('fsdp')
- up_weight_grad: float32 [1024, 4096], P('fsdp', 'tp')
- up_bias_grad: float32 [64, 64], P('tp', 'fsdp')
- down_weight_grad: float32 [4096, 1024], P('tp', 'fsdp')
- down_bias_grad: float32 [1024], P('fsdp')
- mlp_scale_grad: float32 [1024], P('fsdp')
Inputs may be any that keep to these rules, and one draw needn't show every extreme that they name: Block i of image n holds live tokens in its first lengths[n, i] of 528 slots; each image's lengths sum to 1025.
All inputs are finite; a program needn't handle non-finite values.
Results may differ from a plain program's by a relative error of at most 0.02.
Values may be sent and summed in bfloat16 or wider, within the bound.
No kernel may reach another device: no remote copies, remote signals or barrier semaphores. Data moves between devices by JAX's collectives and lax.ppermute only.
A program may use at most 192 MiB of HBM per device.

v0:
```python
import math

import jax
import jax.numpy as jnp
from jax import lax
from jax.sharding import PartitionSpec as P

epsilon = 1e-06
negative = -1e30


def normalize(values, gain, shift):
    center = values - jnp.mean(values, axis=-1, keepdims=True)
    inverse = lax.rsqrt(jnp.mean(center * center, axis=-1, keepdims=True) + epsilon)
    standard = center * inverse
    return (standard * gain + shift, standard, inverse)


def normalize_back(upstream, standard, inverse, gain):
    scaled = upstream * gain
    return inverse * (
        scaled
        - jnp.mean(scaled, axis=-1, keepdims=True)
        - standard * jnp.mean(scaled * standard, axis=-1, keepdims=True)
    )


def gelu_parts(hidden):
    cumulative = 0.5 * (1.0 + jax.scipy.special.erf(hidden * (1.0 / math.sqrt(2.0))))
    density = jnp.exp(-0.5 * hidden * hidden) * (1.0 / math.sqrt(2.0 * math.pi))
    return (cumulative, cumulative + hidden * density)


def key_usable(lengths, slots, slot_count):
    position = jnp.arange(slot_count, dtype=jnp.int32)
    owners = position // slots
    owner_table = owners[:, None] == jnp.arange(lengths.shape[0], dtype=jnp.int32)[None, :]
    row_limit = jnp.sum(jnp.where(owner_table, lengths[None, :], 0), axis=1)
    return position % slots < row_limit


def block_number(slot_count):
    number_blocks = max(1, slot_count // 512)
    while slot_count % number_blocks:
        number_blocks -= 1
    return number_blocks


def unpack_flat(summed, shapes):
    results = []
    offset = 0
    for target in shapes:
        length_here = math.prod(target)
        results.append(summed[offset : offset + length_here].reshape(target))
        offset = offset + length_here
    return results


def attend_image(queries, key_rows, value_rows, usable, number_blocks):
    slot_count, head_count, head_size = queries.shape
    scaling = head_size ** (-0.5)
    grouped = queries.reshape(number_blocks, slot_count // number_blocks, head_count, head_size)

    def one_block(row_block):
        scores = (
            jnp.einsum("qhd,khd->hqk", row_block, key_rows, preferred_element_type=jnp.float32)
            * scaling
        )
        scores = jnp.where(usable[None, None, :], scores, negative)
        maximum = jnp.max(scores, axis=-1, keepdims=True)
        exponent = jnp.exp(scores - maximum)
        summed = jnp.sum(exponent, axis=-1, keepdims=True)
        weights = (exponent / summed).astype(jnp.bfloat16)
        result = jnp.einsum(
            "hqk,khd->qhd", weights, value_rows, preferred_element_type=jnp.float32
        ).astype(jnp.bfloat16)
        return (result, (maximum + jnp.log(summed))[..., 0])

    result, logsum = lax.map(one_block, grouped)
    return (result.reshape(slot_count, head_count, head_size), logsum)


def attend_back(queries, key_rows, value_rows, upstream, logsum, usable, number_blocks):
    slot_count, head_count, head_size = queries.shape
    scaling = head_size ** (-0.5)
    grouped = queries.reshape(number_blocks, slot_count // number_blocks, head_count, head_size)
    upstream_blocks = upstream.reshape(
        number_blocks, slot_count // number_blocks, head_count, head_size
    )

    def one_block(carried, element):
        row_block, grads_block, logs_block = element
        scores = (
            jnp.einsum("qhd,khd->hqk", row_block, key_rows, preferred_element_type=jnp.float32)
            * scaling
        )
        scores = jnp.where(usable[None, None, :], scores, negative)
        probabilities = jnp.exp(scores - logs_block[..., None])
        probs_low = probabilities.astype(jnp.bfloat16)
        value_part = jnp.einsum(
            "hqk,qhd->khd", probs_low, grads_block, preferred_element_type=jnp.float32
        )
        dprobs = jnp.einsum(
            "qhd,khd->hqk", grads_block, value_rows, preferred_element_type=jnp.float32
        )
        row_total = jnp.sum(probabilities * dprobs, axis=-1, keepdims=True)
        dscores = (probabilities * (dprobs - row_total) * scaling).astype(jnp.bfloat16)
        query_grad = jnp.einsum(
            "hqk,khd->qhd", dscores, key_rows, preferred_element_type=jnp.float32
        ).astype(jnp.bfloat16)
        key_part = jnp.einsum(
            "hqk,qhd->khd", dscores, row_block, preferred_element_type=jnp.float32
        )
        return ((carried[0] + key_part, carried[1] + value_part), query_grad)

    zeroed = jnp.zeros(key_rows.shape, jnp.float32)
    (key_grad, value_grad), query_grad = lax.scan(
        one_block, (zeroed, zeroed), (grouped, upstream_blocks, logsum)
    )
    return (
        query_grad.reshape(slot_count, head_count, head_size),
        key_grad.astype(jnp.bfloat16),
        value_grad.astype(jnp.bfloat16),
    )


def body(
    inputs,
    lengths,
    first_gain,
    first_shift,
    qkv_weight,
    qkv_bias,
    proj_weight,
    proj_bias,
    attn_scale,
    second_gain,
    second_shift,
    up_weight,
    up_bias,
    down_weight,
    down_bias,
    mlp_scale,
    cotangent,
):
    images, slots, features = inputs.shape
    shards = lax.axis_size("fsdp")
    groups = lax.axis_size("ctx")
    attn_set = (
        lax.all_gather(first_gain, "fsdp", axis=0, tiled=True),
        lax.all_gather(first_shift, "fsdp", axis=0, tiled=True),
        lax.all_gather(qkv_weight, "fsdp", axis=0, tiled=True),
        lax.all_gather(qkv_bias, "fsdp", axis=2, tiled=True),
        lax.all_gather(proj_weight, "fsdp", axis=1, tiled=True),
        lax.all_gather(proj_bias, "fsdp", axis=0, tiled=True),
        lax.all_gather(attn_scale, "fsdp", axis=0, tiled=True),
    )
    gain_one = attn_set[0].astype(jnp.float32)
    shift_one = attn_set[1].astype(jnp.float32)
    qkv_full = attn_set[2]
    bias_pair = attn_set[3].reshape(2, -1).astype(jnp.float32)
    proj_full = attn_set[4]
    bias_proj = attn_set[5].astype(jnp.float32)
    scale_one = attn_set[6].astype(jnp.float32)
    local_width = qkv_full.shape[2]
    head_size = qkv_bias.shape[2] * shards
    row_count = images * slots
    slot_count = slots * groups
    number_blocks = block_number(slot_count)
    qkv_matrix = qkv_full.reshape(features, 3 * local_width)
    bias_rows = jnp.stack([bias_pair[0], jnp.zeros((local_width,), jnp.float32), bias_pair[1]])
    source = inputs.reshape(row_count, features).astype(jnp.float32)
    normed_one, unit_one, inverse_one = normalize(source, gain_one, shift_one)
    low_one = normed_one.astype(jnp.bfloat16)
    qkv = (
        jnp.dot(low_one, qkv_matrix, preferred_element_type=jnp.float32).reshape(
            row_count, 3, local_width
        )
        + bias_rows
    )
    qkv_low = qkv.astype(jnp.bfloat16).reshape(images, slots, 3, local_width)
    regrouped = lax.all_to_all(qkv_low, "ctx", split_axis=3, concat_axis=1, tiled=True)
    heads_here = regrouped.shape[3] // head_size
    split_rows = regrouped.reshape(images, slot_count, 3, heads_here, head_size)
    queries = split_rows[:, :, 0]
    key_rows = split_rows[:, :, 1]
    value_rows = split_rows[:, :, 2]
    mlp_set = (
        lax.all_gather(second_gain, "fsdp", axis=0, tiled=True),
        lax.all_gather(second_shift, "fsdp", axis=0, tiled=True),
        lax.all_gather(up_weight, "fsdp", axis=0, tiled=True),
        lax.all_gather(up_bias, "fsdp", axis=1, tiled=True),
        lax.all_gather(down_weight, "fsdp", axis=1, tiled=True),
        lax.all_gather(down_bias, "fsdp", axis=0, tiled=True),
        lax.all_gather(mlp_scale, "fsdp", axis=0, tiled=True),
    )
    gain_two = mlp_set[0].astype(jnp.float32)
    shift_two = mlp_set[1].astype(jnp.float32)
    up_full = mlp_set[2]
    bias_up = mlp_set[3].reshape(-1).astype(jnp.float32)
    down_full = mlp_set[4]
    bias_down = mlp_set[5].astype(jnp.float32)
    scale_two = mlp_set[6].astype(jnp.float32)

    def forward_image(element):
        usable = key_usable(element[3], slots, slot_count)
        return attend_image(element[0], element[1], element[2], usable, number_blocks)

    attended_heads, logsum = lax.map(forward_image, (queries, key_rows, value_rows, lengths))
    attended_flat = attended_heads.reshape(images, slot_count, heads_here * head_size)
    mixed = lax.all_to_all(attended_flat, "ctx", split_axis=1, concat_axis=2, tiled=True)
    mixed_rows = mixed.reshape(row_count, local_width)
    proj_part = jnp.dot(mixed_rows, proj_full, preferred_element_type=jnp.float32)
    projected = lax.psum(proj_part.astype(jnp.bfloat16), "tp").astype(jnp.float32) + bias_proj
    resid = source + scale_one * projected
    normed_two, unit_two, inverse_two = normalize(resid, gain_two, shift_two)
    low_two = normed_two.astype(jnp.bfloat16)
    hidden = jnp.dot(low_two, up_full, preferred_element_type=jnp.float32) + bias_up
    cumulative, derivative = gelu_parts(hidden)
    activated = (hidden * cumulative).astype(jnp.bfloat16)
    down_part = jnp.dot(activated, down_full, preferred_element_type=jnp.float32)
    mlp_out = lax.psum(down_part.astype(jnp.bfloat16), "tp").astype(jnp.float32) + bias_down
    output = (resid + scale_two * mlp_out).astype(jnp.bfloat16).reshape(images, slots, features)
    own_length = lax.dynamic_slice_in_dim(lengths, lax.axis_index("ctx"), 1, 1)[:, 0]
    live_rows = (jnp.arange(slots, dtype=jnp.int32)[None, :] < own_length[:, None]).astype(
        jnp.float32
    )
    upstream = (cotangent * live_rows[:, :, None]).reshape(row_count, features)
    grad_scale_two = jnp.sum(upstream * mlp_out, axis=0)
    dmlp = upstream * scale_two
    grad_down_bias = jnp.sum(dmlp, axis=0)
    dmlp_low = dmlp.astype(jnp.bfloat16)
    grad_down = jnp.einsum(
        "rj,rfk->fjk",
        activated,
        dmlp_low.reshape(row_count, shards, features // shards),
        preferred_element_type=jnp.float32,
    )
    dhidden = jnp.dot(dmlp_low, down_full.T, preferred_element_type=jnp.float32) * derivative
    grad_up_bias = jnp.sum(dhidden, axis=0)
    dhidden_low = dhidden.astype(jnp.bfloat16)
    grad_up = jnp.einsum("rd,rj->dj", low_two, dhidden_low, preferred_element_type=jnp.float32)
    dnorm_part = jnp.dot(dhidden_low, up_full.T, preferred_element_type=jnp.float32)
    dnorm_two = lax.psum(dnorm_part.astype(jnp.bfloat16), "tp").astype(jnp.float32)
    grad_gain_two = jnp.sum(dnorm_two * unit_two, axis=0)
    grad_shift_two = jnp.sum(dnorm_two, axis=0)
    mlp_pieces = [
        grad_gain_two.reshape(shards, -1),
        grad_shift_two.reshape(shards, -1),
        grad_up.reshape(shards, -1),
        grad_up_bias.reshape(up_bias.shape[0], shards, up_bias.shape[1])
        .transpose(1, 0, 2)
        .reshape(shards, -1),
        grad_down.reshape(shards, -1),
        grad_down_bias.reshape(shards, -1),
        grad_scale_two.reshape(shards, -1),
    ]
    mlp_shapes = [
        second_gain.shape,
        second_shift.shape,
        up_weight.shape,
        up_bias.shape,
        down_weight.shape,
        down_bias.shape,
        mlp_scale.shape,
    ]
    mlp_packed = jnp.concatenate(mlp_pieces, axis=1).reshape(-1)
    mlp_rows = lax.psum_scatter(
        mlp_packed.astype(jnp.bfloat16), "fsdp", scatter_dimension=0, tiled=True
    )
    mlp_summed = lax.psum(mlp_rows, "ctx").astype(jnp.float32)
    mlp_results = unpack_flat(mlp_summed, mlp_shapes)
    dresid = upstream + normalize_back(dnorm_two, unit_two, inverse_two, gain_two)
    grad_scale_one = jnp.sum(dresid * projected, axis=0)
    dproj = dresid * scale_one
    grad_proj_bias = jnp.sum(dproj, axis=0)
    dproj_low = dproj.astype(jnp.bfloat16)
    grad_proj = jnp.einsum(
        "rj,rfk->fjk",
        mixed_rows,
        dproj_low.reshape(row_count, shards, features // shards),
        preferred_element_type=jnp.float32,
    )
    dmixed = (
        jnp.dot(dproj_low, proj_full.T, preferred_element_type=jnp.float32)
        .astype(jnp.bfloat16)
        .reshape(images, slots, local_width)
    )
    dheads = lax.all_to_all(dmixed, "ctx", split_axis=2, concat_axis=1, tiled=True).reshape(
        images, slot_count, heads_here, head_size
    )

    def backward_image(element):
        usable = key_usable(element[5], slots, slot_count)
        return attend_back(
            element[0], element[1], element[2], element[3], element[4], usable, number_blocks
        )

    query_grad, key_grad, value_grad = lax.map(
        backward_image, (queries, key_rows, value_rows, dheads, logsum, lengths)
    )
    stacked = jnp.stack([query_grad, key_grad, value_grad], axis=2).reshape(
        images, slot_count, 3, heads_here * head_size
    )
    dqkv = lax.all_to_all(stacked, "ctx", split_axis=1, concat_axis=3, tiled=True)
    dqkv_rows = dqkv.reshape(row_count, 3 * local_width)
    grad_qkv = jnp.einsum("rd,rj->dj", low_one, dqkv_rows, preferred_element_type=jnp.float32)
    bias_sums = jnp.sum(dqkv.reshape(row_count, 3, local_width), axis=0, dtype=jnp.float32)
    grad_qkv_bias = jnp.stack([bias_sums[0], bias_sums[2]])
    dnorm_local = jnp.dot(dqkv_rows, qkv_matrix.T, preferred_element_type=jnp.float32)
    dnorm_one = lax.psum(dnorm_local.astype(jnp.bfloat16), "tp").astype(jnp.float32)
    grad_gain_one = jnp.sum(dnorm_one * unit_one, axis=0)
    grad_shift_one = jnp.sum(dnorm_one, axis=0)
    dinput = (
        (dresid + normalize_back(dnorm_one, unit_one, inverse_one, gain_one))
        .astype(jnp.bfloat16)
        .reshape(images, slots, features)
    )
    bias_heads = qkv_bias.shape[1]
    bias_width = qkv_bias.shape[2]
    attn_pieces = [
        grad_gain_one.reshape(shards, -1),
        grad_shift_one.reshape(shards, -1),
        grad_qkv.reshape(shards, -1),
        grad_qkv_bias.reshape(2, bias_heads, shards, bias_width)
        .transpose(2, 0, 1, 3)
        .reshape(shards, -1),
        grad_proj.reshape(shards, -1),
        grad_proj_bias.reshape(shards, -1),
        grad_scale_one.reshape(shards, -1),
    ]
    attn_shapes = [
        first_gain.shape,
        first_shift.shape,
        qkv_weight.shape,
        qkv_bias.shape,
        proj_weight.shape,
        proj_bias.shape,
        attn_scale.shape,
    ]
    attn_packed = jnp.concatenate(attn_pieces, axis=1).reshape(-1)
    attn_rows = lax.psum_scatter(
        attn_packed.astype(jnp.bfloat16), "fsdp", scatter_dimension=0, tiled=True
    )
    attn_summed = lax.psum(attn_rows, "ctx").astype(jnp.float32)
    attn_results = unpack_flat(attn_summed, attn_shapes)
    return (
        output,
        dinput,
        attn_results[0],
        attn_results[1],
        attn_results[2],
        attn_results[3],
        attn_results[4],
        attn_results[5],
        attn_results[6],
        mlp_results[0],
        mlp_results[1],
        mlp_results[2],
        mlp_results[3],
        mlp_results[4],
        mlp_results[5],
        mlp_results[6],
    )


def solution(mesh):
    in_specs = (
        P("fsdp", "ctx", None),
        P("fsdp", None),
        P("fsdp"),
        P("fsdp"),
        P("fsdp", None, "tp"),
        P(None, "tp", "fsdp"),
        P("tp", "fsdp"),
        P("fsdp"),
        P("fsdp"),
        P("fsdp"),
        P("fsdp"),
        P("fsdp", "tp"),
        P("tp", "fsdp"),
        P("tp", "fsdp"),
        P("fsdp"),
        P("fsdp"),
        P("fsdp", "ctx", None),
    )
    out_specs = (
        P("fsdp", "ctx", None),
        P("fsdp", "ctx", None),
        P("fsdp"),
        P("fsdp"),
        P("fsdp", None, "tp"),
        P(None, "tp", "fsdp"),
        P("tp", "fsdp"),
        P("fsdp"),
        P("fsdp"),
        P("fsdp"),
        P("fsdp"),
        P("fsdp", "tp"),
        P("tp", "fsdp"),
        P("tp", "fsdp"),
        P("fsdp"),
        P("fsdp"),
    )
    return jax.shard_map(body, mesh=mesh, in_specs=in_specs, out_specs=out_specs, check_vma=False)
```

profile of v0, /device:TPU:0, one launch (start us, length us, event | category | flops | bytes accessed | tf_op | source)
XLA Modules:
  0.0 989.1 jit_solution(12313928028636652443)
XLA Ops:
  10.0 15.9 %all_gather.46 = bf16[2,8,64]{1,0,2:T(2,128)(2,1)S(1)} all-gather(bf16[2,8,8]{1,0,2:T(2,128)(2,1)S(1)} %copy.208), channel_id=1, replica_groups=mesh['fsdp'=8,'ctx'=2,'tp'=2] {'fsdp'}, dimensions={2}, use_global_device_ids=true | all-gather | bytes 2304 | tf_op jit(solution)/shard_map/all_gather | solution.py:153
  26.2 12.1 %all-gather.2 = bf16[8,1,128]{2,1,0:T(2,128)(2,1)S(1)} all-gather(bf16[1,1,128]{2,1,0:T(2,128)(2,1)} %bitcast.330), channel_id=1, replica_groups=mesh['fsdp'=8,'ctx'=2,'tp'=2] {'fsdp'}, dimensions={0}, use_global_device_ids=true | all-gather | bytes 2304 | tf_op jit(solution)/shard_map/all_gather | solution.py:151
  38.4 9.2 all-gather.1
  59.6 5.1 all-to-all-start
  65.9 30.1 %all-to-all-done = bf16[1,528,3,512]{1,2,0,3:T(4,128)(2,1)} async-done(((bf16[1,528,3,512]{1,2,0,3:T(4,128)(2,1)}), bf16[1,528,3,512]{1,2,0,3:T(4,128)(2,1)}, u32[]{:S(2)}, u32[]{:S(2)}) %all-to-all-start) | async-done | bytes 1622048 | tf_op jit(solution)/shard_map/all_to_all | solution.py:182
  107.8 16.3 %while.47 = (s32[]{:T(128)}, bf16[2,528,4,64]{1,3,2,0:T(8,128)(2,1)}, f32[2,4,528]{2,1,0:T(4,128)S(1)}, pred[1056]{0:T(1024)(128)(4,1)S(1)}, bf16[2,528,4,64]{1,...) while((s32[]{:T(128)}, ...), condition=%wide.region_6.7_spmd, body=%wide.region_3.6_spmd.sunk | while | flops 597845952 | bytes 33816512 | solution.py:79
  132.1 6.8 reduce.5
  139.8 11.9 %all_to_all.60 = bf16[2,2,67584]{2,1,0:T(2,128)(2,1)S(1)} all-to-all(bf16[2,2,67584]{2,1,0:T(2,128)(2,1)} %reshape.467), channel_id=1, replica_groups=mesh['fsdp'=8,'ctx'=2,'tp'=2] {'ctx'}, dimensions={0} | all-to-all | bytes 1081344 | tf_op jit(solution)/shard_map/all_to_all | solution.py:211
  157.2 12.8 %all_gather.53 = bf16[32,64]{0,1:T(8,128)(2,1)S(1)} all-gather(bf16[32,8]{0,1:T(8,128)(2,1)S(1)} %copy-done.29), channel_id=1, replica_groups=mesh['fsdp'=8,'ctx'=2,'tp'=2] {'fsdp'}, dimensions={1}, use_global_device_ids=true | all-gather | bytes 4608 | tf_op jit(solution)/shard_map/all_gather | solution.py:192
  170.2 8.8 all-gather.6
  178.9 10.0 %all-gather.5 = bf16[8,1,128]{2,1,0:T(2,128)(2,1)S(1)} all-gather(bf16[1,1,128]{2,1,0:T(2,128)(2,1)S(1)} %bitcast.333), channel_id=1, replica_groups=mesh['fsdp'=8,'ctx'=2,'tp'=2] {'fsdp'}, dimensions={0}, use_global_device_ids=true | all-gather | bytes 2304 | tf_op jit(solution)/shard_map/all_gather | solution.py:189
  189.0 8.8 all-gather.3
  197.7 10.0 %all-gather = bf16[8,1,128]{2,1,0:T(2,128)(2,1)S(1)} all-gather(bf16[1,1,128]{2,1,0:T(2,128)(2,1)S(1)} %bitcast.335), channel_id=1, replica_groups=mesh['fsdp'=8,'ctx'=2,'tp'=2] {'fsdp'}, dimensions={0}, use_global_device_ids=true | all-gather | bytes 2304 | tf_op jit(solution)/shard_map/all_gather | solution.py:156
  208.3 9.2 all-gather.4
  217.5 10.5 %all-gather.7 = bf16[8,1,128]{2,1,0:T(2,128)(2,1)S(1)} all-gather(bf16[1,1,128]{2,1,0:T(2,128)(2,1)S(1)} %bitcast.338), channel_id=1, replica_groups=mesh['fsdp'=8,'ctx'=2,'tp'=2] {'fsdp'}, dimensions={0}, use_global_device_ids=true | all-gather | bytes 2304 | tf_op jit(solution)/shard_map/all_gather | solution.py:194
  236.6 6.8 all-gather.17.cloned.1.call-done
  243.4 7.6 multiply_convert_fusion.1
  251.1 40.5 %all-gather.19.cloned.1.call-done = bf16[2048,1024]{1,0:T(8,128)(2,1)} async-done(((bf16[2048,128]{1,0:T(8,128)(2,1)}), bf16[2048,1024]{1,0:T(8,128)(2,1)}) %all-gather.19.cloned.1.call-update) | async-done | bytes 4194320 | tf_op jit(solution)/shard_map/all_gather | solution.py:193
  291.5 7.3 fusion.137
  303.6 7.1 convolution_convert_fusion
  310.7 6.1 reshape.424
  317.0 7.8 convert_bitcast_fusion
  324.9 6.5 copy.231
  331.3 6.2 convolution_convert_fusion.5
  337.6 5.2 all-reduce.13.cloned.1.call-done
  353.8 6.6 reduce.6
  370.2 5.8 all-to-all-done.2
  386.4 98.4 %while.48 = (s32[]{:T(128)}, f32[1056,4,64]{0,2,1:T(8,128)}, f32[1056,4,64]{0,2,1:T(8,128)S(1)}, bf16[2,528,4,64]{1,3,2,0:T(8,128)(2,1)}, bf16[2,528,4,64]{1,3,2...) while((s32[]{:T(128)}, f32[1056,4,64]{0,2,1:T(8,128)}, ...), condition=%wide.region_16.17_spmd.clone, body=%wide.region_14.16_spmd.clone.sunk | while | flops 1459820800 | bytes 117614584 | solution.py:117
  386.4 7.3 subtract_exponential_fusion.3
  393.7 5.2 fusion.191
  398.9 15.7 %fusion.192 = f32[1056,4,64]{0,2,1:T(8,128)} fusion(f32[4,528,1056]{2,1,0:T(8,128)} %subtract_exponential_fusion.3, f32[4,528,1056]{2,1,0:T(8,128)} %fusion.191, f32[1056,4,64]{0,2,1:T(8,128)} %get-tuple-element.688, pred[]{:T(512)S(6)} %compare.3, bf16[2,528,4,64]{1,3,2,0:T(8,128)(2,1)} %get-tuple-element.703, s32[]{:T(128)S(6)} %copy.274), kind=kOutput, calls=%fused_computation.26.clone.1 | convolution fusion | flops 297170016 | bytes 41517060 | tf_op jit(solution)/shard_map/while/body/eval_jaxpr/while/body/eval_jaxpr/hqk,qhd->khd/dot_general | solution.py:111
  414.6 5.2 fusion.193
  419.8 15.6 %fusion.194 = bf16[2,528,4,64]{1,3,2,0:T(8,128)(2,1)} fusion(bf16[2,528,4,64]{1,3,2,0:T(8,128)(2,1)} %get-tuple-element.690, s32[]{:T(128)S(6)} %copy.274, bf16[1056,4,64]{0,2,1:T(8,128)(2,1)} %get-tuple-element.705, f32[4,528,1056]{2,1,0:T(8,128)} %subtract_exponential_fusion.3, f32[4,528,1056]{2,1,0:T(8,128)} %fusion.191), kind=kOutput, calls=%fused_computation.31.clone.1 | convolution fusion | flops 296764512 | bytes 39845892 | tf_op jit(solution)/shard_map/while/body/eval_jaxpr/while/body/eval_jaxpr/hqk,khd->qhd/dot_general | solution.py:108
  435.4 7.3 subtract_exponential_fusion.3
  442.7 5.2 fusion.191
  447.9 16.1 %fusion.192 = f32[1056,4,64]{0,2,1:T(8,128)} fusion(f32[4,528,1056]{2,1,0:T(8,128)} %subtract_exponential_fusion.3, f32[4,528,1056]{2,1,0:T(8,128)} %fusion.191, f32[1056,4,64]{0,2,1:T(8,128)} %get-tuple-element.688, pred[]{:T(512)S(6)} %compare.3, bf16[2,528,4,64]{1,3,2,0:T(8,128)(2,1)} %get-tuple-element.703, s32[]{:T(128)S(6)} %copy.274), kind=kOutput, calls=%fused_computation.26.clone.1 | convolution fusion | flops 297170016 | bytes 41517060 | tf_op jit(solution)/shard_map/while/body/eval_jaxpr/while/body/eval_jaxpr/hqk,qhd->khd/dot_general | solution.py:111
  464.0 5.2 fusion.193
  469.2 15.6 %fusion.194 = bf16[2,528,4,64]{1,3,2,0:T(8,128)(2,1)} fusion(bf16[2,528,4,64]{1,3,2,0:T(8,128)(2,1)} %get-tuple-element.690, s32[]{:T(128)S(6)} %copy.274, bf16[1056,4,64]{0,2,1:T(8,128)(2,1)} %get-tuple-element.705, f32[4,528,1056]{2,1,0:T(8,128)} %subtract_exponential_fusion.3, f32[4,528,1056]{2,1,0:T(8,128)} %fusion.191), kind=kOutput, calls=%fused_computation.31.clone.1 | convolution fusion | flops 296764512 | bytes 39845892 | tf_op jit(solution)/shard_map/while/body/eval_jaxpr/while/body/eval_jaxpr/hqk,khd->qhd/dot_general | solution.py:108
  506.8 20.3 %all-to-all-done.3 = bf16[1,1056,3,256]{3,2,0,1:T(4,128)(2,1)} async-done(((bf16[1,1056,3,256]{3,2,0,1:T(4,128)(2,1)}), bf16[1,1056,3,256]{3,2,0,1:T(4,128)(2,1)}, u32[]{:S(2)}, u32[]{:S(2)}) %all-to-all-start.3) | async-done | bytes 1622048 | tf_op jit(solution)/shard_map/all_to_all | solution.py:305
  536.3 5.2 convolution_convert_fusion.2
  541.6 6.3 bitcast_dynamic-update-slice_fusion.1
  552.3 5.0 reshape.415
  559.3 45.9 %all-reduce.17.cloned.1.call-done = (bf16[528,1024]{1,0:T(8,128)(2,1)}, bf16[528,1024]{1,0:T(8,128)(2,1)}) async-done(((bf16[528,1024]{1,0:T(8,128)(2,1)}, bf16[528,1024]{1,0:T(8,128)(2,1)}), (bf16[528,1024]{1,0:T(8,128)(2,1)}, bf16[528,1024]{1,0:T(8,128)(2,1)})) %all-reduce.17.cloned.1.call-update) | async-done | bytes 2162704 | tf_op jit(solution)/shard_map/psum | solution.py:222
  608.3 5.2 fusion.97
  622.5 10.5 %convert_element_type.199 = bf16[2102272]{0:T(1024)(128)(2,1)} reshape(bf16[8,262784]{1,0:T(8,128)(2,1)} %constant_dynamic-update-slice_fusion) | data formatting | bytes 8409088 | tf_op jit(solution)/shard_map/convert_element_type | solution.py:343
  634.1 19.3 %convert_element_type.202 = bf16[4200448]{0:T(1024)(128)(2,1)} reshape(bf16[8,525056]{1,0:T(8,128)(2,1)} %constant_dynamic-update-slice_fusion.6) | data formatting | bytes 16801792 | tf_op jit(solution)/shard_map/convert_element_type | solution.py:269
  656.0 253.2 %all-reduce.15.cloned.1.call-done = (bf16[2102272]{0:T(1024)(128)(2,1)}, bf16[4200448]{0:T(1024)(128)(2,1)}) async-done(((bf16[2102272]{0:T(1024)(128)(2,1)}, bf16[4200448]{0:T(1024)(128)(2,1)}), (bf16[2102272]{0:T(1024)(128)(2,1)}, bf16[4200448]{0:T(1024)(128)(2,1)})) %all-reduce.15.cloned.1.call-update) | async-done | bytes 12605456
  914.2 51.8 %all-reduce.19.cloned.1.call-done = (bf16[262784]{0:T(1024)(128)(2,1)}, bf16[525056]{0:T(1024)(128)(2,1)}) async-done(((bf16[262784]{0:T(1024)(128)(2,1)}, bf16[525056]{0:T(1024)(128)(2,1)}), (bf16[262784]{0:T(1024)(128)(2,1)}, bf16[525056]{0:T(1024)(128)(2,1)})) %all-reduce.19.cloned.1.call-update) | async-done | bytes 1575696 | tf_op jit(solution)/shard_map/psum | solution.py:345
  (246 shorter events, 177.3 us)
Async XLA Ops:
  7.2 40.4 %copy-start = (bf16[1,528,1024]{2,1,0:T(8,128)(2,1)S(1)}, bf16[1,528,1024]{2,1,0:T(8,128)(2,1)}, u32[]{:S(2)}) copy-start(bf16[1,528,1024]{2,1,0:T(8,128)(2,1)} %param.21) | copy-start | bytes 3244036
  7.2 45.0 %all-gather.13.cloned.1.call-start = ((), (), s32[]{:S(2)}) async-start(), calls=%async_computation.4 | async-start | bytes 3538944 | tf_op jit(solution)/shard_map/all_gather | solution.py:152
  38.4 17.7 %copy-start.27 = (f32[8,1,128]{2,1,0:T(1,128)}, f32[8,1,128]{2,1,0:T(1,128)S(1)}, u32[]{:S(2)}) copy-start(f32[8,1,128]{2,1,0:T(1,128)S(1)} %convert_element_type.207) | copy-start | bytes 12292
  47.5 8.5 copy-start.22
  47.9 8.2 copy-start.20
  48.3 7.7 copy-start.24
  59.6 6.2 copy-start.34
  59.6 36.4 %all-to-all-start = ((bf16[1,528,3,512]{1,2,0,3:T(4,128)(2,1)}), bf16[1,528,3,512]{1,2,0,3:T(4,128)(2,1)}, u32[]{:S(2)}, u32[]{:S(2)}) async-start(bf16[1,528,3,512]{1,2,0,3:T(4,128)(2,1)} %copy.211), calls=%async_computation | async-start | bytes 5242880 | tf_op jit(solution)/shard_map/all_to_all | solution.py:182
  64.7 88.1 %all-gather.15.cloned.1.call-start = ((), (), s32[]{:S(2)}) async-start(), calls=%async_computation.5 | async-start | bytes 1179648 | tf_op jit(solution)/shard_map/all_gather | solution.py:154
  65.5 168.6 %all-reduce.11.cloned.1.call-start = ((), (), s32[]{:S(2)}) async-start(), calls=%async_computation.6 | async-start | bytes 2162688 | tf_op jit(solution)/shard_map/psum | solution.py:214
  109.5 2.4 copy-start.14
  124.1 14.9 %copy-start.3 = (bf16[1056,4,64]{0,2,1:T(8,128)(2,1)}, bf16[1056,4,64]{0,2,1:T(8,128)(2,1)S(1)}, u32[]{:S(2)}) copy-start(bf16[1056,4,64]{0,2,1:T(8,128)(2,1)S(1)} %get-tuple-element.732) | copy-start | bytes 1622020
  124.1 14.9 %copy-start.4 = (bf16[1056,4,64]{0,2,1:T(8,128)(2,1)}, bf16[1056,4,64]{0,2,1:T(8,128)(2,1)S(1)}, u32[]{:S(2)}) copy-start(bf16[1056,4,64]{0,2,1:T(8,128)(2,1)S(1)} %get-tuple-element.733) | copy-start | bytes 1622020
  124.1 14.9 %copy-start.11 = (bf16[2,528,4,64]{1,3,2,0:T(8,128)(2,1)}, bf16[2,528,4,64]{1,3,2,0:T(8,128)(2,1)S(1)}, u32[]{:S(2)}) copy-start(bf16[2,528,4,64]{1,3,2,0:T(8,128)(2,1)S(1)} %get-tuple-element.742) | copy-start | bytes 1622020
  152.9 4.3 copy-start.29
  152.9 17.2 %copy-start.30 = (bf16[128]{0:T(256)(128)(2,1)S(1)}, bf16[128]{0:T(256)(128)(2,1)}, u32[]{:S(2)}) copy-start(bf16[128]{0:T(256)(128)(2,1)} %param.31) | copy-start | bytes 772
  152.9 26.0 %copy-start.31 = (bf16[128]{0:T(256)(128)(2,1)S(1)}, bf16[128]{0:T(256)(128)(2,1)}, u32[]{:S(2)}) copy-start(bf16[128]{0:T(256)(128)(2,1)} %param.30) | copy-start | bytes 772
  152.9 36.0 %copy-start.32 = (bf16[128]{0:T(256)(128)(2,1)S(1)}, bf16[128]{0:T(256)(128)(2,1)}, u32[]{:S(2)}) copy-start(bf16[128]{0:T(256)(128)(2,1)} %param.28) | copy-start | bytes 772
  152.9 44.8 %copy-start.33 = (bf16[128]{0:T(256)(128)(2,1)S(1)}, bf16[128]{0:T(256)(128)(2,1)}, u32[]{:S(2)}) copy-start(bf16[128]{0:T(256)(128)(2,1)} %param.29) | copy-start | bytes 772
  153.0 55.4 %copy-start.35 = (bf16[128]{0:T(256)(128)(2,1)S(1)}, bf16[128]{0:T(256)(128)(2,1)}, u32[]{:S(2)}) copy-start(bf16[128]{0:T(256)(128)(2,1)} %param.36) | copy-start | bytes 772
  153.0 64.5 %copy-start.36 = (bf16[128]{0:T(256)(128)(2,1)S(1)}, bf16[128]{0:T(256)(128)(2,1)}, u32[]{:S(2)}) copy-start(bf16[128]{0:T(256)(128)(2,1)} %param.35) | copy-start | bytes 772
  156.0 87.5 %all-gather.17.cloned.1.call-start = ((), (), s32[]{:S(2)}) async-start(), calls=%async_computation.7 | async-start | bytes 4718592 | tf_op jit(solution)/shard_map/all_gather | solution.py:191
  156.5 135.0 %all-gather.19.cloned.1.call-start = ((), (), s32[]{:S(2)}) async-start(), calls=%async_computation.8 | async-start | bytes 4718592 | tf_op jit(solution)/shard_map/all_gather | solution.py:193
  157.1 185.6 %all-reduce.13.cloned.1.call-start = ((), (), s32[]{:S(2)}) async-start(), calls=%async_computation.9 | async-start | bytes 2162688 | tf_op jit(solution)/shard_map/psum | solution.py:244
  291.5 8.6 copy-start.37
  342.8 2.8 copy-start.6
  342.8 2.8 copy-start.10
  345.5 3.1 copy-start.19
  363.3 12.6 %all-to-all-start.2 = ((bf16[2,2,67584]{2,1,0:T(2,128)(2,1)}), bf16[2,2,67584]{2,1,0:T(2,128)(2,1)}, u32[]{:S(2)}, u32[]{:S(2)}) async-start(bf16[2,2,67584]{2,1,0:T(2,128)(2,1)} %reshape.469), calls=%async_computation.2 | async-start | bytes 1081344 | tf_op jit(solution)/shard_map/all_to_all | solution.py:289
  386.4 7.3 copy-start.2
  386.4 7.3 copy-start.5
  435.4 7.3 copy-start.2
  435.4 7.3 copy-start.5
  484.8 3.1 copy-start.13
  485.7 4.2 copy-start.16
  497.4 29.7 %all-to-all-start.3 = ((bf16[1,1056,3,256]{3,2,0,1:T(4,128)(2,1)}), bf16[1,1056,3,256]{3,2,0,1:T(4,128)(2,1)}, u32[]{:S(2)}, u32[]{:S(2)}) async-start(bf16[1,1056,3,256]{3,2,0,1:T(4,128)(2,1)} %copy.223), calls=%async_computation.3 | async-start | bytes 4325376 | tf_op jit(solution)/shard_map/all_to_all | solution.py:305
  502.2 103.0 %all-reduce.17.cloned.1.call-start = ((), (), s32[]{:S(2)}) async-start(), calls=%async_computation.11 | async-start | bytes 4325376 | tf_op jit(solution)/shard_map/psum | solution.py:222
  541.5 367.7 %all-reduce.15.cloned.1.call-start = ((), (), s32[]{:S(2)}) async-start(), calls=%async_computation.10 | async-start | bytes 25210880
  541.6 6.4 copy-start.18
  541.6 6.4 copy-start.21
  541.6 6.4 copy-start.23
  541.6 6.4 copy-start.25
  541.6 6.4 copy-start.28
  557.3 51.0 %copy-start.26 = (f32[8,1,128]{2,1,0:T(1,128)S(1)}, f32[8,1,128]{2,1,0:T(1,128)}, u32[]{:S(2)}) copy-start(f32[8,1,128]{2,1,0:T(1,128)} %convert_element_type.212) | copy-start | bytes 12292
  605.2 3.0 copy-start.9
  608.3 5.2 copy-start.17
  653.5 312.5 %all-reduce.19.cloned.1.call-start = ((), (), s32[]{:S(2)}) async-start(), calls=%async_computation.12 | async-start | bytes 3153920 | tf_op jit(solution)/shard_map/psum | solution.py:345
  966.0 5.4 copy-start.12
  (8 other events, 10.4 us)
Sparse Core Ops, SparseCore 0:
  10.2 41.9 all-gather.12
  67.1 23.5 all-gather.14
  156.1 38.8 all-reduce.10
  196.5 46.9 all-gather.16
  244.9 46.6 all-gather.18
  303.7 38.9 all-reduce.12
  541.6 63.4 all-reduce.16
  653.6 255.5 all-reduce.14
  914.4 51.5 all-reduce.18
where the time goes:
time: 995 us; the launch traced here: 989 us
  waiting for transfers between devices  465 us (47%)
  matrix products  167 us (17%)
  local copies, waits for them, and re-layouts  159 us (16%)
  blocking collectives  119 us (12%)
  other arithmetic  48 us (5%)
  between operations  16.2 us (2%)
  starting transfers between devices  14.8 us (1%)
    unnamed x10, waiting for transfers between devices  255 us
    psum x1, waiting for transfers between devices, body(): attn_summed = lax.psum(attn_rows, 'ctx').astype(jnp.float32)  51.8 us
    unnamed x100, local copies, waits for them, and re-layouts  46.7 us
    psum x1, waiting for transfers between devices, body(): lax.psum(down_part.astype(jnp.bfloat16), 'tp').astype(jnp.float32)  45.9 us
    all_gather x1, waiting for transfers between devices, body(): lax.all_gather(down_weight, 'fsdp', axis=1, tiled=True)  40.5 us
    dot_general x2, matrix products, one_block(): jnp.einsum('hqk,qhd->khd', dscores, row_block, preferred_element_type=jnp...  31.8 us
    dot_general x2, matrix products, one_block(): jnp.einsum('hqk,khd->qhd', dscores, key_rows, preferred_element_type=jnp....  31.2 us
    all_to_all x1, waiting for transfers between devices, body(): lax.all_to_all(qkv_low, 'ctx', split_axis=3, concat_axis=1, tiled=True)  30.1 us
  transfers between devices with their start and end apart: 12, of which 10 were waited for; matrix products, arithmetic and copies ran while one was open for 12% of the time, Pallas kernels for 0%

commit v1 on v0

v1 whole, which is shorter than its diff:
```python
import math

import jax
import jax.numpy as jnp
from jax import lax
from jax.experimental import pallas as pl
from jax.experimental.pallas import tpu as pltpu
from jax.sharding import PartitionSpec as P

epsilon = 1e-06
negative = -1e30
f32 = jnp.float32
bf16 = jnp.bfloat16


def normalize(values, gain, shift):
    center = values - jnp.mean(values, axis=-1, keepdims=True)
    inverse = lax.rsqrt(jnp.mean(center * center, axis=-1, keepdims=True) + epsilon)
    standard = center * inverse
    return (standard * gain + shift, standard, inverse)


def normalize_back(upstream, standard, inverse, gain):
    scaled = upstream * gain
    return inverse * (
        scaled
        - jnp.mean(scaled, axis=-1, keepdims=True)
        - standard * jnp.mean(scaled * standard, axis=-1, keepdims=True)
    )


def gelu_parts(hidden):
    cumulative = 0.5 * (1.0 + jax.scipy.special.erf(hidden * (1.0 / math.sqrt(2.0))))
    density = jnp.exp(-0.5 * hidden * hidden) * (1.0 / math.sqrt(2.0 * math.pi))
    return (cumulative, cumulative + hidden * density)


def dot(left, right, dims):
    return lax.dot_general(left, right, (dims, ((), ())), preferred_element_type=f32)


def exchange_sum(part, axis):
    if lax.axis_size(axis) == 2:
        other = lax.ppermute(part, axis, [(0, 1), (1, 0)])
        return part.astype(f32) + other.astype(f32)
    return lax.psum(part, axis).astype(f32)


def ring_shift(value, axis, step):
    size = lax.axis_size(axis)
    return lax.ppermute(value, axis, [(i, (i + step) % size) for i in range(size)])


def lane_masks(rows, width, head_size):
    lane = lax.broadcasted_iota(jnp.int32, (rows, width), 1)
    return [
        (lane // head_size == i).astype(f32) for i in range(width // head_size)
    ]


def scores_by_key(keys, query, usable):
    scores = dot(keys, query, ((1,), (1,)))
    return jnp.where(usable, scores, negative)


def forward_kernel(live_ref, query_ref, *rest, head_size, blocks):
    key_refs, value_refs, out_ref = rest[:blocks], rest[blocks : 2 * blocks], rest[-1]
    rows, width = query_ref.shape
    masks = lane_masks(rows, width, head_size)
    query = query_ref[...].astype(f32) * head_size ** (-0.5)
    keys = jnp.concatenate([ref[...] for ref in key_refs], axis=0)
    values = jnp.concatenate([ref[...] for ref in value_refs], axis=0)
    column = lax.broadcasted_iota(jnp.int32, (1, blocks * rows), 1)
    usable = column < 0
    for i in range(blocks):
        usable = usable | ((column >= i * rows) & (column < i * rows + live_ref[i]))
    result = jnp.zeros((rows, width), f32)
    for mask in masks:
        scores = dot((query * mask).astype(bf16), keys, ((1,), (1,)))
        scores = jnp.where(usable, scores, negative)
        maximum = jnp.max(scores, axis=-1, keepdims=True)
        exponent = jnp.exp(scores - maximum)
        summed = jnp.sum(exponent, axis=-1, keepdims=True)
        weights = (exponent * (1.0 / summed)).astype(bf16)
        result = result + dot(weights, values, ((1,), (0,))) * mask
    out_ref[...] = result.astype(bf16)


def backward_kernel(live_ref, query_ref, grad_ref, *rest, head_size, blocks):
    key_refs, value_refs = rest[:blocks], rest[blocks : 2 * blocks]
    query_grad_ref, own_ref = rest[2 * blocks], rest[2 * blocks + 1]
    other_refs = rest[2 * blocks + 2 :]
    rows, width = query_ref.shape
    scaling = head_size ** (-0.5)
    masks = lane_masks(rows, width, head_size)
    query = query_ref[...].astype(f32)
    grads = grad_ref[...].astype(f32)
    key_position = lax.broadcasted_iota(jnp.int32, (rows, 1), 0)
    query_grad = jnp.zeros((rows, width), f32)
    key_grads = [jnp.zeros((rows, width), f32) for _ in range(blocks)]
    value_grads = [jnp.zeros((rows, width), f32) for _ in range(blocks)]
    for mask in masks:
        head_query = (query * mask).astype(bf16)
        scaled_query = (query * (mask * scaling)).astype(bf16)
        head_grads = (grads * mask).astype(bf16)
        scores = [
            scores_by_key(key_refs[i][...], scaled_query, key_position < live_ref[i])
            for i in range(blocks)
        ]
        maximum = scores[0].max(axis=0, keepdims=True)
        for item in scores[1:]:
            maximum = jnp.maximum(maximum, item.max(axis=0, keepdims=True))
        exponents = [jnp.exp(item - maximum) for item in scores]
        summed = sum(item.sum(axis=0, keepdims=True) for item in exponents)
        share = 1.0 / summed
        probabilities = [item * share for item in exponents]
        dprobs = [dot(value_refs[i][...], head_grads, ((1,), (1,))) for i in range(blocks)]
        row_total = sum(
            (p * d).sum(axis=0, keepdims=True) for p, d in zip(probabilities, dprobs)
        )
        for i in range(blocks):
            value_grads[i] = value_grads[i] + dot(
                probabilities[i].astype(bf16), head_grads, ((1,), (0,))
            )
            dscores = (probabilities[i] * (dprobs[i] - row_total) * scaling).astype(bf16)
            key_grads[i] = key_grads[i] + dot(dscores, head_query, ((1,), (0,)))
            query_grad = query_grad + dot(dscores, key_refs[i][...], ((0,), (0,))) * mask
    query_grad_ref[...] = query_grad.astype(bf16)
    own_ref[0] = key_grads[0]
    own_ref[1] = value_grads[0]
    for i, ref in enumerate(other_refs):
        ref[0] = key_grads[i + 1].astype(bf16)
        ref[1] = value_grads[i + 1].astype(bf16)


def column_block(rows, width, first):
    return pl.BlockSpec((rows, width), lambda p: (0, first + p))


def attend(live, query, own, others, head_size, interpret=False):
    rows, local = query.shape
    width = 2 * head_size
    pairs = local // width
    sources = [own] + list(others)
    blocks = len(sources)
    return pl.pallas_call(
        lambda *refs: forward_kernel(*refs, head_size=head_size, blocks=blocks),
        grid=(pairs,),
        in_specs=[pl.BlockSpec(memory_space=pltpu.SMEM), column_block(rows, width, 0)]
        + [column_block(rows, width, 0)] * blocks
        + [column_block(rows, width, pairs)] * blocks,
        out_specs=column_block(rows, width, 0),
        out_shape=jax.ShapeDtypeStruct((rows, local), bf16),
        cost_estimate=pl.CostEstimate(
            flops=4 * rows * rows * blocks * local,
            bytes_accessed=2 * rows * local * (2 + 2 * blocks),
            transcendentals=rows * rows * blocks * local // head_size,
        ),
        compiler_params=pltpu.CompilerParams(vmem_limit_bytes=56 * 1024 * 1024),
        name="attend",
        interpret=interpret,
    )(live, query, *sources, *sources)


def attend_back(live, query, grads, own, others, head_size, interpret=False):
    rows, local = query.shape
    width = 2 * head_size
    pairs = local // width
    sources = [own] + list(others)
    blocks = len(sources)
    stacked = pl.BlockSpec((2, rows, width), lambda p: (0, 0, p))
    return pl.pallas_call(
        lambda *refs: backward_kernel(*refs, head_size=head_size, blocks=blocks),
        grid=(pairs,),
        in_specs=[pl.BlockSpec(memory_space=pltpu.SMEM)]
        + [column_block(rows, width, 0)] * 2
        + [column_block(rows, width, 0)] * blocks
        + [column_block(rows, width, pairs)] * blocks,
        out_specs=[column_block(rows, width, 0)] + [stacked] * blocks,
        out_shape=[
            jax.ShapeDtypeStruct((rows, local), bf16),
            jax.ShapeDtypeStruct((2, rows, local), f32),
        ]
        + [jax.ShapeDtypeStruct((2, rows, local), bf16)] * (blocks - 1),
        cost_estimate=pl.CostEstimate(
            flops=10 * rows * rows * blocks * local,
            bytes_accessed=2 * rows * local * (3 + 6 * blocks),
            transcendentals=rows * rows * blocks * local // head_size,
        ),
        compiler_params=pltpu.CompilerParams(vmem_limit_bytes=56 * 1024 * 1024),
        name="attend_back",
        interpret=interpret,
    )(live, query, grads, *sources, *sources)


def body(
    inputs,
    lengths,
    first_gain,
    first_shift,
    qkv_weight,
    qkv_bias,
    proj_weight,
    proj_bias,
    attn_scale,
    second_gain,
    second_shift,
    up_weight,
    up_bias,
    down_weight,
    down_bias,
    mlp_scale,
    cotangent,
):
    images, slots, features = inputs.shape
    assert images == 1
    shards = lax.axis_size("fsdp")
    groups = lax.axis_size("ctx")
    place = lax.axis_index("ctx")
    width = qkv_weight.shape[2]
    inner = up_weight.shape[1]
    heads = qkv_bias.shape[1]
    head_size = qkv_bias.shape[2] * shards

    small = [
        first_gain,
        first_shift,
        qkv_bias,
        proj_bias,
        attn_scale,
        second_gain,
        second_shift,
        up_bias,
        down_bias,
        mlp_scale,
    ]
    sizes = [math.prod(item.shape) for item in small]
    packed = jnp.concatenate([item.reshape(-1) for item in small])
    gathered = lax.all_gather(packed, "fsdp", axis=0)
    full = []
    offset = 0
    for size in sizes:
        full.append(gathered[:, offset : offset + size].astype(f32))
        offset += size
    gain_one, shift_one, bias_pair, bias_proj, scale_one = full[:5]
    gain_two, shift_two, bias_up, bias_down, scale_two = full[5:]
    gain_one, shift_one, bias_proj, scale_one, gain_two, shift_two, bias_down, scale_two = [
        item.reshape(1, features)
        for item in (
            gain_one, shift_one, bias_proj, scale_one, gain_two, shift_two, bias_down, scale_two
        )
    ]
    bias_pair = (
        bias_pair.reshape(shards, 2, heads, -1).transpose(1, 2, 0, 3).reshape(2, width)
    )
    bias_up = bias_up.reshape(shards, up_bias.shape[0], -1).transpose(1, 0, 2).reshape(1, inner)

    qkv_matrix = lax.all_gather(
        qkv_weight.reshape(qkv_weight.shape[0], 3 * width), "fsdp", axis=0, tiled=True
    )
    proj_back = lax.all_gather(proj_weight.T, "fsdp", axis=0, tiled=True)
    up_full = lax.all_gather(up_weight, "fsdp", axis=0, tiled=True)
    down_back = lax.all_gather(down_weight.T, "fsdp", axis=0, tiled=True)

    source = inputs.reshape(slots, features).astype(f32)
    normed_one, unit_one, inverse_one = normalize(source, gain_one, shift_one)
    low_one = normed_one.astype(bf16)
    bias_kv = jnp.concatenate([jnp.zeros((width,), f32), bias_pair[1]])
    own = (dot(low_one, qkv_matrix[:, width:], ((1,), (0,))) + bias_kv).astype(bf16)
    others = [ring_shift(own, "ctx", step) for step in range(1, groups)]
    queries = (dot(low_one, qkv_matrix[:, :width], ((1,), (0,))) + bias_pair[0]).astype(bf16)
    order = (place - jnp.arange(groups, dtype=jnp.int32)) % groups
    live = jnp.take(lengths[0], order)
    mixed = attend(live, queries, own, others, head_size)

    proj_part = dot(mixed, proj_back, ((1,), (1,))).astype(bf16)
    projected = exchange_sum(proj_part, "tp") + bias_proj
    resid = source + scale_one * projected
    normed_two, unit_two, inverse_two = normalize(resid, gain_two, shift_two)
    low_two = normed_two.astype(bf16)
    hidden = dot(low_two, up_full, ((1,), (0,))) + bias_up
    cumulative, derivative = gelu_parts(hidden)
    activated = (hidden * cumulative).astype(bf16)

    row = lax.broadcasted_iota(jnp.int32, (slots, 1), 0)
    live_rows = (row < live[0]).astype(f32)
    upstream = cotangent.reshape(slots, features) * live_rows
    dmlp = upstream * scale_two
    grad_down_bias = jnp.sum(dmlp, axis=0)
    dmlp_low = dmlp.astype(bf16)
    dhidden = dot(dmlp_low, down_back, ((1,), (0,))) * derivative
    grad_up_bias = jnp.sum(dhidden, axis=0)
    dhidden_low = dhidden.astype(bf16)
    dnorm_part = dot(dhidden_low, up_full, ((1,), (1,))).astype(bf16)
    dnorm_two = exchange_sum(dnorm_part, "tp")
    down_part = dot(activated, down_back, ((1,), (1,))).astype(bf16)
    down_part, dnorm_two = lax.optimization_barrier((down_part, dnorm_two))
    mlp_out = exchange_sum(down_part, "tp") + bias_down
    output = (resid + scale_two * mlp_out).astype(bf16).reshape(images, slots, features)
    grad_scale_two = jnp.sum(upstream * mlp_out, axis=0)

    def reduce_shards(matrix):
        return lax.psum_scatter(matrix.astype(bf16), "fsdp", scatter_dimension=0, tiled=True)

    grad_up = exchange_sum(reduce_shards(dot(low_two, dhidden_low, ((0,), (0,)))), "ctx")
    grad_down = exchange_sum(reduce_shards(dot(dmlp_low, activated, ((0,), (0,)))), "ctx").T

    grad_gain_two = jnp.sum(dnorm_two * unit_two, axis=0)
    grad_shift_two = jnp.sum(dnorm_two, axis=0)
    dresid = upstream + normalize_back(dnorm_two, unit_two, inverse_two, gain_two)
    grad_scale_one = jnp.sum(dresid * projected, axis=0)
    dproj = dresid * scale_one
    grad_proj_bias = jnp.sum(dproj, axis=0)
    dproj_low = dproj.astype(bf16)
    dmixed = dot(dproj_low, proj_back, ((1,), (0,))).astype(bf16)
    grad_proj = exchange_sum(reduce_shards(dot(dproj_low, mixed, ((0,), (0,)))), "ctx").T

    query_grad, own_grad, *sent = attend_back(live, queries, dmixed, own, others, head_size)
    for step, item in enumerate(sent):
        own_grad = own_grad + ring_shift(item, "ctx", -(step + 1)).astype(f32)
    own_low = own_grad.astype(bf16)
    dqkv = jnp.concatenate([query_grad, own_low[0], own_low[1]], axis=1)
    dnorm_local = dot(dqkv, qkv_matrix, ((1,), (1,))).astype(bf16)
    dnorm_one = exchange_sum(dnorm_local, "tp")
    grad_qkv = exchange_sum(reduce_shards(dot(low_one, dqkv, ((0,), (0,)))), "ctx")
    grad_qkv_bias = jnp.stack(
        [jnp.sum(query_grad.astype(f32), axis=0), jnp.sum(own_low[1].astype(f32), axis=0)]
    )
    grad_gain_one = jnp.sum(dnorm_one * unit_one, axis=0)
    grad_shift_one = jnp.sum(dnorm_one, axis=0)
    dinput = (
        (dresid + normalize_back(dnorm_one, unit_one, inverse_one, gain_one))
        .astype(bf16)
        .reshape(images, slots, features)
    )

    pieces = [
        grad_gain_one,
        grad_shift_one,
        grad_qkv_bias.reshape(2, heads, shards, -1).transpose(2, 0, 1, 3),
        grad_proj_bias,
        grad_scale_one,
        grad_gain_two,
        grad_shift_two,
        grad_up_bias.reshape(up_bias.shape[0], shards, -1).transpose(1, 0, 2),
        grad_down_bias,
        grad_scale_two,
    ]
    sent_small = jnp.concatenate([item.reshape(shards, -1) for item in pieces], axis=1)
    got = lax.all_to_all(sent_small.astype(bf16), "fsdp", split_axis=0, concat_axis=0, tiled=True)
    total = exchange_sum(jnp.sum(got.astype(f32), axis=0).astype(bf16), "ctx")
    results = []
    offset = 0
    for item, size in zip(small, sizes):
        results.append(total[offset : offset + size].reshape(item.shape))
        offset += size
    (
        out_gain_one,
        out_shift_one,
        out_qkv_bias,
        out_proj_bias,
        out_scale_one,
        out_gain_two,
        out_shift_two,
        out_up_bias,
        out_down_bias,
        out_scale_two,
    ) = results
    return (
        output,
        dinput,
        out_gain_one,
        out_shift_one,
        grad_qkv.reshape(qkv_weight.shape),
        out_qkv_bias,
        grad_proj,
        out_proj_bias,
        out_scale_one,
        out_gain_two,
        out_shift_two,
        grad_up,
        out_up_bias,
        grad_down,
        out_down_bias,
        out_scale_two,
    )


def solution(mesh):
    rows = P("fsdp", "ctx", None)
    vector = P("fsdp")
    params = (
        vector,
        vector,
        P("fsdp", None, "tp"),
        P(None, "tp", "fsdp"),
        P("tp", "fsdp"),
        vector,
        vector,
        vector,
        vector,
        P("fsdp", "tp"),
        P("tp", "fsdp"),
        P("tp", "fsdp"),
        vector,
        vector,
    )
    return jax.shard_map(
        body,
        mesh=mesh,
        in_specs=(rows, P("fsdp", None)) + params + (rows,),
        out_specs=(rows, rows) + params,
        check_vma=False,
    )
```

time: 995 us -> 435 us (0.44)
  waiting for transfers between devices: 465 us -> 241 us
  local copies, waits for them, and re-layouts: 159 us -> 18.8 us
  matrix products: 167 us -> 57.6 us
  blocking collectives: 119 us -> 16.2 us
  Pallas kernels: 0 us -> 40.7 us
  other arithmetic: 48 us -> 22.6 us
    unnamed x10 -> x8, waiting for transfers between devices: 255 us -> 1.98 us
    ppermute x0 -> x11, waiting for transfers between devices: none -> 146 us  [the longest x9 102 us: exchange_sum(): other = lax.ppermute(part, axis, [(0, 1), (1, 0)])]
    dot_general x26 -> x13, matrix products: 167 us -> 57.6 us  [dot(): lax.dot_general(left, right, (dims, ((), ())), preferred_element_type=f32)]
    psum x4 -> x0, waiting for transfers between devices: 103 us -> none  [the longest x1 51.8 us: body(): attn_summed = lax.psum(attn_rows, 'ctx').astype(jnp.float32)]
    all_gather x10 -> x1, blocking collectives: 107 us -> 16.2 us  [body(): gathered = lax.all_gather(packed, 'fsdp', axis=0)]
    all_to_all x3 -> x1, waiting for transfers between devices: 56.1 us -> 5.94 us  [body(): lax.all_to_all(sent_small.astype(bf16), 'fsdp', split_axis=0, concat_axis...]
    pallas_call x0 -> x2, Pallas kernels: none -> 40.7 us  [the longest x1 26.7 us: attend_back(): pl.pallas_call(lambda *refs: backward_kernel(*refs, head_size=head_size,...]
    reshape x15 -> x3, local copies, waits for them, and re-layouts: 38.9 us -> 0.3 us  [the longest x2 0.19 us: body(): packed = jnp.concatenate([item.reshape(-1) for item in small])]
  transfers between devices with their start and end apart: 12 -> 20, of which waited for: 10 -> 13; matrix products, arithmetic and copies ran while one was open for 12% -> 17% of each run, Pallas kernels for 0% -> 9%
where the time goes in v1:
time: 435 us; the launch traced here: 432 us
  waiting for transfers between devices  241 us (55%)
  matrix products  57.6 us (13%)
  Pallas kernels  40.7 us (9%)
  other arithmetic  22.6 us (5%)
  starting transfers between devices  19.7 us (5%)
  local copies, waits for them, and re-layouts  18.8 us (4%)
  blocking collectives  16.2 us (4%)
  between operations  15 us (3%)
    ppermute x9, waiting for transfers between devices, exchange_sum(): other = lax.ppermute(part, axis, [(0, 1), (1, 0)])  102 us
    dot_general x13, matrix products, dot(): lax.dot_general(left, right, (dims, ((), ())), preferred_element_type=f32)  57.6 us
    ppermute x2, waiting for transfers between devices, ring_shift(): lax.ppermute(value, axis, [(i, (i + step) % size) for i in range(size)])  43.5 us
    all_gather x1, waiting for transfers between devices, body(): down_back = lax.all_gather(down_weight.T, 'fsdp', axis=0, tiled=True)  37.7 us
    reduce_scatter x4, waiting for transfers between devices, reduce_shards(): lax.psum_scatter(matrix.astype(bf16), 'fsdp', scatter_dimension=0, tiled=...  28.9 us
    pallas_call x1, Pallas kernels, attend_back(): pl.pallas_call(lambda *refs: backward_kernel(*refs, head_size=head_size,...  26.7 us
    all_gather x1, waiting for transfers between devices, body(): lax.all_gather(qkv_weight.reshape(qkv_weight.shape[0], 3 * width), 'fsdp'...  21.1 us
    all_gather x1, blocking collectives, body(): gathered = lax.all_gather(packed, 'fsdp', axis=0)  16.2 us
  transfers between devices with their start and end apart: 20, of which 13 were waited for; matrix products, arithmetic and copies ran while one was open for 17% of the time, Pallas kernels for 9%

profile of v1, /device:TPU:0, one launch (start us, length us, event | category | flops | bytes accessed | tf_op | source)
XLA Modules:
  0.0 431.9 jit_solution(9525304515292315400)
XLA Ops:
  7.4 2.0 copy.58
  14.0 16.2 %all-gather.1 = bf16[8,1,1408]{2,1,0:T(2,128)(2,1)S(1)} all-gather(bf16[1,1,1408]{2,1,0:T(2,128)(2,1)S(1)} %reshape.412), channel_id=2, replica_groups=mesh['fsdp'=8,'ctx'=2,'tp'=2] {'fsdp'}, dimensions={0}, use_global_device_ids=true | all-gather | bytes 25344 | tf_op jit(solution)/shard_map/all_gather | solution.py:239
  31.2 21.1 %all-gather.7.cloned.1.call-done = bf16[1024,1536]{0,1:T(8,128)(2,1)} async-done(((bf16[128,1536]{0,1:T(8,128)(2,1)}), bf16[1024,1536]{0,1:T(8,128)(2,1)}) %all-gather.7.cloned.1.call-update) | async-done | bytes 3145744 | tf_op jit(solution)/shard_map/all_gather | solution.py:258
  52.4 3.0 add_convert_fusion.3.refs_2_.refs_4_.refs_3_.refs_5_
  55.3 1.6 collective-permute-start
  58.2 2.8 fusion.29.refs_1_
  61.0 20.5 %collective-permute-done.refs_3_.refs_5_.refs_4_.refs_6_ = bf16[528,1024]{1,0:T(8,128)(2,1)} collective-permute-done((bf16[528,1024]{1,0:T(8,128)(2,1)S(1)}, bf16[528,1024]{1,0:T(8,128)(2,1)}, u32[]{:S(2)}, u32[]{:S(2)}) %collective-permute-start) | collective-permute-done | bytes 1081376 | tf_op jit(solution)/shard_map/ppermute | solution.py:51
  81.5 14.0 %attend.1 = bf16[528,512]{1,0:T(8,128)(2,1)} custom-call(s32[2]{0:T(128)} %and_select_fusion.1.refs_0_, bf16[528,512]{1,0:T(8,128)(2,1)} %fusion.29.refs_1_, bf16[528,1024]{1,0:T(8,128)(2,1)} %copy-done.36, bf16[528,1024]{1,0:T(8,128)(2,1)} %collective-permute-done.refs_3_.refs_5_.refs_4_.refs_6_, bf16[528,1024]{1,0:T(8,128)(2,1)} %copy-done.36, ...), custom_call_target="tpu_custom_call" | custom-call | flops 1141899264 | bytes 3244032 | tf_op jit(solution)/shard_map/attend/pallas_call | solution.py:146
  95.5 2.2 convolution_convert_fusion.4
  97.7 1.6 collective-permute-start.1
  99.6 23.3 %collective-permute-done.1 = bf16[528,1024]{1,0:T(8,128)(2,1)S(1)} collective-permute-done((bf16[528,1024]{1,0:T(8,128)(2,1)S(1)}, bf16[528,1024]{1,0:T(8,128)(2,1)S(1)}, u32[]{:S(2)}, u32[]{:S(2)}) %collective-permute-start.1) | collective-permute-done | bytes 1081376 | tf_op jit(solution)/shard_map/ppermute | solution.py:44
  123.9 2.2 fusion.53
  126.5 7.3 %multiply_convert_fusion = (bf16[528,2048]{1,0:T(8,128)(2,1)}, f32[528,2048]{1,0:T(8,128)}) fusion(f32[2048]{0:T(1024)S(1)} %reshape.399, bf16[1024,2048]{1,0:T(8,128)(2,1)} %all-gather.11.cloned.1.call-done, f32[528,1024]{1,0:T(8,128)S(1)} %get-tuple-element.104, f32[1024]{0:T(1024)S(1)} %get-tuple-element.115, f32[1024]{0:T(1024)S(1)} %get-tuple-element.116, ...), kind=kOutput, calls=%fused_computation.7 | convolution fusion | flops 2223783936 | bytes 12865664 | tf_op jit(solution)/shard_map/dot_general | solution.py:39
  133.8 37.7 %all-gather.13.cloned.1.call-done = bf16[1024,2048]{0,1:T(8,128)(2,1)} async-done(((bf16[128,2048]{0,1:T(8,128)(2,1)}), bf16[1024,2048]{0,1:T(8,128)(2,1)}) %all-gather.13.cloned.1.call-update) | async-done | bytes 4194320 | tf_op jit(solution)/shard_map/all_gather | solution.py:263
  171.5 7.5 %fusion.57 = (bf16[2048]{0:T(1024)(128)(2,1)S(1)}, bf16[528,2048]{1,0:T(8,128)(2,1)S(1)}) fusion(f32[528,2048]{1,0:T(8,128)} %get-tuple-element.133, f32[2048]{0:T(1024)S(1)} %reshape.399, bf16[1024,2048]{0,1:T(8,128)(2,1)} %all-gather.13.cloned.1.call-done, f32[1,528,1024]{2,1,0:T(8,128)} %param.33, f32[528]{0:T(1024)S(1)} %fusion.35, ...), kind=kOutput, calls=%fused_computation.139 | convolution fusion | flops 2229188608 | bytes 12863552 | tf_op jit(solution)/shard_map/dot_general | solution.py:39
  179.1 2.4 convolution_convert_fusion.5
  181.5 1.5 collective-permute-start.2
  183.1 2.5 convolution_convert_fusion.6
  185.5 22.1 %collective-permute-done.2 = bf16[528,1024]{1,0:T(8,128)(2,1)S(1)} collective-permute-done((bf16[528,1024]{1,0:T(8,128)(2,1)S(1)}, bf16[528,1024]{1,0:T(8,128)(2,1)S(1)}, u32[]{:S(2)}, u32[]{:S(2)}) %collective-permute-start.2) | collective-permute-done | bytes 1081376 | tf_op jit(solution)/shard_map/ppermute | solution.py:44
  208.1 1.5 collective-permute-start.3
  210.7 22.6 %collective-permute-done.3 = bf16[528,1024]{1,0:T(8,128)(2,1)S(1)} collective-permute-done((bf16[528,1024]{1,0:T(8,128)(2,1)S(1)}, bf16[528,1024]{1,0:T(8,128)(2,1)S(1)}, u32[]{:S(2)}, u32[]{:S(2)}) %collective-permute-start.3) | collective-permute-done | bytes 1081376 | tf_op jit(solution)/shard_map/ppermute | solution.py:44
  233.3 4.3 multiply_reduce_fusion
  237.6 1.4 copy-done.3
  239.0 2.0 convolution_convert_fusion.7
  241.1 7.8 %convolution_convert_fusion = bf16[1024,2048]{1,0:T(8,128)(2,1)} fusion(bf16[528,2048]{1,0:T(8,128)(2,1)} %get-tuple-element.132, f32[1,528,1024]{2,1,0:T(8,128)} %param.33, f32[528]{0:T(1024)S(1)} %fusion.35, f32[1024]{0:T(1024)S(1)} %get-tuple-element.117), kind=kOutput, calls=%fused_computation.9 | convolution fusion | flops 2218311680 | bytes 8525888 | tf_op jit(solution)/shard_map/dot_general | solution.py:39
  249.6 6.9 %convolution_convert_fusion.1 = bf16[1024,2048]{1,0:T(8,128)(2,1)} fusion(bf16[528,2048]{1,0:T(8,128)(2,1)} %copy-done.39, f32[528,1024]{1,0:T(8,128)S(1)} %get-tuple-element.104, f32[1024]{0:T(1024)S(1)} %copy-done.22, f32[1024]{0:T(1024)S(1)} %get-tuple-element.116, f32[528]{0:T(1024)S(1)} %add_rsqrt_fusion, f32[528]{0:T(1024)S(1)} %broadcast_multiply_fusion.4), kind=kOutput, calls=%fused_computation.10 | convolution fusion | flops 2219393024 | bytes 8532096 | tf_op jit(solution)/shard_map/dot_general | solution.py:39
  256.6 1.5 copy-done.4
  258.1 2.8 convolution_convert_fusion.8.refs_2_
  260.9 26.7 %attend_back.1 = (bf16[528,512]{1,0:T(8,128)(2,1)}, f32[2,528,512]{2,1,0:T(8,128)}, bf16[2,528,512]{2,1,0:T(8,128)(2,1)}) custom-call(s32[2]{0:T(128)} %and_select_fusion.1.refs_0_, bf16[528,512]{1,0:T(8,128)(2,1)} %fusion.29.refs_1_, bf16[528,512]{1,0:T(8,128)(2,1)} %convolution_convert_fusion.8.refs_2_, bf16[528,1024]{1,0:T(8,128)(2,1)} %copy-done.36, ...), custom_call_target="tpu_custom_call" | custom-call | flops 2854748160 | bytes 8110080 | tf_op jit(solution)/shard_map/attend_back/pallas_call | solution.py:172
  287.7 1.5 collective-permute-start.4
  289.2 23.1 %collective-permute-done.4 = bf16[2,528,512]{2,1,0:T(8,128)(2,1)S(1)} collective-permute-done((bf16[2,528,512]{2,1,0:T(8,128)(2,1)}, bf16[2,528,512]{2,1,0:T(8,128)(2,1)S(1)}, u32[]{:S(2)}, u32[]{:S(2)}) %collective-permute-start.4) | collective-permute-done | bytes 1081376 | tf_op jit(solution)/shard_map/ppermute | solution.py:51
  312.3 2.1 add_convert_fusion
  315.5 5.2 %convolution_convert_fusion.2 = bf16[1024,1536]{1,0:T(8,128)(2,1)} fusion(bf16[528,512]{1,0:T(8,128)(2,1)S(1)} %get-tuple-element.110, bf16[528,512]{1,0:T(8,128)(2,1)S(1)} %get-tuple-element.111, bf16[528,512]{1,0:T(8,128)(2,1)S(1)} %copy-done.10, bf16[1,528,1024]{2,1,0:T(8,128)(2,1)S(1)} %copy-done.2, f32[1024]{0:T(1024)S(1)} %copy-done.20, ...), kind=kOutput, calls=%fused_computation.11 | convolution fusion | flops 1670627328 | bytes 5861504 | tf_op jit(solution)/shard_map/dot_general | solution.py:39
  320.7 5.3 %convolution_convert_fusion.3 = bf16[528,1024]{1,0:T(8,128)(2,1)} fusion(bf16[1024,1536]{0,1:T(8,128)(2,1)} %all-gather.7.cloned.1.call-done, bf16[528,512]{1,0:T(8,128)(2,1)} %copy-done.11, bf16[528,512]{1,0:T(8,128)(2,1)} %copy-done.12, bf16[528,512]{1,0:T(8,128)(2,1)} %get-tuple-element.23), kind=kOutput, calls=%fused_computation.58 | convolution fusion | flops 1666351104 | bytes 5849088 | tf_op jit(solution)/shard_map/dot_general | solution.py:39
  326.0 1.4 collective-permute-start.5
  329.2 1.5 collective-permute-start.8
  330.7 19.1 %collective-permute-done.5 = bf16[528,1024]{1,0:T(8,128)(2,1)} collective-permute-done((bf16[528,1024]{1,0:T(8,128)(2,1)}, bf16[528,1024]{1,0:T(8,128)(2,1)}, u32[]{:S(2)}, u32[]{:S(2)}) %collective-permute-start.5) | collective-permute-done | bytes 1081376 | tf_op jit(solution)/shard_map/ppermute | solution.py:44
  349.8 2.8 fusion.20
  354.7 3.6 all-to-all-start
  358.4 5.9 %all-to-all-done = bf16[8,2,704]{2,1,0:T(2,128)(2,1)S(1)} async-done(((bf16[8,2,704]{2,1,0:T(2,128)(2,1)}), bf16[8,2,704]{2,1,0:T(2,128)(2,1)S(1)}, u32[]{:S(2)}, u32[]{:S(2)}) %all-to-all-start) | async-done | bytes 22560 | tf_op jit(solution)/shard_map/all_to_all | solution.py:350
  364.5 1.4 collective-permute-start.6
  365.8 3.5 fusion.33
  373.3 1.5 collective-permute-start.9
  375.7 8.7 %collective-permute-done.10 = bf16[128,2048]{1,0:T(8,128)(2,1)S(1)} collective-permute-done((bf16[128,2048]{1,0:T(8,128)(2,1)}, bf16[128,2048]{1,0:T(8,128)(2,1)S(1)}, u32[]{:S(2)}, u32[]{:S(2)}) %collective-permute-start.10) | collective-permute-done | bytes 524320 | tf_op jit(solution)/shard_map/ppermute | solution.py:44
  385.6 1.3 copy.68
  386.9 27.6 %reduce-scatter.5.cloned.1.call-done = bf16[128,1536]{1,0:T(8,128)(2,1)} async-done(((bf16[1024,1536]{1,0:T(8,128)(2,1)}), bf16[128,1536]{1,0:T(8,128)(2,1)}) %reduce-scatter.5.cloned.1.call-update) | async-done | bytes 393232 | tf_op jit(solution)/shard_map/reduce_scatter | solution.py:303
  414.5 1.5 collective-permute-start.7
  417.1 6.2 %collective-permute-done.7 = bf16[128,1536]{1,0:T(8,128)(2,1)S(1)} collective-permute-done((bf16[128,1536]{1,0:T(8,128)(2,1)}, bf16[128,1536]{1,0:T(8,128)(2,1)S(1)}, u32[]{:S(2)}, u32[]{:S(2)}) %collective-permute-start.7) | collective-permute-done | bytes 393248 | tf_op jit(solution)/shard_map/ppermute | solution.py:44
  (185 shorter events, 24.5 us)
Async XLA Ops:
  7.2 49.8 %copy-start = (s32[1,2]{1,0:T(1,128)S(1)}, s32[1,2]{1,0:T(1,128)}, u32[]{:S(2)}) copy-start(s32[1,2]{1,0:T(1,128)} %param.18) | copy-start | bytes 28
  7.2 4.3 copy-start.23
  7.2 4.4 %copy-start.24 = (bf16[32,8]{0,1:T(8,128)(2,1)S(1)}, bf16[32,8]{0,1:T(8,128)(2,1)}, u32[]{:S(2)}) copy-start(bf16[32,8]{0,1:T(8,128)(2,1)} %param.29) | copy-start | bytes 1540
  7.2 4.6 %copy-start.25 = (bf16[128]{0:T(256)(128)(2,1)S(1)}, bf16[128]{0:T(256)(128)(2,1)}, u32[]{:S(2)}) copy-start(bf16[128]{0:T(256)(128)(2,1)} %param.19) | copy-start | bytes 772
  7.2 4.8 %copy-start.26 = (bf16[128]{0:T(256)(128)(2,1)S(1)}, bf16[128]{0:T(256)(128)(2,1)}, u32[]{:S(2)}) copy-start(bf16[128]{0:T(256)(128)(2,1)} %param.20) | copy-start | bytes 772
  7.2 5.3 %copy-start.27 = (bf16[128]{0:T(256)(128)(2,1)S(1)}, bf16[128]{0:T(256)(128)(2,1)}, u32[]{:S(2)}) copy-start(bf16[128]{0:T(256)(128)(2,1)} %param.24) | copy-start | bytes 772
  7.3 5.5 %copy-start.28 = (bf16[128]{0:T(256)(128)(2,1)S(1)}, bf16[128]{0:T(256)(128)(2,1)}, u32[]{:S(2)}) copy-start(bf16[128]{0:T(256)(128)(2,1)} %param.25) | copy-start | bytes 772
  7.3 5.7 %copy-start.29 = (bf16[128]{0:T(256)(128)(2,1)S(1)}, bf16[128]{0:T(256)(128)(2,1)}, u32[]{:S(2)}) copy-start(bf16[128]{0:T(256)(128)(2,1)} %param.26) | copy-start | bytes 772
  7.3 5.9 %copy-start.30 = (bf16[128]{0:T(256)(128)(2,1)S(1)}, bf16[128]{0:T(256)(128)(2,1)}, u32[]{:S(2)}) copy-start(bf16[128]{0:T(256)(128)(2,1)} %param.27) | copy-start | bytes 772
  7.3 6.3 %copy-start.31 = (bf16[128]{0:T(256)(128)(2,1)S(1)}, bf16[128]{0:T(256)(128)(2,1)}, u32[]{:S(2)}) copy-start(bf16[128]{0:T(256)(128)(2,1)} %param.31) | copy-start | bytes 772
  7.3 6.5 %copy-start.32 = (bf16[128]{0:T(256)(128)(2,1)S(1)}, bf16[128]{0:T(256)(128)(2,1)}, u32[]{:S(2)}) copy-start(bf16[128]{0:T(256)(128)(2,1)} %param.32) | copy-start | bytes 772
  7.3 23.2 %copy-start.2 = (bf16[1,528,1024]{2,1,0:T(8,128)(2,1)S(1)}, bf16[1,528,1024]{2,1,0:T(8,128)(2,1)}, u32[]{:S(2)}) copy-start(bf16[1,528,1024]{2,1,0:T(8,128)(2,1)} %param.17) | copy-start | bytes 3244036
  7.3 45.0 %all-gather.7.cloned.1.call-start = ((), (), s32[]{:S(2)}) async-start(), calls=%async_computation.5 | async-start | bytes 3538944 | tf_op jit(solution)/shard_map/all_gather | solution.py:258
  9.4 86.1 %all-gather.9.cloned.1.call-start = ((), (), s32[]{:S(2)}) async-start(), calls=%async_computation.6 | async-start | bytes 1179648 | tf_op jit(solution)/shard_map/all_gather | solution.py:261
  10.1 116.4 %all-gather.11.cloned.1.call-start = ((), (), s32[]{:S(2)}) async-start(), calls=%async_computation.7 | async-start | bytes 4718592 | tf_op jit(solution)/shard_map/all_gather | solution.py:262
  10.9 160.7 %all-gather.13.cloned.1.call-start = ((), (), s32[]{:S(2)}) async-start(), calls=%async_computation.8 | async-start | bytes 4718592 | tf_op jit(solution)/shard_map/all_gather | solution.py:263
  11.5 317.7 %reduce-scatter.7.cloned.1.call-start = ((), (), s32[]{:S(2)}) async-start(), calls=%async_computation.10 | async-start | bytes 1179648 | tf_op jit(solution)/shard_map/reduce_scatter | solution.py:303
  30.3 27.9 %copy-start.19 = (f32[1024]{0:T(1024)}, f32[1024]{0:T(1024)S(1)}, u32[]{:S(2)}) copy-start(f32[1024]{0:T(1024)S(1)} %get-tuple-element.120) | copy-start | bytes 12292
  30.3 96.2 %copy-start.21 = (f32[1024]{0:T(1024)}, f32[1024]{0:T(1024)S(1)}, u32[]{:S(2)}) copy-start(f32[1024]{0:T(1024)S(1)} %get-tuple-element.115) | copy-start | bytes 12292
  55.3 5.7 %copy-start.36 = (bf16[528,1024]{1,0:T(8,128)(2,1)}, bf16[528,1024]{1,0:T(8,128)(2,1)S(1)}, u32[]{:S(2)}) copy-start(bf16[528,1024]{1,0:T(8,128)(2,1)S(1)} %add_convert_fusion.3.refs_2_.refs_4_.refs_3_.refs_5_) | copy-start | bytes 3244036
  55.3 26.2 %collective-permute-start = (bf16[528,1024]{1,0:T(8,128)(2,1)S(1)}, bf16[528,1024]{1,0:T(8,128)(2,1)}, u32[]{:S(2)}, u32[]{:S(2)}) collective-permute-start(bf16[528,1024]{1,0:T(8,128)(2,1)S(1)} %add_convert_fusion.3.refs_2_.refs_4_.refs_3_.refs_5_), channel_id=1, source_target_pairs={{0,2},{2,0},{1,3},{3,1},{4,6},{6,4},{5,7},{7,5},{8,10},{10,8},{9,1... | collective-permute-start | bytes 3244040 | tf_op jit(solution)/shard_map/ppermute | solution.py:51
  97.7 25.2 %copy-start.5 = (bf16[528,1024]{1,0:T(8,128)(2,1)}, bf16[528,1024]{1,0:T(8,128)(2,1)S(1)}, u32[]{:S(2)}) copy-start(bf16[528,1024]{1,0:T(8,128)(2,1)S(1)} %convolution_convert_fusion.4) | copy-start | bytes 3244036
  97.7 25.2 %collective-permute-start.1 = (bf16[528,1024]{1,0:T(8,128)(2,1)S(1)}, bf16[528,1024]{1,0:T(8,128)(2,1)S(1)}, u32[]{:S(2)}, u32[]{:S(2)}) collective-permute-start(bf16[528,1024]{1,0:T(8,128)(2,1)S(1)} %convolution_convert_fusion.4), channel_id=1, source_target_pairs={{0,1},{1,0},{2,3},{3,2},{4,5},{5,4},{6,7},{7,6},{8,9},{9,8},{10,11... | collective-permute-start | bytes 3244040 | tf_op jit(solution)/shard_map/ppermute | solution.py:44
  171.5 7.5 %copy-start.34 = (bf16[1024,2048]{1,0:T(8,128)(2,1)S(1)}, bf16[1024,2048]{1,0:T(8,128)(2,1)}, u32[]{:S(2)}) copy-start(bf16[1024,2048]{1,0:T(8,128)(2,1)} %all-gather.11.cloned.1.call-done) | copy-start | bytes 12582916
  181.5 26.1 %collective-permute-start.2 = (bf16[528,1024]{1,0:T(8,128)(2,1)S(1)}, bf16[528,1024]{1,0:T(8,128)(2,1)S(1)}, u32[]{:S(2)}, u32[]{:S(2)}) collective-permute-start(bf16[528,1024]{1,0:T(8,128)(2,1)S(1)} %convolution_convert_fusion.5), channel_id=1, source_target_pairs={{0,1},{1,0},{2,3},{3,2},{4,5},{5,4},{6,7},{7,6},{8,9},{9,8},{10,11... | collective-permute-start | bytes 3244040 | tf_op jit(solution)/shard_map/ppermute | solution.py:44
  208.0 25.3 %copy-start.6 = (bf16[528,1024]{1,0:T(8,128)(2,1)S(1)}, bf16[528,1024]{1,0:T(8,128)(2,1)}, u32[]{:S(2)}) copy-start(bf16[528,1024]{1,0:T(8,128)(2,1)} %copy-done.5) | copy-start | bytes 3244036
  208.0 25.3 %copy-start.8 = (bf16[528,1024]{1,0:T(8,128)(2,1)S(1)}, bf16[528,1024]{1,0:T(8,128)(2,1)}, u32[]{:S(2)}) copy-start(bf16[528,1024]{1,0:T(8,128)(2,1)} %copy-done.7) | copy-start | bytes 3244036
  208.0 25.3 %copy-start.9 = (f32[1,528,1024]{2,1,0:T(8,128)S(1)}, f32[1,528,1024]{2,1,0:T(8,128)}, u32[]{:S(2)}) copy-start(f32[1,528,1024]{2,1,0:T(8,128)} %param.33) | copy-start | bytes 6488068
  208.1 25.2 %collective-permute-start.3 = (bf16[528,1024]{1,0:T(8,128)(2,1)S(1)}, bf16[528,1024]{1,0:T(8,128)(2,1)S(1)}, u32[]{:S(2)}, u32[]{:S(2)}) collective-permute-start(bf16[528,1024]{1,0:T(8,128)(2,1)S(1)} %convolution_convert_fusion.6), channel_id=1, source_target_pairs={{0,1},{1,0},{2,3},{3,2},{4,5},{5,4},{6,7},{7,6},{8,9},{9,8},{10,11... | collective-permute-start | bytes 3244040 | tf_op jit(solution)/shard_map/ppermute | solution.py:44
  233.3 5.7 %copy-start.37 = (bf16[528,512]{1,0:T(8,128)(2,1)S(1)}, bf16[528,512]{1,0:T(8,128)(2,1)}, u32[]{:S(2)}) copy-start(bf16[528,512]{1,0:T(8,128)(2,1)} %attend.1) | copy-start | bytes 1622020
  241.0 128.3 %reduce-scatter.11.cloned.1.call-start = ((), (), s32[]{:S(2)}) async-start(), calls=%async_computation.12 | async-start | bytes 4718592 | tf_op jit(solution)/shard_map/reduce_scatter | solution.py:303
  248.9 124.4 %reduce-scatter.9.cloned.1.call-start = ((), (), s32[]{:S(2)}) async-start(), calls=%async_computation.11 | async-start | bytes 4718592 | tf_op jit(solution)/shard_map/reduce_scatter | solution.py:303
  256.5 158.0 %reduce-scatter.5.cloned.1.call-start = ((), (), s32[]{:S(2)}) async-start(), calls=%async_computation.9 | async-start | bytes 3538944 | tf_op jit(solution)/shard_map/reduce_scatter | solution.py:303
  287.7 24.6 %collective-permute-start.4 = (bf16[2,528,512]{2,1,0:T(8,128)(2,1)}, bf16[2,528,512]{2,1,0:T(8,128)(2,1)S(1)}, u32[]{:S(2)}, u32[]{:S(2)}) collective-permute-start(bf16[2,528,512]{2,1,0:T(8,128)(2,1)} %get-tuple-element.25), channel_id=1, source_target_pairs={{0,2},{2,0},{1,3},{3,1},{4,6},{6,4},{5,7},{7,5},{8,10},{10,8},{9,1... | collective-permute-start | bytes 3244040 | tf_op jit(solution)/shard_map/ppermute | solution.py:51
  325.9 26.8 %copy-start.18 = (bf16[1024]{0:T(1024)(128)(2,1)S(1)}, bf16[1024]{0:T(1024)(128)(2,1)}, u32[]{:S(2)}) copy-start(bf16[1024]{0:T(1024)(128)(2,1)} %get-tuple-element.106) | copy-start | bytes 6148
  326.0 26.8 %copy-start.17 = (bf16[1024]{0:T(1024)(128)(2,1)S(1)}, bf16[1024]{0:T(1024)(128)(2,1)}, u32[]{:S(2)}) copy-start(bf16[1024]{0:T(1024)(128)(2,1)} %get-tuple-element.107) | copy-start | bytes 6148
  326.0 23.9 %collective-permute-start.5 = (bf16[528,1024]{1,0:T(8,128)(2,1)}, bf16[528,1024]{1,0:T(8,128)(2,1)}, u32[]{:S(2)}, u32[]{:S(2)}) collective-permute-start(bf16[528,1024]{1,0:T(8,128)(2,1)} %convolution_convert_fusion.3), channel_id=1, source_target_pairs={{0,1},{1,0},{2,3},{3,2},{4,5},{5,4},{6,7},{7,6},{8,9},{9,8},{10,11... | collective-permute-start | bytes 3244040 | tf_op jit(solution)/shard_map/ppermute | solution.py:44
  327.4 25.4 %copy-start.16 = (bf16[1024]{0:T(1024)(128)(2,1)S(1)}, bf16[1024]{0:T(1024)(128)(2,1)}, u32[]{:S(2)}) copy-start(bf16[1024]{0:T(1024)(128)(2,1)} %get-tuple-element.97) | copy-start | bytes 6148
  329.2 45.6 %collective-permute-start.8 = (bf16[128,512]{1,0:T(8,128)(2,1)}, bf16[128,512]{1,0:T(8,128)(2,1)S(1)}, u32[]{:S(2)}, u32[]{:S(2)}) collective-permute-start(bf16[128,512]{1,0:T(8,128)(2,1)} %reduce-scatter.7.cloned.1.call-done), channel_id=1, source_target_pairs={{0,2},{2,0},{1,3},{3,1},{4,6},{6,4},{5,7},{7,5},{8,10},{10,8},{9,1... | collective-permute-start | bytes 393224 | tf_op jit(solution)/shard_map/ppermute | solution.py:44
  354.7 9.6 %all-to-all-start = ((bf16[8,2,704]{2,1,0:T(2,128)(2,1)}), bf16[8,2,704]{2,1,0:T(2,128)(2,1)S(1)}, u32[]{:S(2)}, u32[]{:S(2)}) async-start(bf16[8,2,704]{2,1,0:T(2,128)(2,1)} %reshape.415), calls=%async_computation | async-start | bytes 49152 | tf_op jit(solution)/shard_map/all_to_all | solution.py:350
  364.5 10.3 %copy-start.15 = (bf16[128,512]{1,0:T(8,128)(2,1)S(1)}, bf16[128,512]{1,0:T(8,128)(2,1)}, u32[]{:S(2)}) copy-start(bf16[128,512]{1,0:T(8,128)(2,1)} %reduce-scatter.7.cloned.1.call-done) | copy-start | bytes 393220
  364.5 5.6 %collective-permute-start.6 = (bf16[1408]{0:T(1024)(128)(2,1)S(1)}, bf16[1408]{0:T(1024)(128)(2,1)S(1)}, u32[]{:S(2)}, u32[]{:S(2)}) collective-permute-start(bf16[1408]{0:T(1024)(128)(2,1)S(1)} %reduce_sum.202), channel_id=1, source_target_pairs={{0,2},{2,0},{1,3},{3,1},{4,6},{6,4},{5,7},{7,5},{8,10},{10,8},{9,1... | collective-permute-start | bytes 8456 | tf_op jit(solution)/shard_map/ppermute | solution.py:44
  369.4 15.0 %collective-permute-start.10 = (bf16[128,2048]{1,0:T(8,128)(2,1)}, bf16[128,2048]{1,0:T(8,128)(2,1)S(1)}, u32[]{:S(2)}, u32[]{:S(2)}) collective-permute-start(bf16[128,2048]{1,0:T(8,128)(2,1)} %reduce-scatter.11.cloned.1.call-done), channel_id=1, source_target_pairs={{0,2},{2,0},{1,3},{3,1},{4,6},{6,4},{5,7},{7,5},{8,10},{10,8},{9,1... | collective-permute-start | bytes 1572872 | tf_op jit(solution)/shard_map/ppermute | solution.py:44
  373.3 42.7 %collective-permute-start.9 = (bf16[128,2048]{1,0:T(8,128)(2,1)}, bf16[128,2048]{1,0:T(8,128)(2,1)S(1)}, u32[]{:S(2)}, u32[]{:S(2)}) collective-permute-start(bf16[128,2048]{1,0:T(8,128)(2,1)} %reduce-scatter.9.cloned.1.call-done), channel_id=1, source_target_pairs={{0,2},{2,0},{1,3},{3,1},{4,6},{6,4},{5,7},{7,5},{8,10},{10,8},{9,1... | collective-permute-start | bytes 1572872 | tf_op jit(solution)/shard_map/ppermute | solution.py:44
  375.7 40.3 %copy-start.13 = (bf16[128,2048]{1,0:T(8,128)(2,1)S(1)}, bf16[128,2048]{1,0:T(8,128)(2,1)}, u32[]{:S(2)}) copy-start(bf16[128,2048]{1,0:T(8,128)(2,1)} %reduce-scatter.9.cloned.1.call-done) | copy-start | bytes 1572868
  414.5 8.8 %copy-start.14 = (bf16[128,1536]{1,0:T(8,128)(2,1)S(1)}, bf16[128,1536]{1,0:T(8,128)(2,1)}, u32[]{:S(2)}) copy-start(bf16[128,1536]{1,0:T(8,128)(2,1)} %reduce-scatter.5.cloned.1.call-done) | copy-start | bytes 1179652
  414.5 8.8 %collective-permute-start.7 = (bf16[128,1536]{1,0:T(8,128)(2,1)}, bf16[128,1536]{1,0:T(8,128)(2,1)S(1)}, u32[]{:S(2)}, u32[]{:S(2)}) collective-permute-start(bf16[128,1536]{1,0:T(8,128)(2,1)} %reduce-scatter.5.cloned.1.call-done), channel_id=1, source_target_pairs={{0,2},{2,0},{1,3},{3,1},{4,6},{6,4},{5,7},{7,5},{8,10},{10,8},{9,1... | collective-permute-start | bytes 1179656 | tf_op jit(solution)/shard_map/ppermute | solution.py:44
  416.0 8.8 %copy-start.1 = (s32[1,2]{1,0:T(1,128)S(1)}, s32[1,2]{1,0:T(1,128)}, u32[]{:S(2)}) copy-start(s32[1,2]{1,0:T(1,128)} %param.18) | copy-start | bytes 28
  (12 other events, 23.4 us)
Sparse Core Ops, SparseCore 0:
  10.3 42.0 all-gather.6
  53.9 22.2 all-gather.8
  77.9 45.5 all-gather.10
  124.9 46.6 all-gather.12
  241.2 30.7 reduce-scatter.6
  274.1 48.0 reduce-scatter.10
  324.5 48.7 reduce-scatter.8
  375.6 38.8 reduce-scatter.4

commit v2 on v1

--- a/solution.py
+++ b/solution.py
@@ -39,11 +39,26 @@
     return lax.dot_general(left, right, (dims, ((), ())), preferred_element_type=f32)
 
 
+def swap_pair(part, axis):
+    if lax.axis_size(axis) == 2:
+        return lax.ppermute(part, axis, [(0, 1), (1, 0)])
+    return None
+
+
+def pair_sum(part, other, axis):
+    if other is None:
+        return lax.psum(part, axis).astype(f32)
+    return part.astype(f32) + other.astype(f32)
+
+
 def exchange_sum(part, axis):
-    if lax.axis_size(axis) == 2:
-        other = lax.ppermute(part, axis, [(0, 1), (1, 0)])
-        return part.astype(f32) + other.astype(f32)
-    return lax.psum(part, axis).astype(f32)
+    return pair_sum(part, swap_pair(part, axis), axis)
+
+
+def after(value, *events):
+    if value is None:
+        return None
+    return lax.optimization_barrier((value,) + events)[0]
 
 
 def ring_shift(value, axis, step):
@@ -255,12 +270,16 @@
     )
     bias_up = bias_up.reshape(shards, up_bias.shape[0], -1).transpose(1, 0, 2).reshape(1, inner)
 
-    qkv_matrix = lax.all_gather(
-        qkv_weight.reshape(qkv_weight.shape[0], 3 * width), "fsdp", axis=0, tiled=True
-    )
-    proj_back = lax.all_gather(proj_weight.T, "fsdp", axis=0, tiled=True)
-    up_full = lax.all_gather(up_weight, "fsdp", axis=0, tiled=True)
-    down_back = lax.all_gather(down_weight.T, "fsdp", axis=0, tiled=True)
+    attn_part = jnp.concatenate(
+        [qkv_weight.reshape(qkv_weight.shape[0], 3 * width), proj_weight.T], axis=1
+    )
+    attn_full = lax.all_gather(attn_part, "fsdp", axis=0, tiled=True)
+    qkv_matrix = attn_full[:, : 3 * width]
+    proj_back = attn_full[:, 3 * width :]
+    mlp_part = jnp.concatenate([up_weight, down_weight.T], axis=1)
+    mlp_full = lax.all_gather(mlp_part, "fsdp", axis=0, tiled=True)
+    up_full = mlp_full[:, :inner]
+    down_back = mlp_full[:, inner:]
 
     source = inputs.reshape(slots, features).astype(f32)
     normed_one, unit_one, inverse_one = normalize(source, gain_one, shift_one)
@@ -292,18 +311,19 @@
     grad_up_bias = jnp.sum(dhidden, axis=0)
     dhidden_low = dhidden.astype(bf16)
     dnorm_part = dot(dhidden_low, up_full, ((1,), (1,))).astype(bf16)
-    dnorm_two = exchange_sum(dnorm_part, "tp")
+    dnorm_other = swap_pair(dnorm_part, "tp")
+    up_part = dot(low_two, dhidden_low, ((0,), (0,))).astype(bf16)
+    down_grad_part = dot(dmlp_low, activated, ((0,), (0,))).astype(bf16)
     down_part = dot(activated, down_back, ((1,), (1,))).astype(bf16)
-    down_part, dnorm_two = lax.optimization_barrier((down_part, dnorm_two))
-    mlp_out = exchange_sum(down_part, "tp") + bias_down
-    output = (resid + scale_two * mlp_out).astype(bf16).reshape(images, slots, features)
-    grad_scale_two = jnp.sum(upstream * mlp_out, axis=0)
+    dnorm_other = after(dnorm_other, up_part, down_grad_part, down_part)
+    dnorm_two = pair_sum(dnorm_part, dnorm_other, "tp")
+    mlp_other = swap_pair(after(down_part, dnorm_two), "tp")
 
     def reduce_shards(matrix):
-        return lax.psum_scatter(matrix.astype(bf16), "fsdp", scatter_dimension=0, tiled=True)
-
-    grad_up = exchange_sum(reduce_shards(dot(low_two, dhidden_low, ((0,), (0,)))), "ctx")
-    grad_down = exchange_sum(reduce_shards(dot(dmlp_low, activated, ((0,), (0,)))), "ctx").T
+        return lax.psum_scatter(matrix, "fsdp", scatter_dimension=0, tiled=True)
+
+    up_shard = reduce_shards(up_part)
+    down_shard = reduce_shards(down_grad_part)
 
     grad_gain_two = jnp.sum(dnorm_two * unit_two, axis=0)
     grad_shift_two = jnp.sum(dnorm_two, axis=0)
@@ -313,16 +333,26 @@
     grad_proj_bias = jnp.sum(dproj, axis=0)
     dproj_low = dproj.astype(bf16)
     dmixed = dot(dproj_low, proj_back, ((1,), (0,))).astype(bf16)
-    grad_proj = exchange_sum(reduce_shards(dot(dproj_low, mixed, ((0,), (0,)))), "ctx").T
+    proj_grad_part = dot(dproj_low, mixed, ((0,), (0,))).astype(bf16)
+    proj_shard = reduce_shards(proj_grad_part)
 
     query_grad, own_grad, *sent = attend_back(live, queries, dmixed, own, others, head_size)
+    mlp_other = after(mlp_other, query_grad)
+    mlp_out = pair_sum(down_part, mlp_other, "tp") + bias_down
+    output = (resid + scale_two * mlp_out).astype(bf16).reshape(images, slots, features)
+    grad_scale_two = jnp.sum(upstream * mlp_out, axis=0)
     for step, item in enumerate(sent):
         own_grad = own_grad + ring_shift(item, "ctx", -(step + 1)).astype(f32)
     own_low = own_grad.astype(bf16)
     dqkv = jnp.concatenate([query_grad, own_low[0], own_low[1]], axis=1)
     dnorm_local = dot(dqkv, qkv_matrix, ((1,), (1,))).astype(bf16)
     dnorm_one = exchange_sum(dnorm_local, "tp")
-    grad_qkv = exchange_sum(reduce_shards(dot(low_one, dqkv, ((0,), (0,)))), "ctx")
+    qkv_part = dot(low_one, dqkv, ((0,), (0,))).astype(bf16)
+    qkv_shard = reduce_shards(qkv_part)
+    grad_up = exchange_sum(up_shard, "ctx")
+    grad_down = exchange_sum(down_shard, "ctx").T
+    grad_proj = exchange_sum(proj_shard, "ctx").T
+    grad_qkv = exchange_sum(after(qkv_shard, grad_up, grad_down, grad_proj), "ctx")
     grad_qkv_bias = jnp.stack(
         [jnp.sum(query_grad.astype(f32), axis=0), jnp.sum(own_low[1].astype(f32), axis=0)]
     )
@@ -405,6 +435,7 @@
         vector,
         vector,
     )
+
     return jax.shard_map(
         body,
         mesh=mesh,

time: 435 us -> 391 us (0.90)
  waiting for transfers between devices: 241 us -> 193 us
  other arithmetic: 22.6 us -> 31.7 us
  matrix products: 57.6 us -> 52.7 us
    ppermute x9, waiting for transfers between devices: 102 us -> 80.2 us  [swap_pair(): return lax.ppermute(part, axis, [(0, 1), (1, 0)])]
    all_gather x4 -> x2, waiting for transfers between devices: 58.9 us -> 37.4 us  [the longest x1 29.1 us: body(): attn_full = lax.all_gather(attn_part, 'fsdp', axis=0, tiled=True)]
    all_to_all x1, waiting for transfers between devices: 5.94 us -> 0.95 us  [body(): lax.all_to_all(sent_small.astype(bf16), 'fsdp', split_axis=0, concat_axis...]
    dot_general x13, matrix products: 57.6 us -> 52.7 us  [dot(): lax.dot_general(left, right, (dims, ((), ())), preferred_element_type=f32)]
    unnamed x108 -> x111, local copies, waits for them, and re-layouts: 14.6 us -> 11.9 us
  transfers between devices with their start and end apart: 20 -> 18, of which waited for: 13 -> 14; matrix products, arithmetic and copies ran while one was open for 17% -> 18% of each run, Pallas kernels for 9% -> 11%
where the time goes in v2:
time: 391 us; the launch traced here: 385 us
  waiting for transfers between devices  193 us (49%)
  matrix products  52.7 us (13%)
  Pallas kernels  40.7 us (10%)
  other arithmetic  31.7 us (8%)
  starting transfers between devices  19.2 us (5%)
  local copies, waits for them, and re-layouts  16.2 us (4%)
  blocking collectives  16.1 us (4%)
  between operations  15 us (4%)
    ppermute x9, waiting for transfers between devices, swap_pair(): return lax.ppermute(part, axis, [(0, 1), (1, 0)])  80.2 us
    dot_general x13, matrix products, dot(): lax.dot_general(left, right, (dims, ((), ())), preferred_element_type=f32)  52.7 us
    ppermute x2, waiting for transfers between devices, ring_shift(): lax.ppermute(value, axis, [(i, (i + step) % size) for i in range(size)])  44.3 us
    all_gather x1, waiting for transfers between devices, body(): attn_full = lax.all_gather(attn_part, 'fsdp', axis=0, tiled=True)  29.1 us
    reduce_scatter x4, waiting for transfers between devices, reduce_shards(): return lax.psum_scatter(matrix, 'fsdp', scatter_dimension=0, tiled=True)  29.1 us
    pallas_call x1, Pallas kernels, attend_back(): pl.pallas_call(lambda *refs: backward_kernel(*refs, head_size=head_size,...  26.4 us
    all_gather x1, blocking collectives, body(): gathered = lax.all_gather(packed, 'fsdp', axis=0)  16.1 us
    pallas_call x1, Pallas kernels, attend(): pl.pallas_call(lambda *refs: forward_kernel(*refs, head_size=head_size, b...  14.3 us
  transfers between devices with their start and end apart: 18, of which 14 were waited for; matrix products, arithmetic and copies ran while one was open for 18% of the time, Pallas kernels for 11%

profile of v2, /device:TPU:0, one launch (start us, length us, event | category | flops | bytes accessed | tf_op | source)
XLA Modules:
  0.0 384.8 jit_solution(4692969744845941025)
XLA Ops:
  8.6 1.7 pad_maximum_fusion.4
  14.4 16.1 %all-gather.1 = bf16[8,1,1408]{2,1,0:T(2,128)(2,1)S(1)} all-gather(bf16[1,1,1408]{2,1,0:T(2,128)(2,1)S(1)} %reshape.412), channel_id=2, replica_groups=mesh['fsdp'=8,'ctx'=2,'tp'=2] {'fsdp'}, dimensions={0}, use_global_device_ids=true | all-gather | bytes 25344 | tf_op jit(solution)/shard_map/all_gather | solution.py:254
  32.0 29.1 %all-gather.5.cloned.1.call-done = bf16[1024,2048]{0,1:T(8,128)(2,1)} async-done(((bf16[128,2048]{0,1:T(8,128)(2,1)}), bf16[1024,2048]{0,1:T(8,128)(2,1)}) %all-gather.5.cloned.1.call-update) | async-done | bytes 4194320 | tf_op jit(solution)/shard_map/all_gather | solution.py:276
  61.2 2.9 add_convert_fusion.3.refs_2_.refs_4_.refs_3_.refs_5_
  64.1 1.5 collective-permute-start
  67.0 2.9 fusion.50.refs_1_
  69.9 20.4 %collective-permute-done.refs_3_.refs_5_.refs_4_.refs_6_ = bf16[528,1024]{1,0:T(8,128)(2,1)} collective-permute-done((bf16[528,1024]{1,0:T(8,128)(2,1)S(1)}, bf16[528,1024]{1,0:T(8,128)(2,1)}, u32[]{:S(2)}, u32[]{:S(2)}) %collective-permute-start) | collective-permute-done | bytes 1081376 | tf_op jit(solution)/shard_map/ppermute | solution.py:66
  90.3 14.3 %attend.1 = bf16[528,512]{1,0:T(8,128)(2,1)} custom-call(s32[2]{0:T(128)} %and_select_fusion.1.refs_0_, bf16[528,512]{1,0:T(8,128)(2,1)} %fusion.50.refs_1_, bf16[528,1024]{1,0:T(8,128)(2,1)} %copy-done.38, bf16[528,1024]{1,0:T(8,128)(2,1)} %collective-permute-done.refs_3_.refs_5_.refs_4_.refs_6_, bf16[528,1024]{1,0:T(8,128)(2,1)} %copy-done.38, ...), custom_call_target="tpu_custom_call" | custom-call | flops 1141899264 | bytes 3244032 | tf_op jit(solution)/shard_map/attend/pallas_call | solution.py:161
  104.6 2.1 convolution_convert_fusion.3
  106.7 1.5 collective-permute-start.1
  108.6 23.3 %collective-permute-done.1 = bf16[528,1024]{1,0:T(8,128)(2,1)S(1)} collective-permute-done((bf16[528,1024]{1,0:T(8,128)(2,1)S(1)}, bf16[528,1024]{1,0:T(8,128)(2,1)S(1)}, u32[]{:S(2)}, u32[]{:S(2)}) %collective-permute-start.1) | collective-permute-done | bytes 1081376 | tf_op jit(solution)/shard_map/ppermute | solution.py:44
  133.0 2.3 fusion.76
  135.7 8.3 %all-gather.7.cloned.1.call-done = bf16[1024,4096]{0,1:T(8,128)(2,1)} async-done(((bf16[128,4096]{0,1:T(8,128)(2,1)}), bf16[1024,4096]{0,1:T(8,128)(2,1)}) %all-gather.7.cloned.1.call-update) | async-done | bytes 8388624 | tf_op jit(solution)/shard_map/all_gather | solution.py:280
  144.0 5.3 %multiply_convert_fusion = (bf16[528,2048]{1,0:T(8,128)(2,1)S(1)}, f32[528,2048]{1,0:T(8,128)S(1)}) fusion(f32[2048]{0:T(1024)S(1)} %reshape.399, bf16[1024,4096]{0,1:T(8,128)(2,1)} %all-gather.7.cloned.1.call-done, f32[528,1024]{1,0:T(8,128)S(1)} %get-tuple-element.108, f32[1024]{0:T(1024)S(1)} %copy-done.25, f32[1024]{0:T(1024)S(1)} %get-tuple-element.117, ...), kind=kOutput, calls=%fused_computation.7 | convolution fusion | flops 2223783936 | bytes 12865664 | tf_op jit(solution)/shard_map/dot_general | solution.py:39
  149.4 4.5 %fusion.80 = (bf16[2048]{0:T(1024)(128)(2,1)S(1)}, bf16[528,2048]{1,0:T(8,128)(2,1)S(1)}) fusion(f32[528,2048]{1,0:T(8,128)S(1)} %get-tuple-element.134, f32[2048]{0:T(1024)S(1)} %reshape.399, bf16[1024,4096]{0,1:T(8,128)(2,1)S(1)} %copy-done.37, f32[1,528,1024]{2,1,0:T(8,128)S(1)} %copy-done.5, f32[528]{0:T(1024)S(1)} %fusion.58, ...), kind=kOutput, calls=%fused_computation.153 | convolution fusion | flops 2229188608 | bytes 12865536 | tf_op jit(solution)/shard_map/dot_general | solution.py:39
  153.9 3.4 fusion.42
  157.3 1.5 collective-permute-start.2
  158.7 3.4 fusion.45
  162.1 5.2 %convolution_convert_fusion.1 = bf16[1024,2048]{1,0:T(8,128)(2,1)} fusion(bf16[528,2048]{1,0:T(8,128)(2,1)S(1)} %get-tuple-element.133, f32[1,528,1024]{2,1,0:T(8,128)S(1)} %copy-done.5, f32[528]{0:T(1024)S(1)} %fusion.58, f32[1024]{0:T(1024)S(1)} %get-tuple-element.118), kind=kOutput, calls=%fused_computation.10 | convolution fusion | flops 2218311680 | bytes 8525888 | tf_op jit(solution)/shard_map/dot_general | solution.py:39
  167.3 6.9 %convolution_convert_fusion.2 = bf16[1024,2048]{1,0:T(8,128)(2,1)} fusion(bf16[528,2048]{1,0:T(8,128)(2,1)} %copy-done.40, f32[528,1024]{1,0:T(8,128)S(1)} %get-tuple-element.108, f32[1024]{0:T(1024)S(1)} %copy-done.25, f32[1024]{0:T(1024)S(1)} %get-tuple-element.117, f32[528]{0:T(1024)S(1)} %add_rsqrt_fusion, f32[528]{0:T(1024)S(1)} %broadcast_multiply_fusion.4), kind=kOutput, calls=%fused_computation.11 | convolution fusion | flops 2219393024 | bytes 8532096 | tf_op jit(solution)/shard_map/dot_general | solution.py:39
  174.3 9.3 %collective-permute-done.2 = bf16[528,1024]{1,0:T(8,128)(2,1)} collective-permute-done((bf16[528,1024]{1,0:T(8,128)(2,1)}, bf16[528,1024]{1,0:T(8,128)(2,1)}, u32[]{:S(2)}, u32[]{:S(2)}) %collective-permute-start.2) | collective-permute-done | bytes 1081376 | tf_op jit(solution)/shard_map/ppermute | solution.py:44
  183.6 3.3 multiply_reduce_fusion.1
  187.0 3.7 multiply_reduce_fusion.2
  192.0 2.0 convolution_convert_fusion.4
  195.3 3.4 convolution_convert_fusion.5.refs_2_
  198.7 26.4 %attend_back.1 = (bf16[528,512]{1,0:T(8,128)(2,1)}, f32[2,528,512]{2,1,0:T(8,128)}, bf16[2,528,512]{2,1,0:T(8,128)(2,1)}) custom-call(s32[2]{0:T(128)} %and_select_fusion.1.refs_0_, bf16[528,512]{1,0:T(8,128)(2,1)} %fusion.50.refs_1_, bf16[528,512]{1,0:T(8,128)(2,1)} %convolution_convert_fusion.5.refs_2_, bf16[528,1024]{1,0:T(8,128)(2,1)} %copy-done.38, ...), custom_call_target="tpu_custom_call" | custom-call | flops 2854748160 | bytes 8110080 | tf_op jit(solution)/shard_map/attend_back/pallas_call | solution.py:187
  225.1 1.5 collective-permute-start.4
  226.7 23.9 %collective-permute-done.4 = bf16[2,528,512]{2,1,0:T(8,128)(2,1)S(1)} collective-permute-done((bf16[2,528,512]{2,1,0:T(8,128)(2,1)}, bf16[2,528,512]{2,1,0:T(8,128)(2,1)S(1)}, u32[]{:S(2)}, u32[]{:S(2)}) %collective-permute-start.4) | collective-permute-done | bytes 1081376 | tf_op jit(solution)/shard_map/ppermute | solution.py:66
  250.6 2.1 add_convert_fusion
  253.9 5.3 %convolution_convert_fusion = bf16[1024,1536]{1,0:T(8,128)(2,1)} fusion(bf16[528,512]{1,0:T(8,128)(2,1)S(1)} %get-tuple-element.111, bf16[528,512]{1,0:T(8,128)(2,1)S(1)} %get-tuple-element.112, bf16[528,512]{1,0:T(8,128)(2,1)S(1)} %copy-done.11, bf16[1,528,1024]{2,1,0:T(8,128)(2,1)S(1)} %copy-done.2, f32[1024]{0:T(1024)S(1)} %copy-done.24, ...), kind=kOutput, calls=%fused_computation.9 | convolution fusion | flops 1670627328 | bytes 5861504 | tf_op jit(solution)/shard_map/dot_general | solution.py:39
  259.2 1.5 collective-permute-start.3
  260.7 5.3 %fusion.39 = bf16[528,1024]{1,0:T(8,128)(2,1)} fusion(bf16[1024,2048]{0,1:T(8,128)(2,1)} %all-gather.5.cloned.1.call-done, bf16[528,512]{1,0:T(8,128)(2,1)} %copy-done.12, bf16[528,512]{1,0:T(8,128)(2,1)} %copy-done.13, bf16[528,512]{1,0:T(8,128)(2,1)} %get-tuple-element.25), kind=kOutput, calls=%fused_computation.68 | convolution fusion | flops 1666351104 | bytes 5849088 | tf_op jit(solution)/shard_map/dot_general | solution.py:39
  266.8 19.5 %collective-permute-done.3 = bf16[528,1024]{1,0:T(8,128)(2,1)} collective-permute-done((bf16[528,1024]{1,0:T(8,128)(2,1)}, bf16[528,1024]{1,0:T(8,128)(2,1)}, u32[]{:S(2)}, u32[]{:S(2)}) %collective-permute-start.3) | collective-permute-done | bytes 1081376 | tf_op jit(solution)/shard_map/ppermute | solution.py:44
  287.6 4.2 %multiply_reduce_fusion = (bf16[1024]{0:T(1024)(128)(2,1)S(1)}, bf16[1024]{0:T(1024)(128)(2,1)S(1)}, bf16[1,528,1024]{2,1,0:T(8,128)(2,1)}) fusion(bf16[528,1024]{1,0:T(8,128)(2,1)} %collective-permute-done.3, bf16[528,1024]{1,0:T(8,128)(2,1)} %fusion.45, f32[1,528,1024]{2,1,0:T(8,128)} %param.33, f32[1024]{0:T(1024)S(1)} %get-tuple-element.115, ...), kind=kLoop, calls=%fused_computation.42 | loop fusion | flops 6486016 | bytes 7583808 | tf_op jit(solution)/shard_map/reduce_sum | solution.py:343
  292.1 1.5 collective-permute-start.9
  293.6 13.5 %collective-permute-done.5 = bf16[528,1024]{1,0:T(8,128)(2,1)} collective-permute-done((bf16[528,1024]{1,0:T(8,128)(2,1)}, bf16[528,1024]{1,0:T(8,128)(2,1)}, u32[]{:S(2)}, u32[]{:S(2)}) %collective-permute-start.5) | collective-permute-done | bytes 1081376 | tf_op jit(solution)/shard_map/ppermute | solution.py:44
  307.1 2.8 fusion.32
  312.0 3.4 all-to-all-start
  315.5 1.5 collective-permute-start.7
  317.0 3.5 fusion.54
  323.0 3.3 reduce-scatter.9.cloned.1.call-done
  326.3 1.5 collective-permute-start.8
  327.8 2.9 collective-permute-done.7
  330.7 2.3 convert_add_fusion.2
  333.0 8.4 %collective-permute-done.8 = bf16[128,2048]{1,0:T(8,128)(2,1)S(1)} collective-permute-done((bf16[128,2048]{1,0:T(8,128)(2,1)}, bf16[128,2048]{1,0:T(8,128)(2,1)S(1)}, u32[]{:S(2)}, u32[]{:S(2)}) %collective-permute-start.8) | collective-permute-done | bytes 524320 | tf_op jit(solution)/shard_map/ppermute | solution.py:44
  341.6 25.8 %reduce-scatter.5.cloned.1.call-done = bf16[128,1536]{1,0:T(8,128)(2,1)} async-done(((bf16[1024,1536]{1,0:T(8,128)(2,1)}), bf16[128,1536]{1,0:T(8,128)(2,1)}) %reduce-scatter.5.cloned.1.call-update) | async-done | bytes 393232 | tf_op jit(solution)/shard_map/reduce_scatter | solution.py:323
  367.3 1.5 collective-permute-start.10
  372.9 3.3 collective-permute-done.10
  (184 shorter events, 26.1 us)
Async XLA Ops:
  7.2 58.6 %copy-start = (s32[1,2]{1,0:T(1,128)S(1)}, s32[1,2]{1,0:T(1,128)}, u32[]{:S(2)}) copy-start(s32[1,2]{1,0:T(1,128)} %param.18) | copy-start | bytes 28
  7.2 3.3 copy-start.14
  7.2 3.6 copy-start.15
  7.2 53.9 %all-gather.5.cloned.1.call-start = ((), (), s32[]{:S(2)}) async-start(), calls=%async_computation.5 | async-start | bytes 4718592 | tf_op jit(solution)/shard_map/all_gather | solution.py:276
  10.4 2.8 copy-start.31
  10.4 3.0 copy-start.32
  10.4 3.2 copy-start.33
  10.4 3.6 copy-start.34
  10.4 3.8 copy-start.35
  10.4 20.9 %copy-start.2 = (bf16[1,528,1024]{2,1,0:T(8,128)(2,1)S(1)}, bf16[1,528,1024]{2,1,0:T(8,128)(2,1)}, u32[]{:S(2)}) copy-start(bf16[1,528,1024]{2,1,0:T(8,128)(2,1)} %param.17) | copy-start | bytes 3244036
  10.5 133.6 %all-gather.7.cloned.1.call-start = ((), (), s32[]{:S(2)}) async-start(), calls=%async_computation.6 | async-start | bytes 9437184 | tf_op jit(solution)/shard_map/all_gather | solution.py:280
  11.9 280.2 %reduce-scatter.11.cloned.1.call-start = ((), (), s32[]{:S(2)}) async-start(), calls=%async_computation.10 | async-start | bytes 1179648 | tf_op jit(solution)/shard_map/reduce_scatter | solution.py:323
  31.1 35.9 %copy-start.23 = (f32[1024]{0:T(1024)}, f32[1024]{0:T(1024)S(1)}, u32[]{:S(2)}) copy-start(f32[1024]{0:T(1024)S(1)} %get-tuple-element.121) | copy-start | bytes 12292
  64.1 5.8 %copy-start.38 = (bf16[528,1024]{1,0:T(8,128)(2,1)}, bf16[528,1024]{1,0:T(8,128)(2,1)S(1)}, u32[]{:S(2)}) copy-start(bf16[528,1024]{1,0:T(8,128)(2,1)S(1)} %add_convert_fusion.3.refs_2_.refs_4_.refs_3_.refs_5_) | copy-start | bytes 3244036
  64.1 26.2 %collective-permute-start = (bf16[528,1024]{1,0:T(8,128)(2,1)S(1)}, bf16[528,1024]{1,0:T(8,128)(2,1)}, u32[]{:S(2)}, u32[]{:S(2)}) collective-permute-start(bf16[528,1024]{1,0:T(8,128)(2,1)S(1)} %add_convert_fusion.3.refs_2_.refs_4_.refs_3_.refs_5_), channel_id=1, source_target_pairs={{0,2},{2,0},{1,3},{3,1},{4,6},{6,4},{5,7},{7,5},{8,10},{10,8},{9,1... | collective-permute-start | bytes 3244040 | tf_op jit(solution)/shard_map/ppermute | solution.py:66
  104.6 4.0 %copy-start.36 = (s32[2]{0:T(128)S(1)}, s32[2]{0:T(128)}, u32[]{:S(2)}) copy-start(s32[2]{0:T(128)} %and_select_fusion.1.refs_0_) | copy-start | bytes 28
  106.7 25.2 %copy-start.7 = (bf16[528,1024]{1,0:T(8,128)(2,1)}, bf16[528,1024]{1,0:T(8,128)(2,1)S(1)}, u32[]{:S(2)}) copy-start(bf16[528,1024]{1,0:T(8,128)(2,1)S(1)} %convolution_convert_fusion.3) | copy-start | bytes 3244036
  106.7 25.2 %collective-permute-start.1 = (bf16[528,1024]{1,0:T(8,128)(2,1)S(1)}, bf16[528,1024]{1,0:T(8,128)(2,1)S(1)}, u32[]{:S(2)}, u32[]{:S(2)}) collective-permute-start(bf16[528,1024]{1,0:T(8,128)(2,1)S(1)} %convolution_convert_fusion.3), channel_id=1, source_target_pairs={{0,1},{1,0},{2,3},{3,2},{4,5},{5,4},{6,7},{7,6},{8,9},{9,8},{10,11... | collective-permute-start | bytes 3244040 | tf_op jit(solution)/shard_map/ppermute | solution.py:44
  135.3 8.7 %copy-start.25 = (f32[1024]{0:T(1024)S(1)}, f32[1024]{0:T(1024)}, u32[]{:S(2)}) copy-start(f32[1024]{0:T(1024)} %get-tuple-element.116) | copy-start | bytes 12292
  144.0 5.3 %copy-start.5 = (f32[1,528,1024]{2,1,0:T(8,128)S(1)}, f32[1,528,1024]{2,1,0:T(8,128)}, u32[]{:S(2)}) copy-start(f32[1,528,1024]{2,1,0:T(8,128)} %param.33) | copy-start | bytes 6488068
  144.0 5.3 %copy-start.37 = (bf16[1024,4096]{0,1:T(8,128)(2,1)S(1)}, bf16[1024,4096]{0,1:T(8,128)(2,1)}, u32[]{:S(2)}) copy-start(bf16[1024,4096]{0,1:T(8,128)(2,1)} %all-gather.7.cloned.1.call-done) | copy-start | bytes 25165828
  153.9 3.4 copy-start.40
  157.3 26.3 %collective-permute-start.2 = (bf16[528,1024]{1,0:T(8,128)(2,1)}, bf16[528,1024]{1,0:T(8,128)(2,1)}, u32[]{:S(2)}, u32[]{:S(2)}) collective-permute-start(bf16[528,1024]{1,0:T(8,128)(2,1)} %fusion.42), channel_id=1, source_target_pairs={{0,1},{1,0},{2,3},{3,2},{4,5},{5,4},{6,7},{7,6},{8,9},{9,8},{10,11... | collective-permute-start | bytes 3244040 | tf_op jit(solution)/shard_map/ppermute | solution.py:44
  174.3 12.7 %copy-start.6 = (f32[1,528,1024]{2,1,0:T(8,128)S(1)}, f32[1,528,1024]{2,1,0:T(8,128)}, u32[]{:S(2)}) copy-start(f32[1,528,1024]{2,1,0:T(8,128)} %param.33) | copy-start | bytes 6488068
  174.3 12.7 %copy-start.8 = (bf16[528,1024]{1,0:T(8,128)(2,1)S(1)}, bf16[528,1024]{1,0:T(8,128)(2,1)}, u32[]{:S(2)}) copy-start(bf16[528,1024]{1,0:T(8,128)(2,1)} %copy-done.7) | copy-start | bytes 3244036
  174.3 12.7 %copy-start.10 = (bf16[528,1024]{1,0:T(8,128)(2,1)S(1)}, bf16[528,1024]{1,0:T(8,128)(2,1)}, u32[]{:S(2)}) copy-start(bf16[528,1024]{1,0:T(8,128)(2,1)} %copy-done.9) | copy-start | bytes 3244036
  187.0 5.1 %copy-start.39 = (bf16[528,512]{1,0:T(8,128)(2,1)S(1)}, bf16[528,512]{1,0:T(8,128)(2,1)}, u32[]{:S(2)}) copy-start(bf16[528,512]{1,0:T(8,128)(2,1)} %attend.1) | copy-start | bytes 1622020
  194.1 121.4 %reduce-scatter.7.cloned.1.call-start = ((), (), s32[]{:S(2)}) async-start(), calls=%async_computation.8 | async-start | bytes 4718592 | tf_op jit(solution)/shard_map/reduce_scatter | solution.py:323
  194.6 131.6 %reduce-scatter.9.cloned.1.call-start = ((), (), s32[]{:S(2)}) async-start(), calls=%async_computation.9 | async-start | bytes 4718592 | tf_op jit(solution)/shard_map/reduce_scatter | solution.py:323
  195.2 172.1 %reduce-scatter.5.cloned.1.call-start = ((), (), s32[]{:S(2)}) async-start(), calls=%async_computation.7 | async-start | bytes 3538944 | tf_op jit(solution)/shard_map/reduce_scatter | solution.py:323
  225.1 25.4 %collective-permute-start.4 = (bf16[2,528,512]{2,1,0:T(8,128)(2,1)}, bf16[2,528,512]{2,1,0:T(8,128)(2,1)S(1)}, u32[]{:S(2)}, u32[]{:S(2)}) collective-permute-start(bf16[2,528,512]{2,1,0:T(8,128)(2,1)} %get-tuple-element.28), channel_id=1, source_target_pairs={{0,2},{2,0},{1,3},{3,1},{4,6},{6,4},{5,7},{7,5},{8,10},{10,8},{9,1... | collective-permute-start | bytes 3244040 | tf_op jit(solution)/shard_map/ppermute | solution.py:66
  259.2 27.1 %collective-permute-start.3 = (bf16[528,1024]{1,0:T(8,128)(2,1)}, bf16[528,1024]{1,0:T(8,128)(2,1)}, u32[]{:S(2)}, u32[]{:S(2)}) collective-permute-start(bf16[528,1024]{1,0:T(8,128)(2,1)} %fusion.45), channel_id=1, source_target_pairs={{0,1},{1,0},{2,3},{3,2},{4,5},{5,4},{6,7},{7,6},{8,9},{9,8},{10,11... | collective-permute-start | bytes 3244040 | tf_op jit(solution)/shard_map/ppermute | solution.py:44
  266.0 41.2 %collective-permute-start.5 = (bf16[528,1024]{1,0:T(8,128)(2,1)}, bf16[528,1024]{1,0:T(8,128)(2,1)}, u32[]{:S(2)}, u32[]{:S(2)}) collective-permute-start(bf16[528,1024]{1,0:T(8,128)(2,1)} %fusion.39), channel_id=1, source_target_pairs={{0,1},{1,0},{2,3},{3,2},{4,5},{5,4},{6,7},{7,6},{8,9},{9,8},{10,11... | collective-permute-start | bytes 3244040 | tf_op jit(solution)/shard_map/ppermute | solution.py:44
  291.8 18.2 %copy-start.22 = (bf16[1024]{0:T(1024)(128)(2,1)S(1)}, bf16[1024]{0:T(1024)(128)(2,1)}, u32[]{:S(2)}) copy-start(bf16[1024]{0:T(1024)(128)(2,1)} %get-tuple-element.104) | copy-start | bytes 6148
  291.8 18.2 %copy-start.21 = (bf16[1024]{0:T(1024)(128)(2,1)S(1)}, bf16[1024]{0:T(1024)(128)(2,1)}, u32[]{:S(2)}) copy-start(bf16[1024]{0:T(1024)(128)(2,1)} %get-tuple-element.103) | copy-start | bytes 6148
  291.8 18.2 %copy-start.20 = (bf16[1024]{0:T(1024)(128)(2,1)S(1)}, bf16[1024]{0:T(1024)(128)(2,1)}, u32[]{:S(2)}) copy-start(bf16[1024]{0:T(1024)(128)(2,1)} %get-tuple-element.94) | copy-start | bytes 6148
  291.8 18.3 %copy-start.19 = (bf16[1024]{0:T(1024)(128)(2,1)S(1)}, bf16[1024]{0:T(1024)(128)(2,1)}, u32[]{:S(2)}) copy-start(bf16[1024]{0:T(1024)(128)(2,1)} %get-tuple-element.102) | copy-start | bytes 6148
  291.8 25.1 %copy-start.4 = (f32[528,1024]{1,0:T(8,128)S(1)}, f32[528,1024]{1,0:T(8,128)}, u32[]{:S(2)}) copy-start(f32[528,1024]{1,0:T(8,128)} %copy-done.3) | copy-start | bytes 6488068
  292.1 35.7 %collective-permute-start.9 = (bf16[128,512]{1,0:T(8,128)(2,1)}, bf16[128,512]{1,0:T(8,128)(2,1)S(1)}, u32[]{:S(2)}, u32[]{:S(2)}) collective-permute-start(bf16[128,512]{1,0:T(8,128)(2,1)} %reduce-scatter.11.cloned.1.call-done), channel_id=1, source_target_pairs={{0,2},{2,0},{1,3},{3,1},{4,6},{6,4},{5,7},{7,5},{8,10},{10,8},{9,1... | collective-permute-start | bytes 393224 | tf_op jit(solution)/shard_map/ppermute | solution.py:44
  312.0 9.4 %all-to-all-start = ((bf16[8,2,704]{2,1,0:T(2,128)(2,1)}), bf16[8,2,704]{2,1,0:T(2,128)(2,1)S(1)}, u32[]{:S(2)}, u32[]{:S(2)}) async-start(bf16[8,2,704]{2,1,0:T(2,128)(2,1)} %reshape.415), calls=%async_computation | async-start | bytes 49152 | tf_op jit(solution)/shard_map/all_to_all | solution.py:380
  315.4 12.3 %copy-start.18 = (bf16[128,512]{1,0:T(8,128)(2,1)S(1)}, bf16[128,512]{1,0:T(8,128)(2,1)}, u32[]{:S(2)}) copy-start(bf16[128,512]{1,0:T(8,128)(2,1)} %reduce-scatter.11.cloned.1.call-done) | copy-start | bytes 393220
  315.5 15.2 %collective-permute-start.7 = (bf16[128,2048]{1,0:T(8,128)(2,1)}, bf16[128,2048]{1,0:T(8,128)(2,1)}, u32[]{:S(2)}, u32[]{:S(2)}) collective-permute-start(bf16[128,2048]{1,0:T(8,128)(2,1)} %reduce-scatter.7.cloned.1.call-done), channel_id=1, source_target_pairs={{0,2},{2,0},{1,3},{3,1},{4,6},{6,4},{5,7},{7,5},{8,10},{10,8},{9,1... | collective-permute-start | bytes 1572872 | tf_op jit(solution)/shard_map/ppermute | solution.py:44
  321.6 47.2 %collective-permute-start.6 = (bf16[1408]{0:T(1024)(128)(2,1)S(1)}, bf16[1408]{0:T(1024)(128)(2,1)S(1)}, u32[]{:S(2)}, u32[]{:S(2)}) collective-permute-start(bf16[1408]{0:T(1024)(128)(2,1)S(1)} %reduce_sum.202), channel_id=1, source_target_pairs={{0,2},{2,0},{1,3},{3,1},{4,6},{6,4},{5,7},{7,5},{8,10},{10,8},{9,1... | collective-permute-start | bytes 8456 | tf_op jit(solution)/shard_map/ppermute | solution.py:44
  326.3 15.1 %copy-start.16 = (bf16[128,2048]{1,0:T(8,128)(2,1)S(1)}, bf16[128,2048]{1,0:T(8,128)(2,1)}, u32[]{:S(2)}) copy-start(bf16[128,2048]{1,0:T(8,128)(2,1)} %reduce-scatter.9.cloned.1.call-done) | copy-start | bytes 1572868
  326.3 15.1 %collective-permute-start.8 = (bf16[128,2048]{1,0:T(8,128)(2,1)}, bf16[128,2048]{1,0:T(8,128)(2,1)S(1)}, u32[]{:S(2)}, u32[]{:S(2)}) collective-permute-start(bf16[128,2048]{1,0:T(8,128)(2,1)} %reduce-scatter.9.cloned.1.call-done), channel_id=1, source_target_pairs={{0,2},{2,0},{1,3},{3,1},{4,6},{6,4},{5,7},{7,5},{8,10},{10,8},{9,1... | collective-permute-start | bytes 1572872 | tf_op jit(solution)/shard_map/ppermute | solution.py:44
  367.3 8.9 %copy-start.17 = (bf16[128,1536]{1,0:T(8,128)(2,1)S(1)}, bf16[128,1536]{1,0:T(8,128)(2,1)}, u32[]{:S(2)}) copy-start(bf16[128,1536]{1,0:T(8,128)(2,1)} %reduce-scatter.5.cloned.1.call-done) | copy-start | bytes 1179652
  367.3 8.9 %collective-permute-start.10 = (bf16[128,1536]{1,0:T(8,128)(2,1)}, bf16[128,1536]{1,0:T(8,128)(2,1)S(1)}, u32[]{:S(2)}, u32[]{:S(2)}) collective-permute-start(bf16[128,1536]{1,0:T(8,128)(2,1)} %reduce-scatter.5.cloned.1.call-done), channel_id=1, source_target_pairs={{0,2},{2,0},{1,3},{3,1},{4,6},{6,4},{5,7},{7,5},{8,10},{10,8},{9,1... | collective-permute-start | bytes 1179656 | tf_op jit(solution)/shard_map/ppermute | solution.py:44
  371.6 6.1 %copy-start.1 = (s32[1,2]{1,0:T(1,128)S(1)}, s32[1,2]{1,0:T(1,128)}, u32[]{:S(2)}) copy-start(s32[1,2]{1,0:T(1,128)} %param.18) | copy-start | bytes 28
  (11 other events, 16.3 us)
Sparse Core Ops, SparseCore 0:
  10.4 50.6 all-gather.4
  63.3 80.6 all-gather.6
  194.2 30.7 reduce-scatter.10
  227.2 48.1 reduce-scatter.6
  277.5 48.7 reduce-scatter.8
  328.4 38.8 reduce-scatter.4

commit v3 on v2

--- a/solution.py
+++ b/solution.py
@@ -276,8 +276,12 @@
     attn_full = lax.all_gather(attn_part, "fsdp", axis=0, tiled=True)
     qkv_matrix = attn_full[:, : 3 * width]
     proj_back = attn_full[:, 3 * width :]
-    mlp_part = jnp.concatenate([up_weight, down_weight.T], axis=1)
-    mlp_full = lax.all_gather(mlp_part, "fsdp", axis=0, tiled=True)
+    piece = up_weight.shape[0] // groups
+    up_piece = lax.dynamic_slice_in_dim(up_weight, place * piece, piece, 0)
+    down_piece = lax.dynamic_slice_in_dim(down_weight, place * piece, piece, 1)
+    mlp_full = lax.all_gather(
+        jnp.concatenate([up_piece, down_piece.T], axis=1), ("fsdp", "ctx"), axis=0, tiled=True
+    )
     up_full = mlp_full[:, :inner]
     down_back = mlp_full[:, inner:]
 
@@ -317,12 +321,11 @@
     down_part = dot(activated, down_back, ((1,), (1,))).astype(bf16)
     dnorm_other = after(dnorm_other, up_part, down_grad_part, down_part)
     dnorm_two = pair_sum(dnorm_part, dnorm_other, "tp")
-    mlp_other = swap_pair(after(down_part, dnorm_two), "tp")
+    mlp_other = swap_pair(down_part, "tp")
 
     def reduce_shards(matrix):
         return lax.psum_scatter(matrix, "fsdp", scatter_dimension=0, tiled=True)
 
-    up_shard = reduce_shards(up_part)
     down_shard = reduce_shards(down_grad_part)
 
     grad_gain_two = jnp.sum(dnorm_two * unit_two, axis=0)
@@ -334,7 +337,7 @@
     dproj_low = dproj.astype(bf16)
     dmixed = dot(dproj_low, proj_back, ((1,), (0,))).astype(bf16)
     proj_grad_part = dot(dproj_low, mixed, ((0,), (0,))).astype(bf16)
-    proj_shard = reduce_shards(proj_grad_part)
+    up_shard = reduce_shards(jnp.concatenate([up_part, proj_grad_part], axis=1))
 
     query_grad, own_grad, *sent = attend_back(live, queries, dmixed, own, others, head_size)
     mlp_other = after(mlp_other, query_grad)
@@ -349,10 +352,11 @@
     dnorm_one = exchange_sum(dnorm_local, "tp")
     qkv_part = dot(low_one, dqkv, ((0,), (0,))).astype(bf16)
     qkv_shard = reduce_shards(qkv_part)
-    grad_up = exchange_sum(up_shard, "ctx")
     grad_down = exchange_sum(down_shard, "ctx").T
-    grad_proj = exchange_sum(proj_shard, "ctx").T
-    grad_qkv = exchange_sum(after(qkv_shard, grad_up, grad_down, grad_proj), "ctx")
+    up_sum = exchange_sum(up_shard, "ctx")
+    grad_up = up_sum[:, :inner]
+    grad_proj = up_sum[:, inner:].T
+    grad_qkv = exchange_sum(after(qkv_shard, up_sum, grad_down), "ctx")
     grad_qkv_bias = jnp.stack(
         [jnp.sum(query_grad.astype(f32), axis=0), jnp.sum(own_low[1].astype(f32), axis=0)]
     )

time: 391 us -> 359 us (0.918)
  waiting for transfers between devices: 193 us -> 160 us
  matrix products: 52.7 us -> 58.2 us
    reduce_scatter x4 -> x3, waiting for transfers between devices: 29.1 us -> 0.02 us  [reduce_shards(): return lax.psum_scatter(matrix, 'fsdp', scatter_dimension=0, tiled=True)]
    all_gather x1, waiting for transfers between devices: 8.33 us -> 0.02 us  [body(): lax.all_gather(jnp.concatenate([up_piece, down_piece.T], axis=1), ('fsdp'...]
    dot_general x13, matrix products: 52.7 us -> 58.2 us  [dot(): lax.dot_general(left, right, (dims, ((), ())), preferred_element_type=f32)]
    all_to_all x1, waiting for transfers between devices: 0.95 us -> 5.68 us  [body(): lax.all_to_all(sent_small.astype(bf16), 'fsdp', split_axis=0, concat_axis...]
    ppermute x9 -> x8, waiting for transfers between devices: 80.2 us -> 77.4 us  [swap_pair(): return lax.ppermute(part, axis, [(0, 1), (1, 0)])]
    ppermute x9 -> x8, starting transfers between devices: 12.4 us -> 9.91 us  [swap_pair(): return lax.ppermute(part, axis, [(0, 1), (1, 0)])]
    unnamed x111 -> x85, local copies, waits for them, and re-layouts: 11.9 us -> 10.8 us
  transfers between devices with their start and end apart: 18 -> 16, of which waited for: 14 -> 10; matrix products, arithmetic and copies ran while one was open for 18% -> 24% of each run, Pallas kernels for 11% -> 11%
where the time goes in v3:
time: 359 us; the launch traced here: 355 us
  waiting for transfers between devices  160 us (45%)
  matrix products  58.2 us (16%)
  Pallas kernels  40.2 us (11%)
  other arithmetic  29.8 us (8%)
  starting transfers between devices  19.6 us (5%)
  local copies, waits for them, and re-layouts  16.4 us (5%)
  blocking collectives  16.3 us (5%)
  between operations  14.6 us (4%)
    ppermute x8, waiting for transfers between devices, swap_pair(): return lax.ppermute(part, axis, [(0, 1), (1, 0)])  77.4 us
    dot_general x13, matrix products, dot(): lax.dot_general(left, right, (dims, ((), ())), preferred_element_type=f32)  58.2 us
    ppermute x2, waiting for transfers between devices, ring_shift(): lax.ppermute(value, axis, [(i, (i + step) % size) for i in range(size)])  47 us
    all_gather x1, waiting for transfers between devices, body(): attn_full = lax.all_gather(attn_part, 'fsdp', axis=0, tiled=True)  29.6 us
    pallas_call x1, Pallas kernels, attend_back(): pl.pallas_call(lambda *refs: backward_kernel(*refs, head_size=head_size,...  26.2 us
    all_gather x1, blocking collectives, body(): gathered = lax.all_gather(packed, 'fsdp', axis=0)  16.3 us
    pallas_call x1, Pallas kernels, attend(): pl.pallas_call(lambda *refs: forward_kernel(*refs, head_size=head_size, b...  14 us
    unnamed x85, local copies, waits for them, and re-layouts  10.8 us
  transfers between devices with their start and end apart: 16, of which 10 were waited for; matrix products, arithmetic and copies ran while one was open for 24% of the time, Pallas kernels for 11%

profile of v3, /device:TPU:0, one launch (start us, length us, event | category | flops | bytes accessed | tf_op | source)
XLA Modules:
  0.0 355.0 jit_solution(268634588123670992)
XLA Ops:
  7.3 1.3 copy.65
  8.6 1.7 pad_maximum_fusion.4
  14.3 16.3 %all-gather.1 = bf16[8,1,1408]{2,1,0:T(2,128)(2,1)S(1)} all-gather(bf16[1,1,1408]{2,1,0:T(2,128)(2,1)S(1)} %reshape.412), channel_id=2, replica_groups=mesh['fsdp'=8,'ctx'=2,'tp'=2] {'fsdp'}, dimensions={0}, use_global_device_ids=true | all-gather | bytes 25344 | tf_op jit(solution)/shard_map/all_gather | solution.py:254
  31.6 29.6 %all-gather.5.cloned.1.call-done = bf16[1024,2048]{0,1:T(8,128)(2,1)} async-done(((bf16[128,2048]{0,1:T(8,128)(2,1)}), bf16[1024,2048]{0,1:T(8,128)(2,1)}) %all-gather.5.cloned.1.call-update) | async-done | bytes 4194320 | tf_op jit(solution)/shard_map/all_gather | solution.py:276
  61.2 2.9 add_convert_fusion.3.refs_2_.refs_4_.refs_3_.refs_5_
  64.2 1.5 collective-permute-start
  67.0 2.8 fusion.53.refs_1_
  69.9 26.2 %collective-permute-done.refs_3_.refs_5_.refs_4_.refs_6_ = bf16[528,1024]{1,0:T(8,128)(2,1)} collective-permute-done((bf16[528,1024]{1,0:T(8,128)(2,1)S(1)}, bf16[528,1024]{1,0:T(8,128)(2,1)}, u32[]{:S(2)}, u32[]{:S(2)}) %collective-permute-start) | collective-permute-done | bytes 1081376 | tf_op jit(solution)/shard_map/ppermute | solution.py:66
  96.0 14.0 %attend.1 = bf16[528,512]{1,0:T(8,128)(2,1)} custom-call(s32[2]{0:T(128)} %and_select_fusion.1.refs_0_, bf16[528,512]{1,0:T(8,128)(2,1)} %fusion.53.refs_1_, bf16[528,1024]{1,0:T(8,128)(2,1)} %copy-done.24, bf16[528,1024]{1,0:T(8,128)(2,1)} %collective-permute-done.refs_3_.refs_5_.refs_4_.refs_6_, bf16[528,1024]{1,0:T(8,128)(2,1)} %copy-done.24, ...), custom_call_target="tpu_custom_call" | custom-call | flops 1141899264 | bytes 3244032 | tf_op jit(solution)/shard_map/attend/pallas_call | solution.py:161
  110.0 3.1 convolution_convert_fusion.3
  113.1 1.5 collective-permute-start.1
  115.0 23.6 %collective-permute-done.1 = bf16[528,1024]{1,0:T(8,128)(2,1)} collective-permute-done((bf16[528,1024]{1,0:T(8,128)(2,1)}, bf16[528,1024]{1,0:T(8,128)(2,1)}, u32[]{:S(2)}, u32[]{:S(2)}) %collective-permute-start.1) | collective-permute-done | bytes 1081376 | tf_op jit(solution)/shard_map/ppermute | solution.py:44
  138.6 2.2 fusion.78
  141.2 6.1 %multiply_convert_fusion = (bf16[528,2048]{1,0:T(8,128)(2,1)S(1)}, f32[528,2048]{1,0:T(8,128)}) fusion(f32[2048]{0:T(1024)S(1)} %reshape.399, bf16[1024,4096]{1,0:T(8,128)(2,1)} %all-gather.7.cloned.1.call-done, f32[528,1024]{1,0:T(8,128)S(1)} %get-tuple-element.106, f32[1024]{0:T(1024)S(1)} %get-tuple-element.114, f32[1024]{0:T(1024)S(1)} %get-tuple-element.115, ...), kind=kOutput, calls=%fused_computation.8 | convolution fusion | flops 2223783936 | bytes 12865664 | tf_op jit(solution)/shard_map/dot_general | solution.py:39
  147.4 1.3 copy-done.26
  148.7 5.2 %convolution_convert_fusion.1 = bf16[1024,2048]{1,0:T(8,128)(2,1)} fusion(bf16[528,2048]{1,0:T(8,128)(2,1)S(1)} %get-tuple-element.131, f32[1,528,1024]{2,1,0:T(8,128)S(1)} %copy-done.4, f32[528]{0:T(1024)S(1)} %fusion.61, f32[1024]{0:T(1024)S(1)} %get-tuple-element.116), kind=kOutput, calls=%fused_computation.11 | convolution fusion | flops 2218311680 | bytes 8525888 | tf_op jit(solution)/shard_map/dot_general | solution.py:39
  154.5 6.9 %fusion.82 = (bf16[2048]{0:T(1024)(128)(2,1)S(1)}, bf16[528,2048]{1,0:T(8,128)(2,1)S(1)}) fusion(f32[528,2048]{1,0:T(8,128)} %get-tuple-element.132, f32[2048]{0:T(1024)S(1)} %reshape.399, bf16[1024,4096]{1,0:T(8,128)(2,1)} %all-gather.7.cloned.1.call-done, f32[1,528,1024]{2,1,0:T(8,128)} %param.33, f32[528]{0:T(1024)S(1)} %fusion.61, ...), kind=kOutput, calls=%fused_computation.157 | convolution fusion | flops 2229188608 | bytes 12863552 | tf_op jit(solution)/shard_map/dot_general | solution.py:39
  161.4 4.9 %fusion.45 = bf16[528,1024]{1,0:T(8,128)(2,1)S(1)} fusion(bf16[1024,4096]{1,0:T(8,128)(2,1)} %all-gather.7.cloned.1.call-done, bf16[528,2048]{1,0:T(8,128)(2,1)S(1)} %get-tuple-element.134), kind=kOutput, calls=%fused_computation.73 | convolution fusion | flops 2215133184 | bytes 7438336 | tf_op jit(solution)/shard_map/dot_general | solution.py:39
  166.3 1.5 collective-permute-start.3
  167.8 5.6 %fusion.48 = bf16[528,1024]{1,0:T(8,128)(2,1)} fusion(bf16[528,2048]{1,0:T(8,128)(2,1)S(1)} %copy-done.27, bf16[1024,4096]{1,0:T(8,128)(2,1)} %all-gather.7.cloned.1.call-done), kind=kOutput, calls=%fused_computation.74 | convolution fusion | flops 2215133184 | bytes 7438336 | tf_op jit(solution)/shard_map/dot_general | solution.py:39
  173.4 4.0 %convolution_convert_fusion.2 = bf16[1024,2048]{1,0:T(8,128)(2,1)S(1)} fusion(bf16[528,2048]{1,0:T(8,128)(2,1)S(1)} %get-tuple-element.134, f32[528,1024]{1,0:T(8,128)S(1)} %get-tuple-element.106, f32[1024]{0:T(1024)S(1)} %get-tuple-element.114, f32[1024]{0:T(1024)S(1)} %get-tuple-element.115, f32[528]{0:T(1024)S(1)} %add_rsqrt_fusion, ...), kind=kOutput, calls=%fused_computation.12 | convolution fusion | flops 2219393024 | bytes 8532096 | tf_op jit(solution)/shard_map/dot_general | solution.py:39
  177.5 13.2 %collective-permute-done.3 = bf16[528,1024]{1,0:T(8,128)(2,1)S(1)} collective-permute-done((bf16[528,1024]{1,0:T(8,128)(2,1)S(1)}, bf16[528,1024]{1,0:T(8,128)(2,1)S(1)}, u32[]{:S(2)}, u32[]{:S(2)}) %collective-permute-start.3) | collective-permute-done | bytes 1081376 | tf_op jit(solution)/shard_map/ppermute | solution.py:44
  190.6 1.2 multiply_reduce_fusion.1
  191.9 4.0 %multiply_reduce_fusion.2 = (bf16[1024]{0:T(1024)(128)(2,1)S(1)}, bf16[1024]{0:T(1024)(128)(2,1)S(1)}, f32[528,1024]{1,0:T(8,128)}) fusion(bf16[528,1024]{1,0:T(8,128)(2,1)} %collective-permute-done.1, bf16[528,1024]{1,0:T(8,128)(2,1)} %convolution_convert_fusion.3, f32[1024]{0:T(1024)S(1)} %get-tuple-element.117, f32[1024]{0:T(1024)S(1)} %get-tuple-element.121, ...), kind=kLoop, calls=%fused_computation.45 | loop fusion | flops 10811392 | bytes 10840384 | tf_op jit(solution)/shard_map/reduce_sum | solution.py:334
  195.9 2.6 convolution_convert_fusion.4
  198.5 2.7 pad_maximum_fusion
  201.5 3.5 convolution_convert_fusion.5.refs_2_
  205.0 26.2 %attend_back.1 = (bf16[528,512]{1,0:T(8,128)(2,1)}, f32[2,528,512]{2,1,0:T(8,128)}, bf16[2,528,512]{2,1,0:T(8,128)(2,1)}) custom-call(s32[2]{0:T(128)} %and_select_fusion.1.refs_0_, bf16[528,512]{1,0:T(8,128)(2,1)} %fusion.53.refs_1_, bf16[528,512]{1,0:T(8,128)(2,1)} %convolution_convert_fusion.5.refs_2_, bf16[528,1024]{1,0:T(8,128)(2,1)} %copy-done.24, ...), custom_call_target="tpu_custom_call" | custom-call | flops 2854748160 | bytes 8110080 | tf_op jit(solution)/shard_map/attend_back/pallas_call | solution.py:187
  231.2 1.5 collective-permute-start.4
  232.7 1.5 collective-permute-start.2
  234.2 20.8 %collective-permute-done.4 = bf16[2,528,512]{2,1,0:T(8,128)(2,1)S(1)} collective-permute-done((bf16[2,528,512]{2,1,0:T(8,128)(2,1)}, bf16[2,528,512]{2,1,0:T(8,128)(2,1)S(1)}, u32[]{:S(2)}, u32[]{:S(2)}) %collective-permute-start.4) | collective-permute-done | bytes 1081376 | tf_op jit(solution)/shard_map/ppermute | solution.py:66
  255.1 2.0 add_convert_fusion
  258.2 5.3 %convolution_convert_fusion = bf16[1024,1536]{1,0:T(8,128)(2,1)} fusion(bf16[528,512]{1,0:T(8,128)(2,1)S(1)} %get-tuple-element.109, bf16[528,512]{1,0:T(8,128)(2,1)S(1)} %get-tuple-element.110, bf16[528,512]{1,0:T(8,128)(2,1)S(1)} %copy-done.7, bf16[1,528,1024]{2,1,0:T(8,128)(2,1)S(1)} %copy-done.3, f32[1024]{0:T(1024)S(1)} %get-tuple-element.119, ...), kind=kOutput, calls=%fused_computation.10 | convolution fusion | flops 1670627328 | bytes 5861504 | tf_op jit(solution)/shard_map/dot_general | solution.py:39
  263.5 5.2 %fusion.42 = bf16[528,1024]{1,0:T(8,128)(2,1)} fusion(bf16[1024,2048]{0,1:T(8,128)(2,1)} %all-gather.5.cloned.1.call-done, bf16[528,512]{1,0:T(8,128)(2,1)} %copy-done.8, bf16[528,512]{1,0:T(8,128)(2,1)} %copy-done.9, bf16[528,512]{1,0:T(8,128)(2,1)} %get-tuple-element.23), kind=kOutput, calls=%fused_computation.71 | convolution fusion | flops 1666351104 | bytes 5849088 | tf_op jit(solution)/shard_map/dot_general | solution.py:39
  268.7 1.5 collective-permute-start.5
  270.5 1.2 reduce.3
  271.8 4.1 %multiply_reduce_fusion = (bf16[1024]{0:T(1024)(128)(2,1)S(1)}, bf16[1024]{0:T(1024)(128)(2,1)S(1)}, bf16[1,528,1024]{2,1,0:T(8,128)(2,1)}) fusion(bf16[528,1024]{1,0:T(8,128)(2,1)} %collective-permute-done.2, bf16[528,1024]{1,0:T(8,128)(2,1)} %fusion.48, f32[1,528,1024]{2,1,0:T(8,128)} %param.33, f32[1024]{0:T(1024)S(1)} %get-tuple-element.113, ...), kind=kLoop, calls=%fused_computation.43 | loop fusion | flops 6486016 | bytes 7583808 | tf_op jit(solution)/shard_map/reduce_sum | solution.py:346
  276.1 15.7 %collective-permute-done.5 = bf16[528,1024]{1,0:T(8,128)(2,1)} collective-permute-done((bf16[528,1024]{1,0:T(8,128)(2,1)}, bf16[528,1024]{1,0:T(8,128)(2,1)}, u32[]{:S(2)}, u32[]{:S(2)}) %collective-permute-start.5) | collective-permute-done | bytes 1081376 | tf_op jit(solution)/shard_map/ppermute | solution.py:44
  291.9 2.8 fusion.32
  296.7 5.8 %all-to-all-start = ((bf16[8,2,704]{2,1,0:T(2,128)(2,1)}), bf16[8,2,704]{2,1,0:T(2,128)(2,1)S(1)}, u32[]{:S(2)}, u32[]{:S(2)}) async-start(bf16[8,2,704]{2,1,0:T(2,128)(2,1)} %reshape.415), calls=%async_computation | async-start | bytes 49152 | tf_op jit(solution)/shard_map/all_to_all | solution.py:384
  302.4 5.7 %all-to-all-done = bf16[8,2,704]{2,1,0:T(2,128)(2,1)S(1)} async-done(((bf16[8,2,704]{2,1,0:T(2,128)(2,1)}), bf16[8,2,704]{2,1,0:T(2,128)(2,1)S(1)}, u32[]{:S(2)}, u32[]{:S(2)}) %all-to-all-start) | async-done | bytes 22560 | tf_op jit(solution)/shard_map/all_to_all | solution.py:384
  308.5 1.9 collective-permute-start.8
  310.4 4.1 %fusion.57 = bf16[1,528,1024]{2,1,0:T(8,128)(2,1)} fusion(f32[528,1024]{1,0:T(8,128)} %get-tuple-element.104, f32[528]{0:T(1024)S(1)} %broadcast_multiply_fusion, f32[528]{0:T(1024)S(1)} %broadcast_multiply_fusion.5, bf16[1,528,1024]{2,1,0:T(8,128)(2,1)S(1)} %copy-done.3, f32[528]{0:T(1024)S(1)} %broadcast_multiply_fusion.1, ...), kind=kLoop, calls=%fused_computation.83 | loop fusion | flops 7028736 | bytes 6500608 | tf_op jit(solution)/shard_map/reshape | solution.py:368
  314.7 8.8 %collective-permute-done.8 = bf16[128,2048]{1,0:T(8,128)(2,1)S(1)} collective-permute-done((bf16[128,2048]{1,0:T(8,128)(2,1)}, bf16[128,2048]{1,0:T(8,128)(2,1)S(1)}, u32[]{:S(2)}, u32[]{:S(2)}) %collective-permute-start.8) | collective-permute-done | bytes 524320 | tf_op jit(solution)/shard_map/ppermute | solution.py:44
  323.6 12.7 %collective-permute-done.7 = bf16[128,2560]{1,0:T(8,128)(2,1)S(1)} collective-permute-done((bf16[128,2560]{1,0:T(8,128)(2,1)}, bf16[128,2560]{1,0:T(8,128)(2,1)S(1)}, u32[]{:S(2)}, u32[]{:S(2)}) %collective-permute-start.7) | collective-permute-done | bytes 655392 | tf_op jit(solution)/shard_map/ppermute | solution.py:44
  336.5 1.7 collective-permute-start.9
  340.2 1.3 copy.77
  343.4 3.3 collective-permute-done.9
  (157 shorter events, 17.6 us)
Async XLA Ops:
  7.2 3.3 copy-start
  7.2 3.7 %copy-start.12 = (bf16[128,2048]{1,0:T(8,128)(2,1)S(1)}, bf16[128,2048]{1,0:T(8,128)(2,1)}, u32[]{:S(2)}) copy-start(bf16[128,2048]{1,0:T(8,128)(2,1)} %param.28) | copy-start | bytes 1572868
  7.2 54.0 %all-gather.5.cloned.1.call-start = ((), (), s32[]{:S(2)}) async-start(), calls=%async_computation.4 | async-start | bytes 4718592 | tf_op jit(solution)/shard_map/all_gather | solution.py:276
  10.3 1.6 copy-start.13
  10.3 1.7 copy-start.14
  10.3 1.9 copy-start.15
  10.3 2.1 copy-start.16
  10.3 2.5 copy-start.17
  10.3 2.7 copy-start.18
  10.3 3.0 copy-start.19
  10.3 3.2 copy-start.20
  10.3 3.6 %copy-start.21 = (bf16[128]{0:T(256)(128)(2,1)S(1)}, bf16[128]{0:T(256)(128)(2,1)}, u32[]{:S(2)}) copy-start(bf16[128]{0:T(256)(128)(2,1)} %param.31) | copy-start | bytes 772
  10.4 3.8 %copy-start.22 = (bf16[128]{0:T(256)(128)(2,1)S(1)}, bf16[128]{0:T(256)(128)(2,1)}, u32[]{:S(2)}) copy-start(bf16[128]{0:T(256)(128)(2,1)} %param.32) | copy-start | bytes 772
  10.4 130.8 %all-gather.7.cloned.1.call-start = ((), (), s32[]{:S(2)}) async-start(), calls=%async_computation.5 | async-start | bytes 8912896 | tf_op jit(solution)/shard_map/all_gather | solution.py:282
  10.5 20.5 %copy-start.3 = (bf16[1,528,1024]{2,1,0:T(8,128)(2,1)S(1)}, bf16[1,528,1024]{2,1,0:T(8,128)(2,1)}, u32[]{:S(2)}) copy-start(bf16[1,528,1024]{2,1,0:T(8,128)(2,1)} %param.17) | copy-start | bytes 3244036
  11.8 296.7 %reduce-scatter.8.cloned.1.call-start = ((), (), s32[]{:S(2)}) async-start(), calls=%async_computation.8 | async-start | bytes 4718592 | tf_op jit(solution)/shard_map/reduce_scatter | solution.py:327
  61.2 4.6 %copy-start.2 = (s32[1,2]{1,0:T(1,128)S(1)}, s32[1,2]{1,0:T(1,128)}, u32[]{:S(2)}) copy-start(s32[1,2]{1,0:T(1,128)} %param.18) | copy-start | bytes 28
  64.2 5.7 %copy-start.24 = (bf16[528,1024]{1,0:T(8,128)(2,1)}, bf16[528,1024]{1,0:T(8,128)(2,1)S(1)}, u32[]{:S(2)}) copy-start(bf16[528,1024]{1,0:T(8,128)(2,1)S(1)} %add_convert_fusion.3.refs_2_.refs_4_.refs_3_.refs_5_) | copy-start | bytes 3244036
  64.2 31.8 %collective-permute-start = (bf16[528,1024]{1,0:T(8,128)(2,1)S(1)}, bf16[528,1024]{1,0:T(8,128)(2,1)}, u32[]{:S(2)}, u32[]{:S(2)}) collective-permute-start(bf16[528,1024]{1,0:T(8,128)(2,1)S(1)} %add_convert_fusion.3.refs_2_.refs_4_.refs_3_.refs_5_), channel_id=1, source_target_pairs={{0,2},{2,0},{1,3},{3,1},{4,6},{6,4},{5,7},{7,5},{8,10},{10,8},{9,1... | collective-permute-start | bytes 3244040 | tf_op jit(solution)/shard_map/ppermute | solution.py:66
  110.0 4.9 %copy-start.23 = (s32[2]{0:T(128)S(1)}, s32[2]{0:T(128)}, u32[]{:S(2)}) copy-start(s32[2]{0:T(128)} %and_select_fusion.1.refs_0_) | copy-start | bytes 28
  113.1 25.5 %collective-permute-start.1 = (bf16[528,1024]{1,0:T(8,128)(2,1)}, bf16[528,1024]{1,0:T(8,128)(2,1)}, u32[]{:S(2)}, u32[]{:S(2)}) collective-permute-start(bf16[528,1024]{1,0:T(8,128)(2,1)} %convolution_convert_fusion.3), channel_id=1, source_target_pairs={{0,1},{1,0},{2,3},{3,2},{4,5},{5,4},{6,7},{7,6},{8,9},{9,8},{10,11... | collective-permute-start | bytes 3244040 | tf_op jit(solution)/shard_map/ppermute | solution.py:44
  141.2 7.5 %copy-start.4 = (f32[1,528,1024]{2,1,0:T(8,128)S(1)}, f32[1,528,1024]{2,1,0:T(8,128)}, u32[]{:S(2)}) copy-start(f32[1,528,1024]{2,1,0:T(8,128)} %param.33) | copy-start | bytes 6488068
  147.4 1.3 copy-start.26
  153.9 160.6 %reduce-scatter.6.cloned.1.call-start = ((), (), s32[]{:S(2)}) async-start(), calls=%async_computation.7 | async-start | bytes 5898240 | tf_op jit(solution)/shard_map/reduce_scatter | solution.py:327
  161.4 6.4 %copy-start.27 = (bf16[528,2048]{1,0:T(8,128)(2,1)S(1)}, bf16[528,2048]{1,0:T(8,128)(2,1)}, u32[]{:S(2)}) copy-start(bf16[528,2048]{1,0:T(8,128)(2,1)} %copy-done.26) | copy-start | bytes 6488068
  166.3 24.4 %collective-permute-start.3 = (bf16[528,1024]{1,0:T(8,128)(2,1)S(1)}, bf16[528,1024]{1,0:T(8,128)(2,1)S(1)}, u32[]{:S(2)}, u32[]{:S(2)}) collective-permute-start(bf16[528,1024]{1,0:T(8,128)(2,1)S(1)} %fusion.45), channel_id=1, source_target_pairs={{0,1},{1,0},{2,3},{3,2},{4,5},{5,4},{6,7},{7,6},{8,9},{9,8},{10,11... | collective-permute-start | bytes 3244040 | tf_op jit(solution)/shard_map/ppermute | solution.py:44
  177.5 14.4 %copy-start.5 = (f32[1,528,1024]{2,1,0:T(8,128)S(1)}, f32[1,528,1024]{2,1,0:T(8,128)}, u32[]{:S(2)}) copy-start(f32[1,528,1024]{2,1,0:T(8,128)} %param.33) | copy-start | bytes 6488068
  191.9 4.0 %copy-start.25 = (bf16[528,512]{1,0:T(8,128)(2,1)S(1)}, bf16[528,512]{1,0:T(8,128)(2,1)}, u32[]{:S(2)}) copy-start(bf16[528,512]{1,0:T(8,128)(2,1)} %attend.1) | copy-start | bytes 1622020
  201.3 135.2 %reduce-scatter.4.cloned.1.call-start = ((), (), s32[]{:S(2)}) async-start(), calls=%async_computation.6 | async-start | bytes 3538944 | tf_op jit(solution)/shard_map/reduce_scatter | solution.py:327
  231.2 23.8 %collective-permute-start.4 = (bf16[2,528,512]{2,1,0:T(8,128)(2,1)}, bf16[2,528,512]{2,1,0:T(8,128)(2,1)S(1)}, u32[]{:S(2)}, u32[]{:S(2)}) collective-permute-start(bf16[2,528,512]{2,1,0:T(8,128)(2,1)} %get-tuple-element.26), channel_id=1, source_target_pairs={{0,2},{2,0},{1,3},{3,1},{4,6},{6,4},{5,7},{7,5},{8,10},{10,8},{9,1... | collective-permute-start | bytes 3244040 | tf_op jit(solution)/shard_map/ppermute | solution.py:66
  232.7 37.8 %collective-permute-start.2 = (bf16[528,1024]{1,0:T(8,128)(2,1)}, bf16[528,1024]{1,0:T(8,128)(2,1)}, u32[]{:S(2)}, u32[]{:S(2)}) collective-permute-start(bf16[528,1024]{1,0:T(8,128)(2,1)} %fusion.48), channel_id=1, source_target_pairs={{0,1},{1,0},{2,3},{3,2},{4,5},{5,4},{6,7},{7,6},{8,9},{9,8},{10,11... | collective-permute-start | bytes 3244040 | tf_op jit(solution)/shard_map/ppermute | solution.py:44
  257.0 1.2 copy-start.7
  257.2 0.8 copy-start.8
  257.2 1.0 copy-start.9
  268.7 23.1 %collective-permute-start.5 = (bf16[528,1024]{1,0:T(8,128)(2,1)}, bf16[528,1024]{1,0:T(8,128)(2,1)}, u32[]{:S(2)}, u32[]{:S(2)}) collective-permute-start(bf16[528,1024]{1,0:T(8,128)(2,1)} %fusion.42), channel_id=1, source_target_pairs={{0,1},{1,0},{2,3},{3,2},{4,5},{5,4},{6,7},{7,6},{8,9},{9,8},{10,11... | collective-permute-start | bytes 3244040 | tf_op jit(solution)/shard_map/ppermute | solution.py:44
  296.7 11.4 %all-to-all-start = ((bf16[8,2,704]{2,1,0:T(2,128)(2,1)}), bf16[8,2,704]{2,1,0:T(2,128)(2,1)S(1)}, u32[]{:S(2)}, u32[]{:S(2)}) async-start(bf16[8,2,704]{2,1,0:T(2,128)(2,1)} %reshape.415), calls=%async_computation | async-start | bytes 49152 | tf_op jit(solution)/shard_map/all_to_all | solution.py:384
  308.3 6.4 %collective-permute-start.6 = (bf16[1408]{0:T(1024)(128)(2,1)S(1)}, bf16[1408]{0:T(1024)(128)(2,1)S(1)}, u32[]{:S(2)}, u32[]{:S(2)}) collective-permute-start(bf16[1408]{0:T(1024)(128)(2,1)S(1)} %reduce_sum.202), channel_id=1, source_target_pairs={{0,2},{2,0},{1,3},{3,1},{4,6},{6,4},{5,7},{7,5},{8,10},{10,8},{9,1... | collective-permute-start | bytes 8456 | tf_op jit(solution)/shard_map/ppermute | solution.py:44
  308.5 15.0 %copy-start.10 = (bf16[128,2048]{1,0:T(8,128)(2,1)S(1)}, bf16[128,2048]{1,0:T(8,128)(2,1)}, u32[]{:S(2)}) copy-start(bf16[128,2048]{1,0:T(8,128)(2,1)} %reduce-scatter.8.cloned.1.call-done) | copy-start | bytes 1572868
  308.5 15.0 %collective-permute-start.8 = (bf16[128,2048]{1,0:T(8,128)(2,1)}, bf16[128,2048]{1,0:T(8,128)(2,1)S(1)}, u32[]{:S(2)}, u32[]{:S(2)}) collective-permute-start(bf16[128,2048]{1,0:T(8,128)(2,1)} %reduce-scatter.8.cloned.1.call-done), channel_id=1, source_target_pairs={{0,2},{2,0},{1,3},{3,1},{4,6},{6,4},{5,7},{7,5},{8,10},{10,8},{9,1... | collective-permute-start | bytes 1572872 | tf_op jit(solution)/shard_map/ppermute | solution.py:44
  314.5 21.8 %copy-start.6 = (bf16[128,2560]{1,0:T(8,128)(2,1)S(1)}, bf16[128,2560]{1,0:T(8,128)(2,1)}, u32[]{:S(2)}) copy-start(bf16[128,2560]{1,0:T(8,128)(2,1)} %reduce-scatter.6.cloned.1.call-done) | copy-start | bytes 1966084
  314.5 21.8 %collective-permute-start.7 = (bf16[128,2560]{1,0:T(8,128)(2,1)}, bf16[128,2560]{1,0:T(8,128)(2,1)S(1)}, u32[]{:S(2)}, u32[]{:S(2)}) collective-permute-start(bf16[128,2560]{1,0:T(8,128)(2,1)} %reduce-scatter.6.cloned.1.call-done), channel_id=1, source_target_pairs={{0,2},{2,0},{1,3},{3,1},{4,6},{6,4},{5,7},{7,5},{8,10},{10,8},{9,1... | collective-permute-start | bytes 1966088 | tf_op jit(solution)/shard_map/ppermute | solution.py:44
  336.5 10.2 %collective-permute-start.9 = (bf16[128,1536]{1,0:T(8,128)(2,1)}, bf16[128,1536]{1,0:T(8,128)(2,1)S(1)}, u32[]{:S(2)}, u32[]{:S(2)}) collective-permute-start(bf16[128,1536]{1,0:T(8,128)(2,1)} %reduce-scatter.4.cloned.1.call-done), channel_id=1, source_target_pairs={{0,2},{2,0},{1,3},{3,1},{4,6},{6,4},{5,7},{7,5},{8,10},{10,8},{9,1... | collective-permute-start | bytes 1179656 | tf_op jit(solution)/shard_map/ppermute | solution.py:44
  340.2 6.6 %copy-start.11 = (bf16[128,1536]{1,0:T(8,128)(2,1)S(1)}, bf16[128,1536]{1,0:T(8,128)(2,1)}, u32[]{:S(2)}) copy-start(bf16[128,1536]{1,0:T(8,128)(2,1)} %reduce-scatter.4.cloned.1.call-done) | copy-start | bytes 1179652
  342.5 5.7 %copy-start.1 = (bf16[2048,128]{1,0:T(8,128)(2,1)S(1)}, bf16[2048,128]{1,0:T(8,128)(2,1)}, u32[]{:S(2)}) copy-start(bf16[2048,128]{1,0:T(8,128)(2,1)} %param.30) | copy-start | bytes 1572868
Sparse Core Ops, SparseCore 0:
  10.5 50.6 all-gather.4
  64.0 75.3 all-gather.6
  154.0 48.1 reduce-scatter.7
  204.3 58.2 reduce-scatter.5
  264.8 38.8 reduce-scatter.3

commit v4 on v3

--- a/solution.py
+++ b/solution.py
@@ -66,60 +66,61 @@
     return lax.ppermute(value, axis, [(i, (i + step) % size) for i in range(size)])
 
 
-def lane_masks(rows, width, head_size):
+def head_mask(rows, width, head_size, head):
     lane = lax.broadcasted_iota(jnp.int32, (rows, width), 1)
-    return [
-        (lane // head_size == i).astype(f32) for i in range(width // head_size)
-    ]
-
-
-def scores_by_key(keys, query, usable):
-    scores = dot(keys, query, ((1,), (1,)))
-    return jnp.where(usable, scores, negative)
+    return (lane // head_size == head).astype(f32)
 
 
 def forward_kernel(live_ref, query_ref, *rest, head_size, blocks):
     key_refs, value_refs, out_ref = rest[:blocks], rest[blocks : 2 * blocks], rest[-1]
     rows, width = query_ref.shape
-    masks = lane_masks(rows, width, head_size)
-    query = query_ref[...].astype(f32) * head_size ** (-0.5)
-    keys = jnp.concatenate([ref[...] for ref in key_refs], axis=0)
-    values = jnp.concatenate([ref[...] for ref in value_refs], axis=0)
     column = lax.broadcasted_iota(jnp.int32, (1, blocks * rows), 1)
     usable = column < 0
     for i in range(blocks):
         usable = usable | ((column >= i * rows) & (column < i * rows + live_ref[i]))
-    result = jnp.zeros((rows, width), f32)
-    for mask in masks:
-        scores = dot((query * mask).astype(bf16), keys, ((1,), (1,)))
+    out_ref[...] = jnp.zeros((rows, width), bf16)
+
+    def one_head(head, carry):
+        mask = head_mask(rows, width, head_size, head)
+        query = query_ref[...].astype(f32) * (mask * head_size ** (-0.5))
+        keys = jnp.concatenate([ref[...] for ref in key_refs], axis=0)
+        values = jnp.concatenate([ref[...] for ref in value_refs], axis=0)
+        scores = dot(query.astype(bf16), keys, ((1,), (1,)))
         scores = jnp.where(usable, scores, negative)
         maximum = jnp.max(scores, axis=-1, keepdims=True)
         exponent = jnp.exp(scores - maximum)
         summed = jnp.sum(exponent, axis=-1, keepdims=True)
         weights = (exponent * (1.0 / summed)).astype(bf16)
-        result = result + dot(weights, values, ((1,), (0,))) * mask
-    out_ref[...] = result.astype(bf16)
+        result = dot(weights, values, ((1,), (0,))) * mask
+        out_ref[...] = (out_ref[...].astype(f32) + result).astype(bf16)
+        return carry
+
+    lax.fori_loop(0, width // head_size, one_head, 0)
 
 
 def backward_kernel(live_ref, query_ref, grad_ref, *rest, head_size, blocks):
     key_refs, value_refs = rest[:blocks], rest[blocks : 2 * blocks]
-    query_grad_ref, own_ref = rest[2 * blocks], rest[2 * blocks + 1]
-    other_refs = rest[2 * blocks + 2 :]
+    query_grad_ref = rest[2 * blocks]
+    grad_refs = rest[2 * blocks + 1 :]
     rows, width = query_ref.shape
     scaling = head_size ** (-0.5)
-    masks = lane_masks(rows, width, head_size)
-    query = query_ref[...].astype(f32)
-    grads = grad_ref[...].astype(f32)
     key_position = lax.broadcasted_iota(jnp.int32, (rows, 1), 0)
-    query_grad = jnp.zeros((rows, width), f32)
-    key_grads = [jnp.zeros((rows, width), f32) for _ in range(blocks)]
-    value_grads = [jnp.zeros((rows, width), f32) for _ in range(blocks)]
-    for mask in masks:
+    query_grad_ref[...] = jnp.zeros((rows, width), query_grad_ref.dtype)
+    for ref in grad_refs:
+        ref[...] = jnp.zeros((2, rows, width), ref.dtype)
+
+    def one_head(head, carry):
+        mask = head_mask(rows, width, head_size, head)
+        query = query_ref[...].astype(f32)
         head_query = (query * mask).astype(bf16)
         scaled_query = (query * (mask * scaling)).astype(bf16)
-        head_grads = (grads * mask).astype(bf16)
+        head_grads = (grad_ref[...].astype(f32) * mask).astype(bf16)
         scores = [
-            scores_by_key(key_refs[i][...], scaled_query, key_position < live_ref[i])
+            jnp.where(
+                key_position < live_ref[i],
+                dot(key_refs[i][...], scaled_query, ((1,), (1,))),
+                negative,
+            )
             for i in range(blocks)
         ]
         maximum = scores[0].max(axis=0, keepdims=True)
@@ -133,19 +134,18 @@
         row_total = sum(
             (p * d).sum(axis=0, keepdims=True) for p, d in zip(probabilities, dprobs)
         )
-        for i in range(blocks):
-            value_grads[i] = value_grads[i] + dot(
-                probabilities[i].astype(bf16), head_grads, ((1,), (0,))
-            )
+        query_grad = query_grad_ref[...].astype(f32)
+        for i, ref in enumerate(grad_refs):
+            value_grad = dot(probabilities[i].astype(bf16), head_grads, ((1,), (0,)))
+            ref[1] = (ref[1].astype(f32) + value_grad).astype(ref.dtype)
             dscores = (probabilities[i] * (dprobs[i] - row_total) * scaling).astype(bf16)
-            key_grads[i] = key_grads[i] + dot(dscores, head_query, ((1,), (0,)))
+            key_grad = dot(dscores, head_query, ((1,), (0,)))
+            ref[0] = (ref[0].astype(f32) + key_grad).astype(ref.dtype)
             query_grad = query_grad + dot(dscores, key_refs[i][...], ((0,), (0,))) * mask
-    query_grad_ref[...] = query_grad.astype(bf16)
-    own_ref[0] = key_grads[0]
-    own_ref[1] = value_grads[0]
-    for i, ref in enumerate(other_refs):
-        ref[0] = key_grads[i + 1].astype(bf16)
-        ref[1] = value_grads[i + 1].astype(bf16)
+        query_grad_ref[...] = query_grad.astype(bf16)
+        return carry
+
+    lax.fori_loop(0, width // head_size, one_head, 0)
 
 
 def column_block(rows, width, first):
@@ -348,20 +348,24 @@
         own_grad = own_grad + ring_shift(item, "ctx", -(step + 1)).astype(f32)
     own_low = own_grad.astype(bf16)
     dqkv = jnp.concatenate([query_grad, own_low[0], own_low[1]], axis=1)
-    dnorm_local = dot(dqkv, qkv_matrix, ((1,), (1,))).astype(bf16)
-    dnorm_one = exchange_sum(dnorm_local, "tp")
+    dnorm_local = dot(dqkv, qkv_matrix, ((1,), (1,)))
+    grad_gain_one = jnp.sum(dnorm_local * unit_one, axis=0)
+    grad_shift_one = jnp.sum(dnorm_local, axis=0)
+    dnorm_low = dnorm_local.astype(bf16)
+    dnorm_other = swap_pair(dnorm_low, "tp")
+    dnorm_one = pair_sum(dnorm_low, dnorm_other, "tp")
     qkv_part = dot(low_one, dqkv, ((0,), (0,))).astype(bf16)
     qkv_shard = reduce_shards(qkv_part)
-    grad_down = exchange_sum(down_shard, "ctx").T
-    up_sum = exchange_sum(up_shard, "ctx")
+    down_other = swap_pair(down_shard, "ctx")
+    up_other = swap_pair(up_shard, "ctx")
+    grad_down = pair_sum(down_shard, down_other, "ctx").T
+    up_sum = pair_sum(up_shard, up_other, "ctx")
     grad_up = up_sum[:, :inner]
     grad_proj = up_sum[:, inner:].T
     grad_qkv = exchange_sum(after(qkv_shard, up_sum, grad_down), "ctx")
     grad_qkv_bias = jnp.stack(
         [jnp.sum(query_grad.astype(f32), axis=0), jnp.sum(own_low[1].astype(f32), axis=0)]
     )
-    grad_gain_one = jnp.sum(dnorm_one * unit_one, axis=0)
-    grad_shift_one = jnp.sum(dnorm_one, axis=0)
     dinput = (
         (dresid + normalize_back(dnorm_one, unit_one, inverse_one, gain_one))
         .astype(bf16)
@@ -382,7 +386,11 @@
     ]
     sent_small = jnp.concatenate([item.reshape(shards, -1) for item in pieces], axis=1)
     got = lax.all_to_all(sent_small.astype(bf16), "fsdp", split_axis=0, concat_axis=0, tiled=True)
-    total = exchange_sum(jnp.sum(got.astype(f32), axis=0).astype(bf16), "ctx")
+    total = jnp.sum(got.astype(f32), axis=0).astype(bf16)
+    total = exchange_sum(total, "ctx")
+    halves = sizes[0] + sizes[1]
+    first_part = exchange_sum(total[:halves].astype(bf16), "tp")
+    total = jnp.concatenate([first_part, total[halves:]])
     results = []
     offset = 0
     for item, size in zip(small, sizes):

time: 359 us -> 352 us (0.981)
  waiting for transfers between devices: 160 us -> 141 us
  blocking collectives: 16.3 us -> 25.5 us
  Pallas kernels: 40.2 us -> 45.8 us
  starting transfers between devices: 19.6 us -> 15.8 us
    ppermute x8 -> x9, waiting for transfers between devices: 77.4 us -> 63.8 us  [swap_pair(): return lax.ppermute(part, axis, [(0, 1), (1, 0)])]
    all_to_all x0 -> x1, blocking collectives: none -> 9.17 us  [body(): lax.all_to_all(sent_small.astype(bf16), 'fsdp', split_axis=0, concat_axis...]
    all_to_all x1 -> x0, starting transfers between devices: 5.75 us -> none  [body(): lax.all_to_all(sent_small.astype(bf16), 'fsdp', split_axis=0, concat_axis...]
    all_to_all x1 -> x0, waiting for transfers between devices: 5.68 us -> none  [body(): lax.all_to_all(sent_small.astype(bf16), 'fsdp', split_axis=0, concat_axis...]
    pallas_call x1, Pallas kernels: 14 us -> 18.4 us  [attend(): pl.pallas_call(lambda *refs: forward_kernel(*refs, head_size=head_size, b...]
    ppermute x8 -> x9, starting transfers between devices: 9.91 us -> 11.9 us  [swap_pair(): return lax.ppermute(part, axis, [(0, 1), (1, 0)])]
    unnamed x85 -> x87, local copies, waits for them, and re-layouts: 10.8 us -> 11.5 us
  transfers between devices with their start and end apart: 16 -> 16, of which waited for: 10 -> 9; matrix products, arithmetic and copies ran while one was open for 24% -> 25% of each run, Pallas kernels for 11% -> 13%
where the time goes in v4:
time: 352 us; the launch traced here: 348 us
  waiting for transfers between devices  141 us (40%)
  matrix products  57.1 us (16%)
  Pallas kernels  45.8 us (13%)
  other arithmetic  31.1 us (9%)
  blocking collectives  25.5 us (7%)
  local copies, waits for them, and re-layouts  17.6 us (5%)
  starting transfers between devices  15.8 us (4%)
  between operations  14.6 us (4%)
    ppermute x9, waiting for transfers between devices, swap_pair(): return lax.ppermute(part, axis, [(0, 1), (1, 0)])  63.8 us
    dot_general x13, matrix products, dot(): lax.dot_general(left, right, (dims, ((), ())), preferred_element_type=f32)  57.1 us
    ppermute x2, waiting for transfers between devices, ring_shift(): lax.ppermute(value, axis, [(i, (i + step) % size) for i in range(size)])  47 us
    all_gather x1, waiting for transfers between devices, body(): attn_full = lax.all_gather(attn_part, 'fsdp', axis=0, tiled=True)  29.6 us
    pallas_call x1, Pallas kernels, attend_back(): pl.pallas_call(lambda *refs: backward_kernel(*refs, head_size=head_size,...  27.4 us
    pallas_call x1, Pallas kernels, attend(): pl.pallas_call(lambda *refs: forward_kernel(*refs, head_size=head_size, b...  18.4 us
    all_gather x1, blocking collectives, body(): gathered = lax.all_gather(packed, 'fsdp', axis=0)  16.3 us
    ppermute x9, starting transfers between devices, swap_pair(): return lax.ppermute(part, axis, [(0, 1), (1, 0)])  11.9 us
  transfers between devices with their start and end apart: 16, of which 9 were waited for; matrix products, arithmetic and copies ran while one was open for 25% of the time, Pallas kernels for 13%

profile of v4, /device:TPU:0, one launch (start us, length us, event | category | flops | bytes accessed | tf_op | source)
XLA Modules:
  0.0 348.1 jit_solution(5611949586113828883)
XLA Ops:
  7.3 1.3 copy.65
  8.6 1.7 pad_maximum_fusion.4
  14.3 16.3 %all-gather.1 = bf16[8,1,1408]{2,1,0:T(2,128)(2,1)S(1)} all-gather(bf16[1,1,1408]{2,1,0:T(2,128)(2,1)S(1)} %reshape.412), channel_id=2, replica_groups=mesh['fsdp'=8,'ctx'=2,'tp'=2] {'fsdp'}, dimensions={0}, use_global_device_ids=true | all-gather | bytes 25344 | tf_op jit(solution)/shard_map/all_gather | solution.py:254
  31.6 29.6 %all-gather.5.cloned.1.call-done = bf16[1024,2048]{0,1:T(8,128)(2,1)} async-done(((bf16[128,2048]{0,1:T(8,128)(2,1)}), bf16[1024,2048]{0,1:T(8,128)(2,1)}) %all-gather.5.cloned.1.call-update) | async-done | bytes 4194320 | tf_op jit(solution)/shard_map/all_gather | solution.py:276
  61.2 2.9 add_convert_fusion.3.refs_2_.refs_4_.refs_3_.refs_5_
  64.2 1.5 collective-permute-start
  67.0 2.8 fusion.48.refs_1_
  69.8 26.2 %collective-permute-done.refs_3_.refs_5_.refs_4_.refs_6_ = bf16[528,1024]{1,0:T(8,128)(2,1)} collective-permute-done((bf16[528,1024]{1,0:T(8,128)(2,1)S(1)}, bf16[528,1024]{1,0:T(8,128)(2,1)}, u32[]{:S(2)}, u32[]{:S(2)}) %collective-permute-start) | collective-permute-done | bytes 1081376 | tf_op jit(solution)/shard_map/ppermute | solution.py:66
  96.0 18.4 %attend.1 = bf16[528,512]{1,0:T(8,128)(2,1)} custom-call(s32[2]{0:T(128)} %and_select_fusion.1.refs_0_, bf16[528,512]{1,0:T(8,128)(2,1)} %fusion.48.refs_1_, bf16[528,1024]{1,0:T(8,128)(2,1)} %copy-done.25, bf16[528,1024]{1,0:T(8,128)(2,1)} %collective-permute-done.refs_3_.refs_5_.refs_4_.refs_6_, bf16[528,1024]{1,0:T(8,128)(2,1)} %copy-done.25, ...), custom_call_target="tpu_custom_call" | custom-call | flops 1141899264 | bytes 3244032 | tf_op jit(solution)/shard_map/attend/pallas_call | solution.py:161
  114.4 3.1 convolution_convert_fusion.3
  117.5 1.5 collective-permute-start.1
  119.4 23.6 %collective-permute-done.1 = bf16[528,1024]{1,0:T(8,128)(2,1)} collective-permute-done((bf16[528,1024]{1,0:T(8,128)(2,1)}, bf16[528,1024]{1,0:T(8,128)(2,1)}, u32[]{:S(2)}, u32[]{:S(2)}) %collective-permute-start.1) | collective-permute-done | bytes 1081376 | tf_op jit(solution)/shard_map/ppermute | solution.py:44
  143.0 2.2 fusion.74
  145.6 6.1 %multiply_convert_fusion = (bf16[528,2048]{1,0:T(8,128)(2,1)S(1)}, f32[528,2048]{1,0:T(8,128)}) fusion(f32[2048]{0:T(1024)S(1)} %reshape.399, bf16[1024,4096]{1,0:T(8,128)(2,1)} %all-gather.7.cloned.1.call-done, f32[528,1024]{1,0:T(8,128)S(1)} %get-tuple-element.106, f32[1024]{0:T(1024)S(1)} %get-tuple-element.115, f32[1024]{0:T(1024)S(1)} %get-tuple-element.116, ...), kind=kOutput, calls=%fused_computation.8 | convolution fusion | flops 2223783936 | bytes 12865664 | tf_op jit(solution)/shard_map/dot_general | solution.py:39
  151.7 1.3 copy-done.27
  153.1 5.2 %convolution_convert_fusion.1 = bf16[1024,2048]{1,0:T(8,128)(2,1)} fusion(bf16[528,2048]{1,0:T(8,128)(2,1)S(1)} %get-tuple-element.132, f32[1,528,1024]{2,1,0:T(8,128)S(1)} %copy-done.4, f32[528]{0:T(1024)S(1)} %fusion.56, f32[1024]{0:T(1024)S(1)} %get-tuple-element.117), kind=kOutput, calls=%fused_computation.11 | convolution fusion | flops 2218311680 | bytes 8525888 | tf_op jit(solution)/shard_map/dot_general | solution.py:39
  158.9 6.9 %fusion.79 = (bf16[2048]{0:T(1024)(128)(2,1)S(1)}, bf16[528,2048]{1,0:T(8,128)(2,1)S(1)}) fusion(f32[528,2048]{1,0:T(8,128)} %get-tuple-element.133, f32[2048]{0:T(1024)S(1)} %reshape.399, bf16[1024,4096]{1,0:T(8,128)(2,1)} %all-gather.7.cloned.1.call-done, f32[1,528,1024]{2,1,0:T(8,128)} %param.33, f32[528]{0:T(1024)S(1)} %fusion.56, ...), kind=kOutput, calls=%fused_computation.158 | convolution fusion | flops 2229188608 | bytes 12863552 | tf_op jit(solution)/shard_map/dot_general | solution.py:39
  165.8 4.9 %fusion.40 = bf16[528,1024]{1,0:T(8,128)(2,1)S(1)} fusion(bf16[1024,4096]{1,0:T(8,128)(2,1)} %all-gather.7.cloned.1.call-done, bf16[528,2048]{1,0:T(8,128)(2,1)S(1)} %get-tuple-element.136), kind=kOutput, calls=%fused_computation.70 | convolution fusion | flops 2215133184 | bytes 7438336 | tf_op jit(solution)/shard_map/dot_general | solution.py:39
  170.7 1.5 collective-permute-start.3
  172.2 5.6 %fusion.43 = bf16[528,1024]{1,0:T(8,128)(2,1)} fusion(bf16[528,2048]{1,0:T(8,128)(2,1)S(1)} %copy-done.28, bf16[1024,4096]{1,0:T(8,128)(2,1)} %all-gather.7.cloned.1.call-done), kind=kOutput, calls=%fused_computation.71 | convolution fusion | flops 2215133184 | bytes 7438336 | tf_op jit(solution)/shard_map/dot_general | solution.py:39
  177.8 4.0 %convolution_convert_fusion.2 = bf16[1024,2048]{1,0:T(8,128)(2,1)S(1)} fusion(bf16[528,2048]{1,0:T(8,128)(2,1)S(1)} %get-tuple-element.136, f32[528,1024]{1,0:T(8,128)S(1)} %get-tuple-element.106, f32[1024]{0:T(1024)S(1)} %get-tuple-element.115, f32[1024]{0:T(1024)S(1)} %get-tuple-element.116, f32[528]{0:T(1024)S(1)} %add_rsqrt_fusion, ...), kind=kOutput, calls=%fused_computation.12 | convolution fusion | flops 2219393024 | bytes 8532096 | tf_op jit(solution)/shard_map/dot_general | solution.py:39
  181.9 13.2 %collective-permute-done.3 = bf16[528,1024]{1,0:T(8,128)(2,1)S(1)} collective-permute-done((bf16[528,1024]{1,0:T(8,128)(2,1)S(1)}, bf16[528,1024]{1,0:T(8,128)(2,1)S(1)}, u32[]{:S(2)}, u32[]{:S(2)}) %collective-permute-start.3) | collective-permute-done | bytes 1081376 | tf_op jit(solution)/shard_map/ppermute | solution.py:44
  195.0 1.2 multiply_reduce_fusion.1
  196.3 4.0 %multiply_reduce_fusion.2 = (bf16[1024]{0:T(1024)(128)(2,1)S(1)}, bf16[1024]{0:T(1024)(128)(2,1)S(1)}, f32[528,1024]{1,0:T(8,128)}) fusion(bf16[528,1024]{1,0:T(8,128)(2,1)} %collective-permute-done.1, bf16[528,1024]{1,0:T(8,128)(2,1)} %convolution_convert_fusion.3, f32[1024]{0:T(1024)S(1)} %get-tuple-element.118, f32[1024]{0:T(1024)S(1)} %get-tuple-element.122, ...), kind=kLoop, calls=%fused_computation.45 | loop fusion | flops 10811392 | bytes 10840384 | tf_op jit(solution)/shard_map/reduce_sum | solution.py:334
  200.3 2.6 convolution_convert_fusion.4
  202.9 2.7 pad_maximum_fusion
  205.9 3.5 convolution_convert_fusion.5.refs_2_
  209.4 27.4 %attend_back.1 = (bf16[528,512]{1,0:T(8,128)(2,1)}, f32[2,528,512]{2,1,0:T(8,128)}, bf16[2,528,512]{2,1,0:T(8,128)(2,1)}) custom-call(s32[2]{0:T(128)} %and_select_fusion.1.refs_0_, bf16[528,512]{1,0:T(8,128)(2,1)} %fusion.48.refs_1_, bf16[528,512]{1,0:T(8,128)(2,1)} %convolution_convert_fusion.5.refs_2_, bf16[528,1024]{1,0:T(8,128)(2,1)} %copy-done.25, ...), custom_call_target="tpu_custom_call" | custom-call | flops 2854748160 | bytes 8110080 | tf_op jit(solution)/shard_map/attend_back/pallas_call | solution.py:187
  236.8 1.5 collective-permute-start.4
  238.2 1.5 collective-permute-start.2
  239.7 20.9 %collective-permute-done.4 = bf16[2,528,512]{2,1,0:T(8,128)(2,1)S(1)} collective-permute-done((bf16[2,528,512]{2,1,0:T(8,128)(2,1)}, bf16[2,528,512]{2,1,0:T(8,128)(2,1)S(1)}, u32[]{:S(2)}, u32[]{:S(2)}) %collective-permute-start.4) | collective-permute-done | bytes 1081376 | tf_op jit(solution)/shard_map/ppermute | solution.py:66
  260.6 2.0 add_convert_fusion
  263.7 5.1 %convolution_convert_fusion = bf16[1024,1536]{1,0:T(8,128)(2,1)} fusion(bf16[528,512]{1,0:T(8,128)(2,1)S(1)} %get-tuple-element.110, bf16[528,512]{1,0:T(8,128)(2,1)S(1)} %get-tuple-element.111, bf16[528,512]{1,0:T(8,128)(2,1)S(1)} %copy-done.9, bf16[1,528,1024]{2,1,0:T(8,128)(2,1)S(1)} %copy-done.3, f32[1024]{0:T(1024)S(1)} %get-tuple-element.120, ...), kind=kOutput, calls=%fused_computation.10 | convolution fusion | flops 1670627328 | bytes 5861504 | tf_op jit(solution)/shard_map/dot_general | solution.py:39
  269.1 1.2 reduce.3
  270.4 4.1 %multiply_reduce_fusion = (bf16[1024]{0:T(1024)(128)(2,1)S(1)}, bf16[1024]{0:T(1024)(128)(2,1)S(1)}, bf16[1,528,1024]{2,1,0:T(8,128)(2,1)}) fusion(bf16[528,1024]{1,0:T(8,128)(2,1)} %collective-permute-done.2, bf16[528,1024]{1,0:T(8,128)(2,1)} %fusion.43, f32[1,528,1024]{2,1,0:T(8,128)} %param.33, f32[1024]{0:T(1024)S(1)} %get-tuple-element.114, ...), kind=kLoop, calls=%fused_computation.43 | loop fusion | flops 6486016 | bytes 7583808 | tf_op jit(solution)/shard_map/reduce_sum | solution.py:346
  274.8 4.3 %fusion.73 = (bf16[1024]{0:T(1024)(128)(2,1)S(1)}, bf16[1024]{0:T(1024)(128)(2,1)S(1)}, bf16[528,1024]{1,0:T(8,128)(2,1)S(1)}) fusion(f32[528]{0:T(1024)S(1)} %add_rsqrt_fusion.1, f32[528]{0:T(1024)S(1)} %broadcast_multiply_fusion.5, bf16[1,528,1024]{2,1,0:T(8,128)(2,1)S(1)} %copy-done.3, bf16[1024,2048]{0,1:T(8,128)(2,1)} %all-gather.5.cloned.1.call-done, ...), kind=kOutput, calls=%fused_computation.153 | convolution fusion | flops 1669593088 | bytes 6938752 | tf_op jit(solution)/shard_map/dot_general | solution.py:39
  279.1 1.5 collective-permute-start.5
  282.0 9.2 %all_to_all.6 = bf16[8,2,704]{2,1,0:T(2,128)(2,1)S(1)} all-to-all(bf16[8,2,704]{2,1,0:T(2,128)(2,1)S(1)} %reshape.415), channel_id=1, replica_groups=mesh['fsdp'=8,'ctx'=2,'tp'=2] {'fsdp'}, dimensions={0} | all-to-all | bytes 45056 | tf_op jit(solution)/shard_map/all_to_all | solution.py:388
  291.3 1.3 collective-permute-start.6
  292.6 2.4 collective-permute-done.6
  298.0 4.1 %collective-permute-done.7 = bf16[256]{0:T(256)(128)(2,1)S(1)} collective-permute-done((bf16[256]{0:T(256)(128)(2,1)S(1)}, bf16[256]{0:T(256)(128)(2,1)S(1)}, u32[]{:S(2)}, u32[]{:S(2)}) %collective-permute-start.7) | collective-permute-done | bytes 544 | tf_op jit(solution)/shard_map/ppermute | solution.py:44
  302.6 1.4 collective-permute-start.9
  305.6 12.1 %collective-permute-done.9 = bf16[128,2048]{1,0:T(8,128)(2,1)} collective-permute-done((bf16[128,2048]{1,0:T(8,128)(2,1)}, bf16[128,2048]{1,0:T(8,128)(2,1)}, u32[]{:S(2)}, u32[]{:S(2)}) %collective-permute-start.9) | collective-permute-done | bytes 524320 | tf_op jit(solution)/shard_map/ppermute | solution.py:44
  317.7 2.3 add_bitcast_fusion
  320.0 8.4 %collective-permute-done.8 = bf16[128,2560]{1,0:T(8,128)(2,1)S(1)} collective-permute-done((bf16[128,2560]{1,0:T(8,128)(2,1)}, bf16[128,2560]{1,0:T(8,128)(2,1)S(1)}, u32[]{:S(2)}, u32[]{:S(2)}) %collective-permute-start.8) | collective-permute-done | bytes 655392 | tf_op jit(solution)/shard_map/ppermute | solution.py:44
  328.7 1.5 collective-permute-start.10
  330.2 4.1 %fusion.52 = bf16[1,528,1024]{2,1,0:T(8,128)(2,1)} fusion(f32[528,1024]{1,0:T(8,128)} %get-tuple-element.104, f32[528]{0:T(1024)S(1)} %broadcast_multiply_fusion, f32[528]{0:T(1024)S(1)} %broadcast_multiply_fusion.5, bf16[1,528,1024]{2,1,0:T(8,128)(2,1)S(1)} %copy-done.3, f32[528]{0:T(1024)S(1)} %broadcast_multiply_fusion.1, ...), kind=kLoop, calls=%fused_computation.80 | loop fusion | flops 7028736 | bytes 6500608 | tf_op jit(solution)/shard_map/reshape | solution.py:372
  334.3 2.6 copy.77
  (163 shorter events, 20.6 us)
Async XLA Ops:
  7.2 3.3 copy-start
  7.2 3.7 %copy-start.13 = (bf16[128,2048]{1,0:T(8,128)(2,1)S(1)}, bf16[128,2048]{1,0:T(8,128)(2,1)}, u32[]{:S(2)}) copy-start(bf16[128,2048]{1,0:T(8,128)(2,1)} %param.28) | copy-start | bytes 1572868
  7.2 54.0 %all-gather.5.cloned.1.call-start = ((), (), s32[]{:S(2)}) async-start(), calls=%async_computation.4 | async-start | bytes 4718592 | tf_op jit(solution)/shard_map/all_gather | solution.py:276
  10.3 1.6 copy-start.14
  10.3 1.7 copy-start.15
  10.3 1.9 copy-start.16
  10.3 2.1 copy-start.17
  10.3 2.5 copy-start.18
  10.3 2.7 copy-start.19
  10.3 3.0 copy-start.20
  10.3 3.2 copy-start.21
  10.3 3.6 %copy-start.22 = (bf16[128]{0:T(256)(128)(2,1)S(1)}, bf16[128]{0:T(256)(128)(2,1)}, u32[]{:S(2)}) copy-start(bf16[128]{0:T(256)(128)(2,1)} %param.31) | copy-start | bytes 772
  10.4 3.8 %copy-start.23 = (bf16[128]{0:T(256)(128)(2,1)S(1)}, bf16[128]{0:T(256)(128)(2,1)}, u32[]{:S(2)}) copy-start(bf16[128]{0:T(256)(128)(2,1)} %param.32) | copy-start | bytes 772
  10.4 135.2 %all-gather.7.cloned.1.call-start = ((), (), s32[]{:S(2)}) async-start(), calls=%async_computation.5 | async-start | bytes 8912896 | tf_op jit(solution)/shard_map/all_gather | solution.py:282
  10.5 20.5 %copy-start.3 = (bf16[1,528,1024]{2,1,0:T(8,128)(2,1)S(1)}, bf16[1,528,1024]{2,1,0:T(8,128)(2,1)}, u32[]{:S(2)}) copy-start(bf16[1,528,1024]{2,1,0:T(8,128)(2,1)} %param.17) | copy-start | bytes 3244036
  11.8 290.8 %reduce-scatter.8.cloned.1.call-start = ((), (), s32[]{:S(2)}) async-start(), calls=%async_computation.8 | async-start | bytes 4718592 | tf_op jit(solution)/shard_map/reduce_scatter | solution.py:327
  61.2 4.6 %copy-start.2 = (s32[1,2]{1,0:T(1,128)S(1)}, s32[1,2]{1,0:T(1,128)}, u32[]{:S(2)}) copy-start(s32[1,2]{1,0:T(1,128)} %param.18) | copy-start | bytes 28
  64.2 5.7 %copy-start.25 = (bf16[528,1024]{1,0:T(8,128)(2,1)}, bf16[528,1024]{1,0:T(8,128)(2,1)S(1)}, u32[]{:S(2)}) copy-start(bf16[528,1024]{1,0:T(8,128)(2,1)S(1)} %add_convert_fusion.3.refs_2_.refs_4_.refs_3_.refs_5_) | copy-start | bytes 3244036
  64.2 31.8 %collective-permute-start = (bf16[528,1024]{1,0:T(8,128)(2,1)S(1)}, bf16[528,1024]{1,0:T(8,128)(2,1)}, u32[]{:S(2)}, u32[]{:S(2)}) collective-permute-start(bf16[528,1024]{1,0:T(8,128)(2,1)S(1)} %add_convert_fusion.3.refs_2_.refs_4_.refs_3_.refs_5_), channel_id=1, source_target_pairs={{0,2},{2,0},{1,3},{3,1},{4,6},{6,4},{5,7},{7,5},{8,10},{10,8},{9,1... | collective-permute-start | bytes 3244040 | tf_op jit(solution)/shard_map/ppermute | solution.py:66
  114.4 4.9 %copy-start.24 = (s32[2]{0:T(128)S(1)}, s32[2]{0:T(128)}, u32[]{:S(2)}) copy-start(s32[2]{0:T(128)} %and_select_fusion.1.refs_0_) | copy-start | bytes 28
  117.5 25.5 %collective-permute-start.1 = (bf16[528,1024]{1,0:T(8,128)(2,1)}, bf16[528,1024]{1,0:T(8,128)(2,1)}, u32[]{:S(2)}, u32[]{:S(2)}) collective-permute-start(bf16[528,1024]{1,0:T(8,128)(2,1)} %convolution_convert_fusion.3), channel_id=1, source_target_pairs={{0,1},{1,0},{2,3},{3,2},{4,5},{5,4},{6,7},{7,6},{8,9},{9,8},{10,11... | collective-permute-start | bytes 3244040 | tf_op jit(solution)/shard_map/ppermute | solution.py:44
  145.6 7.5 %copy-start.4 = (f32[1,528,1024]{2,1,0:T(8,128)S(1)}, f32[1,528,1024]{2,1,0:T(8,128)}, u32[]{:S(2)}) copy-start(f32[1,528,1024]{2,1,0:T(8,128)} %param.33) | copy-start | bytes 6488068
  151.7 1.3 copy-start.27
  158.3 146.6 %reduce-scatter.6.cloned.1.call-start = ((), (), s32[]{:S(2)}) async-start(), calls=%async_computation.7 | async-start | bytes 5898240 | tf_op jit(solution)/shard_map/reduce_scatter | solution.py:327
  165.8 6.4 %copy-start.28 = (bf16[528,2048]{1,0:T(8,128)(2,1)S(1)}, bf16[528,2048]{1,0:T(8,128)(2,1)}, u32[]{:S(2)}) copy-start(bf16[528,2048]{1,0:T(8,128)(2,1)} %copy-done.27) | copy-start | bytes 6488068
  170.7 24.4 %collective-permute-start.3 = (bf16[528,1024]{1,0:T(8,128)(2,1)S(1)}, bf16[528,1024]{1,0:T(8,128)(2,1)S(1)}, u32[]{:S(2)}, u32[]{:S(2)}) collective-permute-start(bf16[528,1024]{1,0:T(8,128)(2,1)S(1)} %fusion.40), channel_id=1, source_target_pairs={{0,1},{1,0},{2,3},{3,2},{4,5},{5,4},{6,7},{7,6},{8,9},{9,8},{10,11... | collective-permute-start | bytes 3244040 | tf_op jit(solution)/shard_map/ppermute | solution.py:44
  181.9 14.4 %copy-start.5 = (f32[1,528,1024]{2,1,0:T(8,128)S(1)}, f32[1,528,1024]{2,1,0:T(8,128)}, u32[]{:S(2)}) copy-start(f32[1,528,1024]{2,1,0:T(8,128)} %param.33) | copy-start | bytes 6488068
  196.3 4.0 %copy-start.26 = (bf16[528,512]{1,0:T(8,128)(2,1)S(1)}, bf16[528,512]{1,0:T(8,128)(2,1)}, u32[]{:S(2)}) copy-start(bf16[528,512]{1,0:T(8,128)(2,1)} %attend.1) | copy-start | bytes 1622020
  205.7 123.0 %reduce-scatter.4.cloned.1.call-start = ((), (), s32[]{:S(2)}) async-start(), calls=%async_computation.6 | async-start | bytes 3538944 | tf_op jit(solution)/shard_map/reduce_scatter | solution.py:327
  236.8 23.8 %collective-permute-start.4 = (bf16[2,528,512]{2,1,0:T(8,128)(2,1)}, bf16[2,528,512]{2,1,0:T(8,128)(2,1)S(1)}, u32[]{:S(2)}, u32[]{:S(2)}) collective-permute-start(bf16[2,528,512]{2,1,0:T(8,128)(2,1)} %get-tuple-element.26), channel_id=1, source_target_pairs={{0,2},{2,0},{1,3},{3,1},{4,6},{6,4},{5,7},{7,5},{8,10},{10,8},{9,1... | collective-permute-start | bytes 3244040 | tf_op jit(solution)/shard_map/ppermute | solution.py:66
  238.2 30.9 %collective-permute-start.2 = (bf16[528,1024]{1,0:T(8,128)(2,1)}, bf16[528,1024]{1,0:T(8,128)(2,1)}, u32[]{:S(2)}, u32[]{:S(2)}) collective-permute-start(bf16[528,1024]{1,0:T(8,128)(2,1)} %fusion.43), channel_id=1, source_target_pairs={{0,1},{1,0},{2,3},{3,2},{4,5},{5,4},{6,7},{7,6},{8,9},{9,8},{10,11... | collective-permute-start | bytes 3244040 | tf_op jit(solution)/shard_map/ppermute | solution.py:44
  262.5 1.2 copy-start.9
  262.7 0.8 copy-start.10
  262.7 1.0 copy-start.11
  279.1 40.9 %copy-start.6 = (bf16[528,1024]{1,0:T(8,128)(2,1)}, bf16[528,1024]{1,0:T(8,128)(2,1)S(1)}, u32[]{:S(2)}) copy-start(bf16[528,1024]{1,0:T(8,128)(2,1)S(1)} %get-tuple-element.108) | copy-start | bytes 3244036
  279.1 25.0 %collective-permute-start.5 = (bf16[528,1024]{1,0:T(8,128)(2,1)S(1)}, bf16[528,1024]{1,0:T(8,128)(2,1)S(1)}, u32[]{:S(2)}, u32[]{:S(2)}) collective-permute-start(bf16[528,1024]{1,0:T(8,128)(2,1)S(1)} %get-tuple-element.108), channel_id=1, source_target_pairs={{0,1},{1,0},{2,3},{3,2},{4,5},{5,4},{6,7},{7,6},{8,9},{9,8},{10,11... | collective-permute-start | bytes 3244040 | tf_op jit(solution)/shard_map/ppermute | solution.py:44
  291.3 3.7 %collective-permute-start.6 = (bf16[1408]{0:T(1024)(128)(2,1)S(1)}, bf16[1408]{0:T(1024)(128)(2,1)S(1)}, u32[]{:S(2)}, u32[]{:S(2)}) collective-permute-start(bf16[1408]{0:T(1024)(128)(2,1)S(1)} %reduce_sum.202), channel_id=1, source_target_pairs={{0,2},{2,0},{1,3},{3,1},{4,6},{6,4},{5,7},{7,5},{8,10},{10,8},{9,1... | collective-permute-start | bytes 8456 | tf_op jit(solution)/shard_map/ppermute | solution.py:44
  295.0 7.1 %collective-permute-start.7 = (bf16[256]{0:T(256)(128)(2,1)S(1)}, bf16[256]{0:T(256)(128)(2,1)S(1)}, u32[]{:S(2)}, u32[]{:S(2)}) collective-permute-start(bf16[256]{0:T(256)(128)(2,1)S(1)} %slice.263), channel_id=1, source_target_pairs={{0,1},{1,0},{2,3},{3,2},{4,5},{5,4},{6,7},{7,6},{8,9},{9,8},{10,11... | collective-permute-start | bytes 1544 | tf_op jit(solution)/shard_map/ppermute | solution.py:44
  302.6 15.1 %collective-permute-start.9 = (bf16[128,2048]{1,0:T(8,128)(2,1)}, bf16[128,2048]{1,0:T(8,128)(2,1)}, u32[]{:S(2)}, u32[]{:S(2)}) collective-permute-start(bf16[128,2048]{1,0:T(8,128)(2,1)} %reduce-scatter.8.cloned.1.call-done), channel_id=1, source_target_pairs={{0,2},{2,0},{1,3},{3,1},{4,6},{6,4},{5,7},{7,5},{8,10},{10,8},{9,1... | collective-permute-start | bytes 1572872 | tf_op jit(solution)/shard_map/ppermute | solution.py:44
  304.1 16.0 %copy-start.7 = (bf16[528,1024]{1,0:T(8,128)(2,1)}, bf16[528,1024]{1,0:T(8,128)(2,1)S(1)}, u32[]{:S(2)}) copy-start(bf16[528,1024]{1,0:T(8,128)(2,1)S(1)} %collective-permute-done.5) | copy-start | bytes 3244036
  304.9 23.6 %copy-start.8 = (bf16[128,2560]{1,0:T(8,128)(2,1)S(1)}, bf16[128,2560]{1,0:T(8,128)(2,1)}, u32[]{:S(2)}) copy-start(bf16[128,2560]{1,0:T(8,128)(2,1)} %reduce-scatter.6.cloned.1.call-done) | copy-start | bytes 1966084
  304.9 23.5 %collective-permute-start.8 = (bf16[128,2560]{1,0:T(8,128)(2,1)}, bf16[128,2560]{1,0:T(8,128)(2,1)S(1)}, u32[]{:S(2)}, u32[]{:S(2)}) collective-permute-start(bf16[128,2560]{1,0:T(8,128)(2,1)} %reduce-scatter.6.cloned.1.call-done), channel_id=1, source_target_pairs={{0,2},{2,0},{1,3},{3,1},{4,6},{6,4},{5,7},{7,5},{8,10},{10,8},{9,1... | collective-permute-start | bytes 1966088 | tf_op jit(solution)/shard_map/ppermute | solution.py:44
  328.7 10.1 %collective-permute-start.10 = (bf16[128,1536]{1,0:T(8,128)(2,1)}, bf16[128,1536]{1,0:T(8,128)(2,1)}, u32[]{:S(2)}, u32[]{:S(2)}) collective-permute-start(bf16[128,1536]{1,0:T(8,128)(2,1)} %reduce-scatter.4.cloned.1.call-done), channel_id=1, source_target_pairs={{0,2},{2,0},{1,3},{3,1},{4,6},{6,4},{5,7},{7,5},{8,10},{10,8},{9,1... | collective-permute-start | bytes 1179656 | tf_op jit(solution)/shard_map/ppermute | solution.py:44
  334.3 4.5 %copy-start.12 = (bf16[128,1536]{1,0:T(8,128)(2,1)S(1)}, bf16[128,1536]{1,0:T(8,128)(2,1)}, u32[]{:S(2)}) copy-start(bf16[128,1536]{1,0:T(8,128)(2,1)} %reduce-scatter.4.cloned.1.call-done) | copy-start | bytes 1179652
  338.0 3.4 copy-start.1
Sparse Core Ops, SparseCore 0:
  10.5 50.6 all-gather.4
  64.0 75.3 all-gather.6
  158.4 48.1 reduce-scatter.7
  208.7 58.2 reduce-scatter.5
  269.2 39.4 reduce-scatter.3

commit v5 on v4

--- a/solution.py
+++ b/solution.py
@@ -5,7 +5,9 @@
 from jax import lax
 from jax.experimental import pallas as pl
 from jax.experimental.pallas import tpu as pltpu
+from jax.experimental.layout import Layout, with_layout_constraint
 from jax.sharding import PartitionSpec as P
+
 
 epsilon = 1e-06
 negative = -1e30
@@ -53,6 +55,10 @@
 
 def exchange_sum(part, axis):
     return pair_sum(part, swap_pair(part, axis), axis)
+
+
+def rows_major(matrix):
+    return with_layout_constraint(matrix, Layout(major_to_minor=(0, 1)))
 
 
 def after(value, *events):
@@ -78,24 +84,21 @@
     usable = column < 0
     for i in range(blocks):
         usable = usable | ((column >= i * rows) & (column < i * rows + live_ref[i]))
-    out_ref[...] = jnp.zeros((rows, width), bf16)
-
-    def one_head(head, carry):
+    bias = jnp.where(usable, 0.0, negative)
+    query = query_ref[...].astype(f32)
+    keys = jnp.concatenate([ref[...] for ref in key_refs], axis=0)
+    values = jnp.concatenate([ref[...] for ref in value_refs], axis=0)
+    result = jnp.zeros((rows, width), f32)
+    for head in range(width // head_size):
         mask = head_mask(rows, width, head_size, head)
-        query = query_ref[...].astype(f32) * (mask * head_size ** (-0.5))
-        keys = jnp.concatenate([ref[...] for ref in key_refs], axis=0)
-        values = jnp.concatenate([ref[...] for ref in value_refs], axis=0)
-        scores = dot(query.astype(bf16), keys, ((1,), (1,)))
-        scores = jnp.where(usable, scores, negative)
+        scores = dot((query * (mask * head_size ** (-0.5))).astype(bf16), keys, ((1,), (1,)))
+        scores = scores + bias
         maximum = jnp.max(scores, axis=-1, keepdims=True)
         exponent = jnp.exp(scores - maximum)
         summed = jnp.sum(exponent, axis=-1, keepdims=True)
-        weights = (exponent * (1.0 / summed)).astype(bf16)
-        result = dot(weights, values, ((1,), (0,))) * mask
-        out_ref[...] = (out_ref[...].astype(f32) + result).astype(bf16)
-        return carry
-
-    lax.fori_loop(0, width // head_size, one_head, 0)
+        attended = dot(exponent.astype(bf16), values, ((1,), (0,)))
+        result = result + attended * (mask * (1.0 / summed))
+    out_ref[...] = result.astype(bf16)
 
 
 def backward_kernel(live_ref, query_ref, grad_ref, *rest, head_size, blocks):
@@ -177,20 +180,21 @@
     )(live, query, *sources, *sources)
 
 
-def attend_back(live, query, grads, own, others, head_size, interpret=False):
-    rows, local = query.shape
+def attend_back(live, query, grads, own, others, head_size, first, count, interpret=False):
+    rows, full = query.shape
     width = 2 * head_size
-    pairs = local // width
+    local = count * width
+    pairs = full // width
     sources = [own] + list(others)
     blocks = len(sources)
     stacked = pl.BlockSpec((2, rows, width), lambda p: (0, 0, p))
     return pl.pallas_call(
         lambda *refs: backward_kernel(*refs, head_size=head_size, blocks=blocks),
-        grid=(pairs,),
+        grid=(count,),
         in_specs=[pl.BlockSpec(memory_space=pltpu.SMEM)]
-        + [column_block(rows, width, 0)] * 2
-        + [column_block(rows, width, 0)] * blocks
-        + [column_block(rows, width, pairs)] * blocks,
+        + [column_block(rows, width, first)] * 2
+        + [column_block(rows, width, first)] * blocks
+        + [column_block(rows, width, pairs + first)] * blocks,
         out_specs=[column_block(rows, width, 0)] + [stacked] * blocks,
         out_shape=[
             jax.ShapeDtypeStruct((rows, local), bf16),
@@ -203,7 +207,6 @@
             transcendentals=rows * rows * blocks * local // head_size,
         ),
         compiler_params=pltpu.CompilerParams(vmem_limit_bytes=56 * 1024 * 1024),
-        name="attend_back",
         interpret=interpret,
     )(live, query, grads, *sources, *sources)
 
@@ -314,19 +317,32 @@
     dhidden = dot(dmlp_low, down_back, ((1,), (0,))) * derivative
     grad_up_bias = jnp.sum(dhidden, axis=0)
     dhidden_low = dhidden.astype(bf16)
+
+    def reduce_shards(matrix):
+        return lax.psum_scatter(matrix, "fsdp", scatter_dimension=0, tiled=True)
+
+    up_part = dot(low_two, dhidden_low, ((0,), (0,))).astype(bf16)
+    up_shard = reduce_shards(up_part)
     dnorm_part = dot(dhidden_low, up_full, ((1,), (1,))).astype(bf16)
     dnorm_other = swap_pair(dnorm_part, "tp")
-    up_part = dot(low_two, dhidden_low, ((0,), (0,))).astype(bf16)
-    down_grad_part = dot(dmlp_low, activated, ((0,), (0,))).astype(bf16)
+    part = inner // groups
+    if groups == 2:
+        sent_units = lax.dynamic_slice_in_dim(activated, (1 - place) * part, part, 1)
+        kept_units = lax.dynamic_slice_in_dim(activated, place * part, part, 1)
+        down_sent = dot(dmlp_low, sent_units, ((0,), (0,))).astype(bf16)
+        down_got = swap_pair(down_sent, "ctx")
+        down_kept = dot(dmlp_low, kept_units, ((0,), (0,))).astype(bf16)
+        down_half = (down_kept.astype(f32) + down_got.astype(f32)).astype(bf16)
+    else:
+        down_half = lax.psum_scatter(
+            dot(dmlp_low, activated, ((0,), (0,))).astype(bf16),
+            "ctx",
+            scatter_dimension=1,
+            tiled=True,
+        )
     down_part = dot(activated, down_back, ((1,), (1,))).astype(bf16)
-    dnorm_other = after(dnorm_other, up_part, down_grad_part, down_part)
     dnorm_two = pair_sum(dnorm_part, dnorm_other, "tp")
     mlp_other = swap_pair(down_part, "tp")
-
-    def reduce_shards(matrix):
-        return lax.psum_scatter(matrix, "fsdp", scatter_dimension=0, tiled=True)
-
-    down_shard = reduce_shards(down_grad_part)
 
     grad_gain_two = jnp.sum(dnorm_two * unit_two, axis=0)
     grad_shift_two = jnp.sum(dnorm_two, axis=0)
@@ -337,17 +353,34 @@
     dproj_low = dproj.astype(bf16)
     dmixed = dot(dproj_low, proj_back, ((1,), (0,))).astype(bf16)
     proj_grad_part = dot(dproj_low, mixed, ((0,), (0,))).astype(bf16)
-    up_shard = reduce_shards(jnp.concatenate([up_part, proj_grad_part], axis=1))
-
-    query_grad, own_grad, *sent = attend_back(live, queries, dmixed, own, others, head_size)
-    mlp_other = after(mlp_other, query_grad)
+    down_shard = rows_major(
+        reduce_shards(rows_major(jnp.concatenate([down_half, proj_grad_part], axis=1)))
+    )
+
+    pairs = width // (2 * head_size)
+    cuts = [0, pairs // 2, pairs] if pairs > 1 else [0, pairs]
+    query_parts, own_parts = [], []
+    for first, last in zip(cuts[:-1], cuts[1:]):
+        query_piece, own_grad, *sent = attend_back(
+            live, queries, dmixed, own, others, head_size, first, last - first
+        )
+        query_parts.append(query_piece)
+        returned = [
+            ring_shift(item, "ctx", -(step + 1)) for step, item in enumerate(sent)
+        ]
+        own_parts.append((own_grad, returned))
+    mlp_other = after(mlp_other, query_parts[-1])
     mlp_out = pair_sum(down_part, mlp_other, "tp") + bias_down
     output = (resid + scale_two * mlp_out).astype(bf16).reshape(images, slots, features)
     grad_scale_two = jnp.sum(upstream * mlp_out, axis=0)
-    for step, item in enumerate(sent):
-        own_grad = own_grad + ring_shift(item, "ctx", -(step + 1)).astype(f32)
-    own_low = own_grad.astype(bf16)
-    dqkv = jnp.concatenate([query_grad, own_low[0], own_low[1]], axis=1)
+    totals = []
+    for own_grad, returned in own_parts:
+        for item in returned:
+            own_grad = own_grad + item.astype(f32)
+        totals.append(own_grad.astype(bf16))
+    key_low = [item[0] for item in totals]
+    value_low = [item[1] for item in totals]
+    dqkv = jnp.concatenate(query_parts + key_low + value_low, axis=1)
     dnorm_local = dot(dqkv, qkv_matrix, ((1,), (1,)))
     grad_gain_one = jnp.sum(dnorm_local * unit_one, axis=0)
     grad_shift_one = jnp.sum(dnorm_local, axis=0)
@@ -356,15 +389,23 @@
     dnorm_one = pair_sum(dnorm_low, dnorm_other, "tp")
     qkv_part = dot(low_one, dqkv, ((0,), (0,))).astype(bf16)
     qkv_shard = reduce_shards(qkv_part)
+    up_other = swap_pair(up_shard, "ctx")
+    grad_up = pair_sum(up_shard, up_other, "ctx")
     down_other = swap_pair(down_shard, "ctx")
-    up_other = swap_pair(up_shard, "ctx")
-    grad_down = pair_sum(down_shard, down_other, "ctx").T
-    up_sum = pair_sum(up_shard, up_other, "ctx")
-    grad_up = up_sum[:, :inner]
-    grad_proj = up_sum[:, inner:].T
-    grad_qkv = exchange_sum(after(qkv_shard, up_sum, grad_down), "ctx")
-    grad_qkv_bias = jnp.stack(
-        [jnp.sum(query_grad.astype(f32), axis=0), jnp.sum(own_low[1].astype(f32), axis=0)]
+    grad_proj = pair_sum(
+        down_shard[:, part:], None if down_other is None else down_other[:, part:], "ctx"
+    ).T
+    if groups == 2:
+        mine, yours = down_shard[:, :part], down_other[:, :part]
+        grad_down = jnp.concatenate(
+            [jnp.where(place == 0, mine, yours), jnp.where(place == 0, yours, mine)], axis=1
+        )
+    else:
+        grad_down = lax.all_gather(down_shard[:, :part], "ctx", axis=1, tiled=True)
+    grad_down = grad_down.astype(f32).T
+    grad_qkv = exchange_sum(after(qkv_shard, grad_up, grad_down), "ctx")
+    grad_qkv_bias = jnp.concatenate(
+        [jnp.sum(item.astype(f32), axis=0) for item in query_parts + value_low]
     )
     dinput = (
         (dresid + normalize_back(dnorm_one, unit_one, inverse_one, gain_one))

time: 352 us -> 367 us (1.043)
  waiting for transfers between devices: 141 us -> 156 us
    ppermute x9 -> x10, waiting for transfers between devices: 63.8 us -> 80 us  [swap_pair(): return lax.ppermute(part, axis, [(0, 1), (1, 0)])]
    ppermute x2 -> x3, waiting for transfers between devices: 47 us -> 35.5 us  [ring_shift(): lax.ppermute(value, axis, [(i, (i + step) % size) for i in range(size)])]
    reduce_scatter x3, waiting for transfers between devices: 0.04 us -> 11.4 us  [reduce_shards(): return lax.psum_scatter(matrix, 'fsdp', scatter_dimension=0, tiled=True)]
    pallas_call x1, Pallas kernels: 18.4 us -> 12.6 us  [attend(): pl.pallas_call(lambda *refs: forward_kernel(*refs, head_size=head_size, b...]
    pallas_call x1 -> x2, Pallas kernels: 27.4 us -> 29.8 us  [attend_back(): pl.pallas_call(lambda *refs: backward_kernel(*refs, head_size=head_size,...]
    unnamed x87 -> x112, local copies, waits for them, and re-layouts: 11.5 us -> 12.5 us
    dot_general x13 -> x14, matrix products: 57.1 us -> 57.3 us  [dot(): lax.dot_general(left, right, (dims, ((), ())), preferred_element_type=f32)]
    ppermute x9 -> x10, starting transfers between devices: 11.9 us -> 12 us  [swap_pair(): return lax.ppermute(part, axis, [(0, 1), (1, 0)])]
  transfers between devices with their start and end apart: 16 -> 18, of which waited for: 9 -> 11; matrix products, arithmetic and copies ran while one was open for 25% -> 21% of each run, Pallas kernels for 13% -> 12%
where the time goes in v5:
time: 367 us; the launch traced here: 363 us
  waiting for transfers between devices  156 us (43%)
  matrix products  57.3 us (16%)
  Pallas kernels  42.4 us (12%)
  other arithmetic  31.9 us (9%)
  blocking collectives  26.7 us (7%)
  local copies, waits for them, and re-layouts  17.5 us (5%)
  starting transfers between devices  15.9 us (4%)
  between operations  14.8 us (4%)
    ppermute x10, waiting for transfers between devices, swap_pair(): return lax.ppermute(part, axis, [(0, 1), (1, 0)])  80 us
    dot_general x14, matrix products, dot(): lax.dot_general(left, right, (dims, ((), ())), preferred_element_type=f32)  57.3 us
    ppermute x3, waiting for transfers between devices, ring_shift(): lax.ppermute(value, axis, [(i, (i + step) % size) for i in range(size)])  35.5 us
    pallas_call x2, Pallas kernels, attend_back(): pl.pallas_call(lambda *refs: backward_kernel(*refs, head_size=head_size,...  29.8 us
    all_gather x1, waiting for transfers between devices, body(): attn_full = lax.all_gather(attn_part, 'fsdp', axis=0, tiled=True)  29.4 us
    all_gather x1, blocking collectives, body(): gathered = lax.all_gather(packed, 'fsdp', axis=0)  16.6 us
    pallas_call x1, Pallas kernels, attend(): pl.pallas_call(lambda *refs: forward_kernel(*refs, head_size=head_size, b...  12.6 us
    unnamed x112, local copies, waits for them, and re-layouts  12.5 us
  transfers between devices with their start and end apart: 18, of which 11 were waited for; matrix products, arithmetic and copies ran while one was open for 21% of the time, Pallas kernels for 12%

profile of v5, /device:TPU:0, one launch (start us, length us, event | category | flops | bytes accessed | tf_op | source)
XLA Modules:
  0.0 362.9 jit_solution(18115806235269279273)
XLA Ops:
  7.3 1.3 copy.68
  8.6 1.7 pad_maximum_fusion.1
  14.3 16.6 %all-gather.1 = bf16[8,1,1408]{2,1,0:T(2,128)(2,1)S(1)} all-gather(bf16[1,1,1408]{2,1,0:T(2,128)(2,1)S(1)} %reshape.410), channel_id=2, replica_groups=mesh['fsdp'=8,'ctx'=2,'tp'=2] {'fsdp'}, dimensions={0}, use_global_device_ids=true | all-gather | bytes 25344 | tf_op jit(solution)/shard_map/all_gather | solution.py:257
  31.9 29.4 %all-gather.5.cloned.1.call-done = bf16[1024,2048]{0,1:T(8,128)(2,1)} async-done(((bf16[128,2048]{0,1:T(8,128)(2,1)}), bf16[1024,2048]{0,1:T(8,128)(2,1)}) %all-gather.5.cloned.1.call-update) | async-done | bytes 4194320 | tf_op jit(solution)/shard_map/all_gather | solution.py:279
  61.3 2.9 add_convert_fusion.3.refs_2_.refs_4_.refs_3_.refs_5_
  64.3 1.5 collective-permute-start
  67.1 2.8 fusion.48.refs_1_
  69.9 26.2 %collective-permute-done.refs_3_.refs_5_.refs_4_.refs_6_ = bf16[528,1024]{1,0:T(8,128)(2,1)} collective-permute-done((bf16[528,1024]{1,0:T(8,128)(2,1)S(1)}, bf16[528,1024]{1,0:T(8,128)(2,1)}, u32[]{:S(2)}, u32[]{:S(2)}) %collective-permute-start) | collective-permute-done | bytes 1081376 | tf_op jit(solution)/shard_map/ppermute | solution.py:72
  96.1 12.6 %attend.1 = bf16[528,512]{1,0:T(8,128)(2,1)} custom-call(s32[2]{0:T(128)} %and_select_fusion.1.refs_0_, bf16[528,512]{1,0:T(8,128)(2,1)} %fusion.48.refs_1_, bf16[528,1024]{1,0:T(8,128)(2,1)} %copy-done.9, bf16[528,1024]{1,0:T(8,128)(2,1)} %collective-permute-done.refs_3_.refs_5_.refs_4_.refs_6_, bf16[528,1024]{1,0:T(8,128)(2,1)} %copy-done.9, ...), custom_call_target="tpu_custom_call" | custom-call | flops 1141899264 | bytes 3244032 | tf_op jit(solution)/shard_map/attend/pallas_call | solution.py:164
  108.7 3.3 convolution_convert_fusion.3
  112.0 1.5 collective-permute-start.1
  115.1 22.4 %collective-permute-done.1 = bf16[528,1024]{1,0:T(8,128)(2,1)} collective-permute-done((bf16[528,1024]{1,0:T(8,128)(2,1)}, bf16[528,1024]{1,0:T(8,128)(2,1)}, u32[]{:S(2)}, u32[]{:S(2)}) %collective-permute-start.1) | collective-permute-done | bytes 1081376 | tf_op jit(solution)/shard_map/ppermute | solution.py:46
  137.4 2.3 fusion.78
  140.2 6.6 %multiply_convert_fusion = (bf16[528,2048]{1,0:T(8,128)(2,1)}, f32[528,2048]{1,0:T(8,128)S(1)}) fusion(f32[2048]{0:T(1024)S(1)} %reshape.397, bf16[1024,4096]{1,0:T(8,128)(2,1)} %all-gather.7.cloned.1.call-done, f32[528,1024]{1,0:T(8,128)S(1)} %get-tuple-element.110, f32[1024]{0:T(1024)S(1)} %get-tuple-element.122, f32[1024]{0:T(1024)S(1)} %get-tuple-element.123, ...), kind=kOutput, calls=%fused_computation.7 | convolution fusion | flops 2223783936 | bytes 12865664 | tf_op jit(solution)/shard_map/dot_general | solution.py:41
  146.8 4.4 %fusion.85 = (bf16[2048]{0:T(1024)(128)(2,1)S(1)}, bf16[528,2048]{1,0:T(8,128)(2,1)S(1)}) fusion(f32[528,2048]{1,0:T(8,128)S(1)} %get-tuple-element.143, f32[2048]{0:T(1024)S(1)} %reshape.397, bf16[528,1024]{1,0:T(8,128)(2,1)S(1)} %copy-done.16, bf16[1024,4096]{1,0:T(8,128)(2,1)S(1)} %copy-done.36), kind=kOutput, calls=%fused_computation.172 | convolution fusion | flops 2227566592 | bytes 11776000 | tf_op jit(solution)/shard_map/dot_general | solution.py:41
  151.2 3.4 fusion.40
  154.6 1.5 collective-permute-start.3
  156.1 4.7 %convolution_convert_fusion.2 = bf16[1024,1024]{1,0:T(8,128)(2,1)} fusion(bf16[528,1024]{1,0:T(8,128)(2,1)} %multiply_convert_fusion.2, bf16[528,2048]{1,0:T(8,128)(2,1)} %get-tuple-element.142, s32[]{:T(128)S(6)} %select_n.68), kind=kOutput, calls=%fused_computation.65 | convolution fusion | flops 1108344832 | bytes 4259844 | tf_op jit(solution)/shard_map/dot_general | solution.py:41
  160.8 1.4 collective-permute-start.10
  162.2 18.1 %collective-permute-done.3 = bf16[528,1024]{1,0:T(8,128)(2,1)} collective-permute-done((bf16[528,1024]{1,0:T(8,128)(2,1)}, bf16[528,1024]{1,0:T(8,128)(2,1)}, u32[]{:S(2)}, u32[]{:S(2)}) %collective-permute-start.3) | collective-permute-done | bytes 1081376 | tf_op jit(solution)/shard_map/ppermute | solution.py:46
  180.3 2.7 multiply_reduce_fusion.1
  183.0 3.3 multiply_reduce_fusion.2
  186.4 1.4 copy-done.6
  188.8 19.2 %collective-permute-done.10 = bf16[1024,1024]{1,0:T(8,128)(2,1)} collective-permute-done((bf16[1024,1024]{1,0:T(8,128)(2,1)}, bf16[1024,1024]{1,0:T(8,128)(2,1)}, u32[]{:S(2)}, u32[]{:S(2)}) %collective-permute-start.10) | collective-permute-done | bytes 2097184 | tf_op jit(solution)/shard_map/ppermute | solution.py:46
  208.0 3.4 add_convert_fusion
  211.4 1.9 pad_maximum_fusion
  213.4 6.9 %convolution_convert_fusion = bf16[1024,2048]{1,0:T(8,128)(2,1)} fusion(bf16[528,2048]{1,0:T(8,128)(2,1)} %copy-done.39, f32[528,1024]{1,0:T(8,128)S(1)} %get-tuple-element.110, f32[1024]{0:T(1024)S(1)} %get-tuple-element.122, f32[1024]{0:T(1024)S(1)} %get-tuple-element.123, f32[528]{0:T(1024)S(1)} %add_rsqrt_fusion, f32[528]{0:T(1024)S(1)} %broadcast_multiply_fusion.4), kind=kOutput, calls=%fused_computation.10 | convolution fusion | flops 2219393024 | bytes 8532096 | tf_op jit(solution)/shard_map/dot_general | solution.py:41
  220.3 6.4 %fusion.43 = bf16[528,1024]{1,0:T(8,128)(2,1)} fusion(bf16[528,2048]{1,0:T(8,128)(2,1)} %get-tuple-element.142, bf16[1024,4096]{1,0:T(8,128)(2,1)} %all-gather.7.cloned.1.call-done), kind=kOutput, calls=%fused_computation.70 | convolution fusion | flops 2215133184 | bytes 7438336 | tf_op jit(solution)/shard_map/dot_general | solution.py:41
  227.3 2.8 convolution_convert_fusion.5.refs_2_
  230.1 15.0 %shard_map.289 = (bf16[528,256]{1,0:T(8,128)(2,1)}, f32[2,528,256]{2,1,0:T(8,128)}, bf16[2,528,256]{2,1,0:T(8,128)(2,1)}) custom-call(s32[2]{0:T(128)} %and_select_fusion.1.refs_0_, bf16[528,512]{1,0:T(8,128)(2,1)} %fusion.48.refs_1_, bf16[528,512]{1,0:T(8,128)(2,1)} %convolution_convert_fusion.5.refs_2_, bf16[528,1024]{1,0:T(8,128)(2,1)} %copy-done.9, ...), custom_call_target="tpu_custom_call" | custom-call | flops 1427374080 | bytes 4055040 | tf_op jit(solution)/shard_map/pallas_call | solution.py:191
  245.7 14.8 %shard_map.288 = (bf16[528,256]{1,0:T(8,128)(2,1)}, f32[2,528,256]{2,1,0:T(8,128)}, bf16[2,528,256]{2,1,0:T(8,128)(2,1)}) custom-call(s32[2]{0:T(128)} %and_select_fusion.1.refs_0_, bf16[528,512]{1,0:T(8,128)(2,1)} %fusion.48.refs_1_, bf16[528,512]{1,0:T(8,128)(2,1)} %convolution_convert_fusion.5.refs_2_, bf16[528,1024]{1,0:T(8,128)(2,1)} %copy-done.9, ...), custom_call_target="tpu_custom_call" | custom-call | flops 1427374080 | bytes 4055040 | tf_op jit(solution)/shard_map/pallas_call | solution.py:191
  260.5 1.5 collective-permute-start.5
  263.4 9.4 %collective-permute-done.5 = bf16[2,528,256]{2,1,0:T(8,128)(2,1)S(1)} collective-permute-done((bf16[2,528,256]{2,1,0:T(8,128)(2,1)}, bf16[2,528,256]{2,1,0:T(8,128)(2,1)S(1)}, u32[]{:S(2)}, u32[]{:S(2)}) %collective-permute-start.5) | collective-permute-done | bytes 540704 | tf_op jit(solution)/shard_map/ppermute | solution.py:72
  274.9 4.3 %convolution_convert_fusion.1 = bf16[1024,1536]{1,0:T(8,128)(2,1)} fusion(bf16[528,1536]{1,0:T(8,128)(2,1)S(1)} %bitcast_dynamic-update-slice_fusion, bf16[1,528,1024]{2,1,0:T(8,128)(2,1)S(1)} %copy-done.3, f32[1024]{0:T(1024)S(1)} %get-tuple-element.127, f32[1024]{0:T(1024)S(1)} %get-tuple-element.128, f32[528]{0:T(1024)S(1)} %add_rsqrt_fusion.1, ...), kind=kOutput, calls=%fused_computation.11 | convolution fusion | flops 1665761280 | bytes 5861504 | tf_op jit(solution)/shard_map/dot_general | solution.py:41
  279.4 4.3 %multiply_reduce_fusion = (bf16[1024]{0:T(1024)(128)(2,1)S(1)}, bf16[1024]{0:T(1024)(128)(2,1)S(1)}, bf16[1,528,1024]{2,1,0:T(8,128)(2,1)}) fusion(bf16[528,1024]{1,0:T(8,128)(2,1)} %collective-permute-done.2, bf16[528,1024]{1,0:T(8,128)(2,1)} %fusion.43, f32[1,528,1024]{2,1,0:T(8,128)} %param.33, f32[1024]{0:T(1024)S(1)} %get-tuple-element.121, ...), kind=kLoop, calls=%fused_computation.43 | loop fusion | flops 6486016 | bytes 7583808 | tf_op jit(solution)/shard_map/reduce_sum | solution.py:375
  284.1 4.4 %fusion.77 = (bf16[1024]{0:T(1024)(128)(2,1)S(1)}, bf16[1024]{0:T(1024)(128)(2,1)S(1)}, bf16[528,1024]{1,0:T(8,128)(2,1)S(1)}) fusion(f32[528]{0:T(1024)S(1)} %add_rsqrt_fusion.1, f32[528]{0:T(1024)S(1)} %broadcast_multiply_fusion.5, bf16[1,528,1024]{2,1,0:T(8,128)(2,1)S(1)} %copy-done.3, bf16[528,1536]{1,0:T(8,128)(2,1)} %copy-done.24, ...), kind=kOutput, calls=%fused_computation.165 | convolution fusion | flops 1664727040 | bytes 6938752 | tf_op jit(solution)/shard_map/dot_general | solution.py:41
  288.5 1.6 collective-permute-start.6
  291.5 10.1 %all_to_all.6 = bf16[8,2,704]{2,1,0:T(2,128)(2,1)S(1)} all-to-all(bf16[8,2,704]{2,1,0:T(2,128)(2,1)S(1)} %reshape.413), channel_id=1, replica_groups=mesh['fsdp'=8,'ctx'=2,'tp'=2] {'fsdp'}, dimensions={0} | all-to-all | bytes 45056 | tf_op jit(solution)/shard_map/all_to_all | solution.py:429
  301.7 1.5 collective-permute-start.7
  303.2 2.2 collective-permute-done.7
  308.0 3.5 collective-permute-done.8
  312.9 1.9 collective-permute-start.11
  315.0 10.3 %collective-permute-done.11 = bf16[128,1536]{1,0:T(8,128)(2,1)} collective-permute-done((bf16[128,1536]{1,0:T(8,128)(2,1)}, bf16[128,1536]{1,0:T(8,128)(2,1)}, u32[]{:S(2)}, u32[]{:S(2)}) %collective-permute-start.11) | collective-permute-done | bytes 393248 | tf_op jit(solution)/shard_map/ppermute | solution.py:46
  327.4 4.3 %collective-permute-done.9 = bf16[128,2048]{1,0:T(8,128)(2,1)S(1)} collective-permute-done((bf16[128,2048]{1,0:T(8,128)(2,1)}, bf16[128,2048]{1,0:T(8,128)(2,1)S(1)}, u32[]{:S(2)}, u32[]{:S(2)}) %collective-permute-start.9) | collective-permute-done | bytes 524320 | tf_op jit(solution)/shard_map/ppermute | solution.py:46
  332.8 11.4 %reduce-scatter.4.cloned.1.call-done = bf16[128,1536]{1,0:T(8,128)(2,1)} async-done(((bf16[1024,1536]{1,0:T(8,128)(2,1)}), bf16[128,1536]{1,0:T(8,128)(2,1)}) %reduce-scatter.4.cloned.1.call-update) | async-done | bytes 393232 | tf_op jit(solution)/shard_map/reduce_scatter | solution.py:322
  344.2 1.5 collective-permute-start.12
  345.6 3.5 fusion.54
  349.1 2.6 copy.81
  (198 shorter events, 27.7 us)
Async XLA Ops:
  7.2 3.3 copy-start
  7.2 3.7 %copy-start.23 = (bf16[128,2048]{1,0:T(8,128)(2,1)S(1)}, bf16[128,2048]{1,0:T(8,128)(2,1)}, u32[]{:S(2)}) copy-start(bf16[128,2048]{1,0:T(8,128)(2,1)} %param.28) | copy-start | bytes 1572868
  7.2 54.1 %all-gather.5.cloned.1.call-start = ((), (), s32[]{:S(2)}) async-start(), calls=%async_computation.4 | async-start | bytes 4718592 | tf_op jit(solution)/shard_map/all_gather | solution.py:279
  10.3 3.2 copy-start.33
  10.3 3.6 copy-start.34
  10.4 3.8 %copy-start.35 = (bf16[128]{0:T(256)(128)(2,1)S(1)}, bf16[128]{0:T(256)(128)(2,1)}, u32[]{:S(2)}) copy-start(bf16[128]{0:T(256)(128)(2,1)} %param.32) | copy-start | bytes 772
  10.4 129.7 %all-gather.7.cloned.1.call-start = ((), (), s32[]{:S(2)}) async-start(), calls=%async_computation.5 | async-start | bytes 8912896 | tf_op jit(solution)/shard_map/all_gather | solution.py:285
  10.5 20.7 %copy-start.3 = (bf16[1,528,1024]{2,1,0:T(8,128)(2,1)S(1)}, bf16[1,528,1024]{2,1,0:T(8,128)(2,1)}, u32[]{:S(2)}) copy-start(bf16[1,528,1024]{2,1,0:T(8,128)(2,1)} %param.17) | copy-start | bytes 3244036
  11.8 301.1 %reduce-scatter.8.cloned.1.call-start = ((), (), s32[]{:S(2)}) async-start(), calls=%async_computation.8 | async-start | bytes 3538944 | tf_op jit(solution)/shard_map/reduce_scatter | solution.py:322
  61.3 4.6 %copy-start.2 = (s32[1,2]{1,0:T(1,128)S(1)}, s32[1,2]{1,0:T(1,128)}, u32[]{:S(2)}) copy-start(s32[1,2]{1,0:T(1,128)} %param.18) | copy-start | bytes 28
  64.3 5.7 %copy-start.9 = (bf16[528,1024]{1,0:T(8,128)(2,1)}, bf16[528,1024]{1,0:T(8,128)(2,1)S(1)}, u32[]{:S(2)}) copy-start(bf16[528,1024]{1,0:T(8,128)(2,1)S(1)} %add_convert_fusion.3.refs_2_.refs_4_.refs_3_.refs_5_) | copy-start | bytes 3244036
  64.3 31.8 %collective-permute-start = (bf16[528,1024]{1,0:T(8,128)(2,1)S(1)}, bf16[528,1024]{1,0:T(8,128)(2,1)}, u32[]{:S(2)}, u32[]{:S(2)}) collective-permute-start(bf16[528,1024]{1,0:T(8,128)(2,1)S(1)} %add_convert_fusion.3.refs_2_.refs_4_.refs_3_.refs_5_), channel_id=1, source_target_pairs={{0,2},{2,0},{1,3},{3,1},{4,6},{6,4},{5,7},{7,5},{8,10},{10,8},{9,1... | collective-permute-start | bytes 3244040 | tf_op jit(solution)/shard_map/ppermute | solution.py:72
  108.7 5.0 %copy-start.25 = (s32[2]{0:T(128)S(1)}, s32[2]{0:T(128)}, u32[]{:S(2)}) copy-start(s32[2]{0:T(128)} %and_select_fusion.1.refs_0_) | copy-start | bytes 28
  108.7 5.1 %copy-start.4 = (f32[1,528,1024]{2,1,0:T(8,128)S(1)}, f32[1,528,1024]{2,1,0:T(8,128)}, u32[]{:S(2)}) copy-start(f32[1,528,1024]{2,1,0:T(8,128)} %param.33) | copy-start | bytes 6488068
  112.0 25.5 %collective-permute-start.1 = (bf16[528,1024]{1,0:T(8,128)(2,1)}, bf16[528,1024]{1,0:T(8,128)(2,1)}, u32[]{:S(2)}, u32[]{:S(2)}) collective-permute-start(bf16[528,1024]{1,0:T(8,128)(2,1)} %convolution_convert_fusion.3), channel_id=1, source_target_pairs={{0,1},{1,0},{2,3},{3,2},{4,5},{5,4},{6,7},{7,6},{8,9},{9,8},{10,11... | collective-permute-start | bytes 3244040 | tf_op jit(solution)/shard_map/ppermute | solution.py:46
  140.1 6.6 %copy-start.16 = (bf16[528,1024]{1,0:T(8,128)(2,1)S(1)}, bf16[528,1024]{1,0:T(8,128)(2,1)}, u32[]{:S(2)}) copy-start(bf16[528,1024]{1,0:T(8,128)(2,1)} %multiply_convert_fusion.2) | copy-start | bytes 3244036
  140.1 6.6 %copy-start.36 = (bf16[1024,4096]{1,0:T(8,128)(2,1)S(1)}, bf16[1024,4096]{1,0:T(8,128)(2,1)}, u32[]{:S(2)}) copy-start(bf16[1024,4096]{1,0:T(8,128)(2,1)} %all-gather.7.cloned.1.call-done) | copy-start | bytes 25165828
  151.2 3.4 copy-start.39
  154.6 25.7 %collective-permute-start.3 = (bf16[528,1024]{1,0:T(8,128)(2,1)}, bf16[528,1024]{1,0:T(8,128)(2,1)}, u32[]{:S(2)}, u32[]{:S(2)}) collective-permute-start(bf16[528,1024]{1,0:T(8,128)(2,1)} %fusion.40), channel_id=1, source_target_pairs={{0,1},{1,0},{2,3},{3,2},{4,5},{5,4},{6,7},{7,6},{8,9},{9,8},{10,11... | collective-permute-start | bytes 3244040 | tf_op jit(solution)/shard_map/ppermute | solution.py:46
  160.8 47.2 %collective-permute-start.10 = (bf16[1024,1024]{1,0:T(8,128)(2,1)}, bf16[1024,1024]{1,0:T(8,128)(2,1)}, u32[]{:S(2)}, u32[]{:S(2)}) collective-permute-start(bf16[1024,1024]{1,0:T(8,128)(2,1)} %convolution_convert_fusion.2), channel_id=1, source_target_pairs={{0,2},{2,0},{1,3},{3,1},{4,6},{6,4},{5,7},{7,5},{8,10},{10,8},{9,1... | collective-permute-start | bytes 6291464 | tf_op jit(solution)/shard_map/ppermute | solution.py:46
  162.2 20.8 %copy-start.5 = (f32[1,528,1024]{2,1,0:T(8,128)S(1)}, f32[1,528,1024]{2,1,0:T(8,128)}, u32[]{:S(2)}) copy-start(f32[1,528,1024]{2,1,0:T(8,128)} %param.33) | copy-start | bytes 6488068
  183.0 4.7 %copy-start.37 = (bf16[528,512]{1,0:T(8,128)(2,1)S(1)}, bf16[528,512]{1,0:T(8,128)(2,1)}, u32[]{:S(2)}) copy-start(bf16[528,512]{1,0:T(8,128)(2,1)} %attend.1) | copy-start | bytes 1622020
  186.4 21.6 %copy-start.17 = (bf16[528,1024]{1,0:T(8,128)(2,1)S(1)}, bf16[528,1024]{1,0:T(8,128)(2,1)}, u32[]{:S(2)}) copy-start(bf16[528,1024]{1,0:T(8,128)(2,1)} %multiply_convert_fusion.2) | copy-start | bytes 3244036
  186.4 21.6 %copy-start.38 = (bf16[528,2048]{1,0:T(8,128)(2,1)S(1)}, bf16[528,2048]{1,0:T(8,128)(2,1)}, u32[]{:S(2)}) copy-start(bf16[528,2048]{1,0:T(8,128)(2,1)} %get-tuple-element.142) | copy-start | bytes 6488068
  213.3 101.4 %reduce-scatter.6.cloned.1.call-start = ((), (), s32[]{:S(2)}) async-start(), calls=%async_computation.7 | async-start | bytes 4718592 | tf_op jit(solution)/shard_map/reduce_scatter | solution.py:322
  220.3 123.9 %reduce-scatter.4.cloned.1.call-start = ((), (), s32[]{:S(2)}) async-start(), calls=%async_computation.6 | async-start | bytes 3538944 | tf_op jit(solution)/shard_map/reduce_scatter | solution.py:322
  220.3 7.0 %copy-start.7 = (f32[528,1024]{1,0:T(8,128)S(1)}, f32[528,1024]{1,0:T(8,128)}, u32[]{:S(2)}) copy-start(f32[528,1024]{1,0:T(8,128)} %copy-done.6) | copy-start | bytes 6488068
  226.7 52.7 %collective-permute-start.2 = (bf16[528,1024]{1,0:T(8,128)(2,1)}, bf16[528,1024]{1,0:T(8,128)(2,1)}, u32[]{:S(2)}, u32[]{:S(2)}) collective-permute-start(bf16[528,1024]{1,0:T(8,128)(2,1)} %fusion.43), channel_id=1, source_target_pairs={{0,1},{1,0},{2,3},{3,2},{4,5},{5,4},{6,7},{7,6},{8,9},{9,8},{10,11... | collective-permute-start | bytes 3244040 | tf_op jit(solution)/shard_map/ppermute | solution.py:46
  245.1 17.0 %copy-start.22 = (bf16[528,256]{1,0:T(8,128)(2,1)S(1)}, bf16[528,256]{1,0:T(8,128)(2,1)}, u32[]{:S(2)}) copy-start(bf16[528,256]{1,0:T(8,128)(2,1)} %get-tuple-element.26) | copy-start | bytes 811012
  245.1 18.1 %copy-start.19 = (f32[2,528,256]{2,1,0:T(8,128)S(1)}, f32[2,528,256]{2,1,0:T(8,128)}, u32[]{:S(2)}) copy-start(f32[2,528,256]{2,1,0:T(8,128)} %get-tuple-element.27) | copy-start | bytes 3244036
  245.1 18.1 %collective-permute-start.4 = (bf16[2,528,256]{2,1,0:T(8,128)(2,1)}, bf16[2,528,256]{2,1,0:T(8,128)(2,1)S(1)}, u32[]{:S(2)}, u32[]{:S(2)}) collective-permute-start(bf16[2,528,256]{2,1,0:T(8,128)(2,1)} %get-tuple-element.28), channel_id=1, source_target_pairs={{0,2},{2,0},{1,3},{3,1},{4,6},{6,4},{5,7},{7,5},{8,10},{10,8},{9,1... | collective-permute-start | bytes 1622024 | tf_op jit(solution)/shard_map/ppermute | solution.py:72
  260.5 12.2 %copy-start.18 = (f32[2,528,256]{2,1,0:T(8,128)S(1)}, f32[2,528,256]{2,1,0:T(8,128)}, u32[]{:S(2)}) copy-start(f32[2,528,256]{2,1,0:T(8,128)} %get-tuple-element.29) | copy-start | bytes 3244036
  260.5 12.2 %collective-permute-start.5 = (bf16[2,528,256]{2,1,0:T(8,128)(2,1)}, bf16[2,528,256]{2,1,0:T(8,128)(2,1)S(1)}, u32[]{:S(2)}, u32[]{:S(2)}) collective-permute-start(bf16[2,528,256]{2,1,0:T(8,128)(2,1)} %get-tuple-element.30), channel_id=1, source_target_pairs={{0,2},{2,0},{1,3},{3,1},{4,6},{6,4},{5,7},{7,5},{8,10},{10,8},{9,1... | collective-permute-start | bytes 1622024 | tf_op jit(solution)/shard_map/ppermute | solution.py:72
  263.4 9.6 %copy-start.12 = (bf16[2,528,256]{2,1,0:T(8,128)(2,1)}, bf16[2,528,256]{2,1,0:T(8,128)(2,1)S(1)}, u32[]{:S(2)}) copy-start(bf16[2,528,256]{2,1,0:T(8,128)(2,1)S(1)} %add_convert_fusion.5) | copy-start | bytes 1622020
  279.4 4.3 %copy-start.13 = (bf16[2,528,256]{2,1,0:T(8,128)(2,1)S(1)}, bf16[2,528,256]{2,1,0:T(8,128)(2,1)}, u32[]{:S(2)}) copy-start(bf16[2,528,256]{2,1,0:T(8,128)(2,1)} %copy-done.12) | copy-start | bytes 1622020
  279.4 4.4 %copy-start.15 = (bf16[2,528,256]{2,1,0:T(8,128)(2,1)S(1)}, bf16[2,528,256]{2,1,0:T(8,128)(2,1)}, u32[]{:S(2)}) copy-start(bf16[2,528,256]{2,1,0:T(8,128)(2,1)} %copy-done.14) | copy-start | bytes 1622020
  288.5 26.4 %copy-start.10 = (bf16[528,1024]{1,0:T(8,128)(2,1)}, bf16[528,1024]{1,0:T(8,128)(2,1)S(1)}, u32[]{:S(2)}) copy-start(bf16[528,1024]{1,0:T(8,128)(2,1)S(1)} %get-tuple-element.112) | copy-start | bytes 3244036
  288.5 23.5 %collective-permute-start.6 = (bf16[528,1024]{1,0:T(8,128)(2,1)S(1)}, bf16[528,1024]{1,0:T(8,128)(2,1)S(1)}, u32[]{:S(2)}, u32[]{:S(2)}) collective-permute-start(bf16[528,1024]{1,0:T(8,128)(2,1)S(1)} %get-tuple-element.112), channel_id=1, source_target_pairs={{0,1},{1,0},{2,3},{3,2},{4,5},{5,4},{6,7},{7,6},{8,9},{9,8},{10,11... | collective-permute-start | bytes 3244040 | tf_op jit(solution)/shard_map/ppermute | solution.py:46
  301.7 3.7 %collective-permute-start.7 = (bf16[1408]{0:T(1024)(128)(2,1)S(1)}, bf16[1408]{0:T(1024)(128)(2,1)S(1)}, u32[]{:S(2)}, u32[]{:S(2)}) collective-permute-start(bf16[1408]{0:T(1024)(128)(2,1)S(1)} %reduce_sum.222), channel_id=1, source_target_pairs={{0,2},{2,0},{1,3},{3,1},{4,6},{6,4},{5,7},{7,5},{8,10},{10,8},{9,1... | collective-permute-start | bytes 8456 | tf_op jit(solution)/shard_map/ppermute | solution.py:46
  305.4 6.1 %collective-permute-start.8 = (bf16[256]{0:T(256)(128)(2,1)S(1)}, bf16[256]{0:T(256)(128)(2,1)S(1)}, u32[]{:S(2)}, u32[]{:S(2)}) collective-permute-start(bf16[256]{0:T(256)(128)(2,1)S(1)} %slice.294), channel_id=1, source_target_pairs={{0,1},{1,0},{2,3},{3,2},{4,5},{5,4},{6,7},{7,6},{8,9},{9,8},{10,11... | collective-permute-start | bytes 1544 | tf_op jit(solution)/shard_map/ppermute | solution.py:46
  312.0 3.0 copy-start.11
  312.9 12.4 %collective-permute-start.11 = (bf16[128,1536]{1,0:T(8,128)(2,1)}, bf16[128,1536]{1,0:T(8,128)(2,1)}, u32[]{:S(2)}, u32[]{:S(2)}) collective-permute-start(bf16[128,1536]{1,0:T(8,128)(2,1)} %reduce-scatter.8.cloned.1.call-done), channel_id=1, source_target_pairs={{0,2},{2,0},{1,3},{3,1},{4,6},{6,4},{5,7},{7,5},{8,10},{10,8},{9,1... | collective-permute-start | bytes 1179656 | tf_op jit(solution)/shard_map/ppermute | solution.py:46
  314.7 17.0 %copy-start.20 = (bf16[128,2048]{1,0:T(8,128)(2,1)S(1)}, bf16[128,2048]{1,0:T(8,128)(2,1)}, u32[]{:S(2)}) copy-start(bf16[128,2048]{1,0:T(8,128)(2,1)} %reduce-scatter.6.cloned.1.call-done) | copy-start | bytes 1572868
  314.7 16.9 %collective-permute-start.9 = (bf16[128,2048]{1,0:T(8,128)(2,1)}, bf16[128,2048]{1,0:T(8,128)(2,1)S(1)}, u32[]{:S(2)}, u32[]{:S(2)}) collective-permute-start(bf16[128,2048]{1,0:T(8,128)(2,1)} %reduce-scatter.6.cloned.1.call-done), channel_id=1, source_target_pairs={{0,2},{2,0},{1,3},{3,1},{4,6},{6,4},{5,7},{7,5},{8,10},{10,8},{9,1... | collective-permute-start | bytes 1572872 | tf_op jit(solution)/shard_map/ppermute | solution.py:46
  315.0 30.7 %copy-start.8 = (f32[528,1024]{1,0:T(8,128)S(1)}, f32[528,1024]{1,0:T(8,128)}, u32[]{:S(2)}) copy-start(f32[528,1024]{1,0:T(8,128)} %copy-done.6) | copy-start | bytes 6488068
  344.2 9.4 %collective-permute-start.12 = (bf16[128,1536]{1,0:T(8,128)(2,1)}, bf16[128,1536]{1,0:T(8,128)(2,1)}, u32[]{:S(2)}, u32[]{:S(2)}) collective-permute-start(bf16[128,1536]{1,0:T(8,128)(2,1)} %reduce-scatter.4.cloned.1.call-done), channel_id=1, source_target_pairs={{0,2},{2,0},{1,3},{3,1},{4,6},{6,4},{5,7},{7,5},{8,10},{10,8},{9,1... | collective-permute-start | bytes 1179656 | tf_op jit(solution)/shard_map/ppermute | solution.py:46
  349.1 4.4 %copy-start.21 = (bf16[128,1536]{1,0:T(8,128)(2,1)S(1)}, bf16[128,1536]{1,0:T(8,128)(2,1)}, u32[]{:S(2)}) copy-start(bf16[128,1536]{1,0:T(8,128)(2,1)} %reduce-scatter.4.cloned.1.call-done) | copy-start | bytes 1179652
  352.7 3.4 copy-start.1
  (10 other events, 18.8 us)
Sparse Core Ops, SparseCore 0:
  10.5 50.7 all-gather.4
  64.1 75.3 all-gather.6
  213.4 38.0 reduce-scatter.7
  253.7 49.4 reduce-scatter.5
  305.3 38.8 reduce-scatter.3

commit v6 on v5

--- a/solution.py
+++ b/solution.py
@@ -55,6 +55,29 @@
 
 def exchange_sum(part, axis):
     return pair_sum(part, swap_pair(part, axis), axis)
+
+
+def gather_by_permutes(shard, axis):
+    size = lax.axis_size(axis)
+    index = lax.axis_index(axis)
+    steps = size // 2
+    rows, columns = shard.shape
+    pieces = [shard]
+    for k in range(1, steps):
+        pieces.append(
+            lax.ppermute(shard, axis, [(i, (i + 2 * k) % size) for i in range(size)])
+        )
+    backward = jnp.concatenate(pieces[::-1] * 2, axis=0)
+    start = (steps - 1 - index // 2) * rows
+    same = lax.dynamic_slice_in_dim(backward, start, steps * rows, 0)
+    other = lax.ppermute(same, axis, [(i, i ^ 1) for i in range(size)])
+    same = same.reshape(steps, 1, rows, columns)
+    other = other.reshape(steps, 1, rows, columns)
+    even = (index % 2 == 0) == (
+        lax.broadcasted_iota(jnp.int32, (1, 2, 1, 1), 1) == 0
+    )
+    full = jnp.where(even, same, other)
+    return full.reshape(size * rows, columns)
 
 
 def rows_major(matrix):
@@ -273,12 +296,10 @@
     )
     bias_up = bias_up.reshape(shards, up_bias.shape[0], -1).transpose(1, 0, 2).reshape(1, inner)
 
-    attn_part = jnp.concatenate(
-        [qkv_weight.reshape(qkv_weight.shape[0], 3 * width), proj_weight.T], axis=1
-    )
-    attn_full = lax.all_gather(attn_part, "fsdp", axis=0, tiled=True)
-    qkv_matrix = attn_full[:, : 3 * width]
-    proj_back = attn_full[:, 3 * width :]
+    qkv_matrix = lax.all_gather(
+        qkv_weight.reshape(qkv_weight.shape[0], 3 * width), "fsdp", axis=0, tiled=True
+    )
+    proj_back = gather_by_permutes(proj_weight.T, "fsdp")
     piece = up_weight.shape[0] // groups
     up_piece = lax.dynamic_slice_in_dim(up_weight, place * piece, piece, 0)
     down_piece = lax.dynamic_slice_in_dim(down_weight, place * piece, piece, 1)
@@ -332,6 +353,7 @@
         down_sent = dot(dmlp_low, sent_units, ((0,), (0,))).astype(bf16)
         down_got = swap_pair(down_sent, "ctx")
         down_kept = dot(dmlp_low, kept_units, ((0,), (0,))).astype(bf16)
+        down_kept = lax.optimization_barrier(down_kept)
         down_half = (down_kept.astype(f32) + down_got.astype(f32)).astype(bf16)
     else:
         down_half = lax.psum_scatter(

time: 367 us -> 364 us (level)
  waiting for transfers between devices: 156 us -> 128 us
  blocking collectives: 26.7 us -> 38.4 us
  local copies, waits for them, and re-layouts: 17.5 us -> 24.8 us
  starting transfers between devices: 15.9 us -> 22.5 us
    all_gather x1, waiting for transfers between devices: 29.4 us -> 2.86 us  [body(): lax.all_gather(qkv_weight.reshape(qkv_weight.shape[0], 3 * width), 'fsdp'...]
    all_gather x1, blocking collectives: 16.6 us -> 29.1 us  [body(): gathered = lax.all_gather(packed, 'fsdp', axis=0)]
    ppermute x0 -> x4, starting transfers between devices: none -> 7.11 us  [the longest x3 7.04 us: gather_by_permutes(): lax.ppermute(shard, axis, [(i, (i + 2 * k) % size) for i in range(size)])]
    unnamed x112 -> x122, local copies, waits for them, and re-layouts: 12.5 us -> 18 us
  transfers between devices with their start and end apart: 18 -> 22, of which waited for: 11 -> 13; matrix products, arithmetic and copies ran while one was open for 21% -> 24% of each run, Pallas kernels for 12% -> 12%
where the time goes in v6:
time: 364 us; the launch traced here: 360 us
  waiting for transfers between devices  128 us (35%)
  matrix products  56.3 us (15%)
  Pallas kernels  42.4 us (12%)
  blocking collectives  38.4 us (11%)
  other arithmetic  32.9 us (9%)
  local copies, waits for them, and re-layouts  24.8 us (7%)
  starting transfers between devices  22.5 us (6%)
  between operations  14.9 us (4%)
    ppermute x10, waiting for transfers between devices, swap_pair(): return lax.ppermute(part, axis, [(0, 1), (1, 0)])  80.2 us
    dot_general x14, matrix products, dot(): lax.dot_general(left, right, (dims, ((), ())), preferred_element_type=f32)  56.3 us
    ppermute x3, waiting for transfers between devices, ring_shift(): lax.ppermute(value, axis, [(i, (i + step) % size) for i in range(size)])  33.2 us
    pallas_call x2, Pallas kernels, attend_back(): pl.pallas_call(lambda *refs: backward_kernel(*refs, head_size=head_size,...  29.7 us
    all_gather x1, blocking collectives, body(): gathered = lax.all_gather(packed, 'fsdp', axis=0)  29.1 us
    unnamed x122, local copies, waits for them, and re-layouts  18 us
    pallas_call x1, Pallas kernels, attend(): pl.pallas_call(lambda *refs: forward_kernel(*refs, head_size=head_size, b...  12.6 us
    ppermute x10, starting transfers between devices, swap_pair(): return lax.ppermute(part, axis, [(0, 1), (1, 0)])  11.4 us
  transfers between devices with their start and end apart: 22, of which 13 were waited for; matrix products, arithmetic and copies ran while one was open for 24% of the time, Pallas kernels for 12%

profile of v6, /device:TPU:0, one launch (start us, length us, event | category | flops | bytes accessed | tf_op | source)
XLA Modules:
  0.0 360.3 jit_solution(13456559277527183866)
XLA Ops:
  7.3 2.0 copy.67
  11.0 3.1 collective-permute-start.3
  14.1 2.6 collective-permute-start.2
  20.5 29.1 %all-gather.1 = bf16[8,1,1408]{2,1,0:T(2,128)(2,1)S(1)} all-gather(bf16[1,1,1408]{2,1,0:T(2,128)(2,1)S(1)} %reshape.425), channel_id=2, replica_groups=mesh['fsdp'=8,'ctx'=2,'tp'=2] {'fsdp'}, dimensions={0}, use_global_device_ids=true | all-gather | bytes 25344 | tf_op jit(solution)/shard_map/all_gather | solution.py:280
  55.3 2.9 all-gather.5.cloned.1.call-done
  58.1 2.9 add_convert_fusion.3.refs_2_.refs_4_.refs_3_.refs_5_
  61.1 1.6 collective-permute-start
  66.6 3.3 fusion.46.refs_1_
  69.9 23.0 %collective-permute-done.refs_3_.refs_5_.refs_4_.refs_6_ = bf16[528,1024]{1,0:T(8,128)(2,1)} collective-permute-done((bf16[528,1024]{1,0:T(8,128)(2,1)S(1)}, bf16[528,1024]{1,0:T(8,128)(2,1)}, u32[]{:S(2)}, u32[]{:S(2)}) %collective-permute-start) | collective-permute-done | bytes 1081376 | tf_op jit(solution)/shard_map/ppermute | solution.py:95
  92.9 12.6 %attend.1 = bf16[528,512]{1,0:T(8,128)(2,1)} custom-call(s32[2]{0:T(128)} %and_select_fusion.1.refs_0_, bf16[528,512]{1,0:T(8,128)(2,1)} %fusion.46.refs_1_, bf16[528,1024]{1,0:T(8,128)(2,1)} %copy-done.9, bf16[528,1024]{1,0:T(8,128)(2,1)} %collective-permute-done.refs_3_.refs_5_.refs_4_.refs_6_, bf16[528,1024]{1,0:T(8,128)(2,1)} %copy-done.9, ...), custom_call_target="tpu_custom_call" | custom-call | flops 1141899264 | bytes 3244032 | tf_op jit(solution)/shard_map/attend/pallas_call | solution.py:187
  105.5 2.9 convolution_convert_fusion.4
  108.5 1.5 collective-permute-start.5
  111.6 22.4 %collective-permute-done.5 = bf16[528,1024]{1,0:T(8,128)(2,1)} collective-permute-done((bf16[528,1024]{1,0:T(8,128)(2,1)}, bf16[528,1024]{1,0:T(8,128)(2,1)}, u32[]{:S(2)}, u32[]{:S(2)}) %collective-permute-start.5) | collective-permute-done | bytes 1081376 | tf_op jit(solution)/shard_map/ppermute | solution.py:46
  134.0 2.2 fusion.74
  137.6 6.6 %multiply_convert_fusion = (bf16[528,2048]{1,0:T(8,128)(2,1)}, f32[528,2048]{1,0:T(8,128)S(1)}) fusion(f32[2048]{0:T(1024)S(1)} %reshape.412, bf16[1024,4096]{1,0:T(8,128)(2,1)} %all-gather.7.cloned.1.call-done, f32[528,1024]{1,0:T(8,128)S(1)} %get-tuple-element.110, f32[1024]{0:T(1024)S(1)} %get-tuple-element.122, f32[1024]{0:T(1024)S(1)} %get-tuple-element.123, ...), kind=kOutput, calls=%fused_computation.7 | convolution fusion | flops 2223783936 | bytes 12865664 | tf_op jit(solution)/shard_map/dot_general | solution.py:41
  144.2 4.4 %fusion.81 = (bf16[2048]{0:T(1024)(128)(2,1)S(1)}, bf16[528,2048]{1,0:T(8,128)(2,1)S(1)}) fusion(f32[528,2048]{1,0:T(8,128)S(1)} %get-tuple-element.143, f32[2048]{0:T(1024)S(1)} %reshape.412, bf16[528,1024]{1,0:T(8,128)(2,1)S(1)} %copy-done.18, bf16[1024,4096]{1,0:T(8,128)(2,1)S(1)} %copy-done.38), kind=kOutput, calls=%fused_computation.179 | convolution fusion | flops 2227566592 | bytes 11776000 | tf_op jit(solution)/shard_map/dot_general | solution.py:41
  148.6 3.4 fusion.38
  152.0 1.5 collective-permute-start.7
  153.5 4.8 %convolution_convert_fusion.2 = bf16[1024,1024]{1,0:T(8,128)(2,1)} fusion(bf16[528,1024]{1,0:T(8,128)(2,1)} %multiply_convert_fusion.2, bf16[528,2048]{1,0:T(8,128)(2,1)} %get-tuple-element.142, s32[]{:T(128)S(6)} %select_n.90), kind=kOutput, calls=%fused_computation.63 | convolution fusion | flops 1108344832 | bytes 4259844 | tf_op jit(solution)/shard_map/dot_general | solution.py:41
  158.9 3.4 convolution_convert_fusion.3
  162.4 16.0 %collective-permute-done.7 = bf16[528,1024]{1,0:T(8,128)(2,1)} collective-permute-done((bf16[528,1024]{1,0:T(8,128)(2,1)}, bf16[528,1024]{1,0:T(8,128)(2,1)}, u32[]{:S(2)}, u32[]{:S(2)}) %collective-permute-start.7) | collective-permute-done | bytes 1081376 | tf_op jit(solution)/shard_map/ppermute | solution.py:46
  178.3 2.7 multiply_reduce_fusion.1
  181.1 3.3 multiply_reduce_fusion.2
  186.8 19.3 %collective-permute-done.14 = bf16[1024,1024]{1,0:T(8,128)(2,1)} collective-permute-done((bf16[1024,1024]{1,0:T(8,128)(2,1)}, bf16[1024,1024]{1,0:T(8,128)(2,1)}, u32[]{:S(2)}, u32[]{:S(2)}) %collective-permute-start.14) | collective-permute-done | bytes 2097184 | tf_op jit(solution)/shard_map/ppermute | solution.py:46
  206.1 2.5 add_convert_fusion
  208.6 2.0 pad_maximum_fusion
  210.7 6.9 %convolution_convert_fusion = bf16[1024,2048]{1,0:T(8,128)(2,1)} fusion(bf16[528,2048]{1,0:T(8,128)(2,1)} %copy-done.40, f32[528,1024]{1,0:T(8,128)S(1)} %get-tuple-element.110, f32[1024]{0:T(1024)S(1)} %get-tuple-element.122, f32[1024]{0:T(1024)S(1)} %get-tuple-element.123, f32[528]{0:T(1024)S(1)} %add_rsqrt_fusion, f32[528]{0:T(1024)S(1)} %broadcast_multiply_fusion.4), kind=kOutput, calls=%fused_computation.10 | convolution fusion | flops 2219393024 | bytes 8532096 | tf_op jit(solution)/shard_map/dot_general | solution.py:41
  217.7 6.4 %fusion.41 = bf16[528,1024]{1,0:T(8,128)(2,1)} fusion(bf16[528,2048]{1,0:T(8,128)(2,1)} %get-tuple-element.142, bf16[1024,4096]{1,0:T(8,128)(2,1)} %all-gather.7.cloned.1.call-done), kind=kOutput, calls=%fused_computation.69 | convolution fusion | flops 2215133184 | bytes 7438336 | tf_op jit(solution)/shard_map/dot_general | solution.py:41
  224.6 1.5 convolution_convert_fusion.6.refs_2_
  226.2 15.0 %shard_map.289 = (bf16[528,256]{1,0:T(8,128)(2,1)}, f32[2,528,256]{2,1,0:T(8,128)}, bf16[2,528,256]{2,1,0:T(8,128)(2,1)}) custom-call(s32[2]{0:T(128)} %and_select_fusion.1.refs_0_, bf16[528,512]{1,0:T(8,128)(2,1)} %fusion.46.refs_1_, bf16[528,512]{1,0:T(8,128)(2,1)} %convolution_convert_fusion.6.refs_2_, bf16[528,1024]{1,0:T(8,128)(2,1)} %copy-done.9, ...), custom_call_target="tpu_custom_call" | custom-call | flops 1427374080 | bytes 4055040 | tf_op jit(solution)/shard_map/pallas_call | solution.py:214
  241.8 14.8 %shard_map.288 = (bf16[528,256]{1,0:T(8,128)(2,1)}, f32[2,528,256]{2,1,0:T(8,128)}, bf16[2,528,256]{2,1,0:T(8,128)(2,1)}) custom-call(s32[2]{0:T(128)} %and_select_fusion.1.refs_0_, bf16[528,512]{1,0:T(8,128)(2,1)} %fusion.46.refs_1_, bf16[528,512]{1,0:T(8,128)(2,1)} %convolution_convert_fusion.6.refs_2_, bf16[528,1024]{1,0:T(8,128)(2,1)} %copy-done.9, ...), custom_call_target="tpu_custom_call" | custom-call | flops 1427374080 | bytes 4055040 | tf_op jit(solution)/shard_map/pallas_call | solution.py:214
  256.6 1.5 collective-permute-start.9
  259.4 10.2 %collective-permute-done.9 = bf16[2,528,256]{2,1,0:T(8,128)(2,1)S(1)} collective-permute-done((bf16[2,528,256]{2,1,0:T(8,128)(2,1)}, bf16[2,528,256]{2,1,0:T(8,128)(2,1)S(1)}, u32[]{:S(2)}, u32[]{:S(2)}) %collective-permute-start.9) | collective-permute-done | bytes 540704 | tf_op jit(solution)/shard_map/ppermute | solution.py:95
  271.8 4.3 %convolution_convert_fusion.1 = bf16[1024,1536]{1,0:T(8,128)(2,1)} fusion(bf16[528,1536]{1,0:T(8,128)(2,1)S(1)} %bitcast_dynamic-update-slice_fusion, bf16[1,528,1024]{2,1,0:T(8,128)(2,1)S(1)} %copy-done.3, f32[1024]{0:T(1024)S(1)} %get-tuple-element.127, f32[1024]{0:T(1024)S(1)} %get-tuple-element.128, f32[528]{0:T(1024)S(1)} %add_rsqrt_fusion.1, ...), kind=kOutput, calls=%fused_computation.11 | convolution fusion | flops 1665761280 | bytes 5861504 | tf_op jit(solution)/shard_map/dot_general | solution.py:41
  276.4 4.3 %multiply_reduce_fusion = (bf16[1024]{0:T(1024)(128)(2,1)S(1)}, bf16[1024]{0:T(1024)(128)(2,1)S(1)}, bf16[1,528,1024]{2,1,0:T(8,128)(2,1)}) fusion(bf16[528,1024]{1,0:T(8,128)(2,1)} %collective-permute-done.6, bf16[528,1024]{1,0:T(8,128)(2,1)} %fusion.41, f32[1,528,1024]{2,1,0:T(8,128)} %param.33, f32[1024]{0:T(1024)S(1)} %get-tuple-element.121, ...), kind=kLoop, calls=%fused_computation.41 | loop fusion | flops 6486016 | bytes 7583808 | tf_op jit(solution)/shard_map/reduce_sum | solution.py:397
  281.1 4.4 %fusion.73 = (bf16[1024]{0:T(1024)(128)(2,1)S(1)}, bf16[1024]{0:T(1024)(128)(2,1)S(1)}, bf16[528,1024]{1,0:T(8,128)(2,1)S(1)}) fusion(f32[528]{0:T(1024)S(1)} %add_rsqrt_fusion.1, f32[528]{0:T(1024)S(1)} %broadcast_multiply_fusion.5, bf16[1,528,1024]{2,1,0:T(8,128)(2,1)S(1)} %copy-done.3, bf16[528,1536]{1,0:T(8,128)(2,1)} %copy-done.26, ...), kind=kOutput, calls=%fused_computation.172 | convolution fusion | flops 1664727040 | bytes 6938752 | tf_op jit(solution)/shard_map/dot_general | solution.py:41
  285.5 1.5 collective-permute-start.10
  288.3 9.3 %all_to_all.6 = bf16[8,2,704]{2,1,0:T(2,128)(2,1)S(1)} all-to-all(bf16[8,2,704]{2,1,0:T(2,128)(2,1)S(1)} %reshape.428), channel_id=1, replica_groups=mesh['fsdp'=8,'ctx'=2,'tp'=2] {'fsdp'}, dimensions={0} | all-to-all | bytes 45056 | tf_op jit(solution)/shard_map/all_to_all | solution.py:451
  297.7 1.6 collective-permute-start.11
  299.3 2.1 collective-permute-done.11
  304.0 5.3 %collective-permute-done.12 = bf16[256]{0:T(256)(128)(2,1)S(1)} collective-permute-done((bf16[256]{0:T(256)(128)(2,1)S(1)}, bf16[256]{0:T(256)(128)(2,1)S(1)}, u32[]{:S(2)}, u32[]{:S(2)}) %collective-permute-start.12) | collective-permute-done | bytes 544 | tf_op jit(solution)/shard_map/ppermute | solution.py:46
  310.6 1.5 collective-permute-start.15
  312.8 10.3 %collective-permute-done.15 = bf16[128,1536]{1,0:T(8,128)(2,1)} collective-permute-done((bf16[128,1536]{1,0:T(8,128)(2,1)}, bf16[128,1536]{1,0:T(8,128)(2,1)}, u32[]{:S(2)}, u32[]{:S(2)}) %collective-permute-start.15) | collective-permute-done | bytes 393248 | tf_op jit(solution)/shard_map/ppermute | solution.py:46
  325.2 4.9 %collective-permute-done.13 = bf16[128,2048]{1,0:T(8,128)(2,1)S(1)} collective-permute-done((bf16[128,2048]{1,0:T(8,128)(2,1)}, bf16[128,2048]{1,0:T(8,128)(2,1)S(1)}, u32[]{:S(2)}, u32[]{:S(2)}) %collective-permute-start.13) | collective-permute-done | bytes 524320 | tf_op jit(solution)/shard_map/ppermute | solution.py:46
  331.2 10.4 %reduce-scatter.4.cloned.1.call-done = bf16[128,1536]{1,0:T(8,128)(2,1)} async-done(((bf16[1024,1536]{1,0:T(8,128)(2,1)}), bf16[128,1536]{1,0:T(8,128)(2,1)}) %reduce-scatter.4.cloned.1.call-update) | async-done | bytes 393232 | tf_op jit(solution)/shard_map/reduce_scatter | solution.py:343
  341.6 1.5 collective-permute-start.16
  343.1 3.5 fusion.52
  346.5 2.6 copy.80
  (222 shorter events, 40.0 us)
Async XLA Ops:
  7.2 50.9 %all-gather.5.cloned.1.call-start = ((), (), s32[]{:S(2)}) async-start(), calls=%async_computation.4 | async-start | bytes 3538944 | tf_op jit(solution)/shard_map/all_gather | solution.py:299
  9.3 8.7 %copy-start.28 = (bf16[2,8,8]{2,1,0:T(8,128)(2,1)S(1)}, bf16[2,8,8]{2,1,0:T(8,128)(2,1)}, u32[]{:S(2)}) copy-start(bf16[2,8,8]{2,1,0:T(8,128)(2,1)} %param.22) | copy-start | bytes 772
  9.3 8.8 %copy-start.29 = (bf16[32,8]{0,1:T(8,128)(2,1)S(1)}, bf16[32,8]{0,1:T(8,128)(2,1)}, u32[]{:S(2)}) copy-start(bf16[32,8]{0,1:T(8,128)(2,1)} %param.29) | copy-start | bytes 1540
  9.3 9.0 %copy-start.30 = (bf16[128]{0:T(256)(128)(2,1)S(1)}, bf16[128]{0:T(256)(128)(2,1)}, u32[]{:S(2)}) copy-start(bf16[128]{0:T(256)(128)(2,1)} %param.19) | copy-start | bytes 772
  9.3 9.3 %copy-start.31 = (bf16[128]{0:T(256)(128)(2,1)S(1)}, bf16[128]{0:T(256)(128)(2,1)}, u32[]{:S(2)}) copy-start(bf16[128]{0:T(256)(128)(2,1)} %param.20) | copy-start | bytes 772
  9.3 9.7 %copy-start.32 = (bf16[128]{0:T(256)(128)(2,1)S(1)}, bf16[128]{0:T(256)(128)(2,1)}, u32[]{:S(2)}) copy-start(bf16[128]{0:T(256)(128)(2,1)} %param.24) | copy-start | bytes 772
  9.3 9.9 %copy-start.33 = (bf16[128]{0:T(256)(128)(2,1)S(1)}, bf16[128]{0:T(256)(128)(2,1)}, u32[]{:S(2)}) copy-start(bf16[128]{0:T(256)(128)(2,1)} %param.25) | copy-start | bytes 772
  9.3 10.1 %copy-start.34 = (bf16[128]{0:T(256)(128)(2,1)S(1)}, bf16[128]{0:T(256)(128)(2,1)}, u32[]{:S(2)}) copy-start(bf16[128]{0:T(256)(128)(2,1)} %param.26) | copy-start | bytes 772
  9.4 10.3 %copy-start.35 = (bf16[128]{0:T(256)(128)(2,1)S(1)}, bf16[128]{0:T(256)(128)(2,1)}, u32[]{:S(2)}) copy-start(bf16[128]{0:T(256)(128)(2,1)} %param.27) | copy-start | bytes 772
  9.4 10.7 %copy-start.36 = (bf16[128]{0:T(256)(128)(2,1)S(1)}, bf16[128]{0:T(256)(128)(2,1)}, u32[]{:S(2)}) copy-start(bf16[128]{0:T(256)(128)(2,1)} %param.31) | copy-start | bytes 772
  9.4 10.9 %copy-start.37 = (bf16[128]{0:T(256)(128)(2,1)S(1)}, bf16[128]{0:T(256)(128)(2,1)}, u32[]{:S(2)}) copy-start(bf16[128]{0:T(256)(128)(2,1)} %param.32) | copy-start | bytes 772
  9.4 128.2 %all-gather.7.cloned.1.call-start = ((), (), s32[]{:S(2)}) async-start(), calls=%async_computation.5 | async-start | bytes 8912896 | tf_op jit(solution)/shard_map/all_gather | solution.py:306
  9.5 40.3 %copy-start.3 = (bf16[1,528,1024]{2,1,0:T(8,128)(2,1)S(1)}, bf16[1,528,1024]{2,1,0:T(8,128)(2,1)}, u32[]{:S(2)}) copy-start(bf16[1,528,1024]{2,1,0:T(8,128)(2,1)} %param.17) | copy-start | bytes 3244036
  10.8 299.9 %reduce-scatter.8.cloned.1.call-start = ((), (), s32[]{:S(2)}) async-start(), calls=%async_computation.8 | async-start | bytes 3538944 | tf_op jit(solution)/shard_map/reduce_scatter | solution.py:343
  11.0 41.0 %collective-permute-start.3 = (bf16[128,512]{1,0:T(8,128)(2,1)S(1)}, bf16[128,512]{1,0:T(8,128)(2,1)S(1)}, u32[]{:S(2)}, u32[]{:S(2)}) collective-permute-start(bf16[128,512]{1,0:T(8,128)(2,1)S(1)} %bitcast.178), channel_id=1, source_target_pairs={{0,8},{4,12},{8,16},{12,20},{16,24},{20,28},{24,0},{28,4},{1,9},{5... | collective-permute-start | bytes 393224 | tf_op jit(solution)/shard_map/ppermute | solution.py:68
  14.1 37.2 %collective-permute-start.2 = (bf16[128,512]{1,0:T(8,128)(2,1)S(1)}, bf16[128,512]{1,0:T(8,128)(2,1)S(1)}, u32[]{:S(2)}, u32[]{:S(2)}) collective-permute-start(bf16[128,512]{1,0:T(8,128)(2,1)S(1)} %bitcast.179), channel_id=1, source_target_pairs={{0,16},{4,20},{8,24},{12,28},{16,0},{20,4},{24,8},{28,12},{1,17},{... | collective-permute-start | bytes 393224 | tf_op jit(solution)/shard_map/ppermute | solution.py:68
  16.7 33.9 %collective-permute-start.1 = (bf16[128,512]{1,0:T(8,128)(2,1)S(1)}, bf16[128,512]{1,0:T(8,128)(2,1)S(1)}, u32[]{:S(2)}, u32[]{:S(2)}) collective-permute-start(bf16[128,512]{1,0:T(8,128)(2,1)S(1)} %bitcast.180), channel_id=1, source_target_pairs={{0,24},{4,28},{8,0},{12,4},{16,8},{20,12},{24,16},{28,20},{1,25},{... | collective-permute-start | bytes 393224 | tf_op jit(solution)/shard_map/ppermute | solution.py:68
  58.1 6.6 %copy-start.2 = (s32[1,2]{1,0:T(1,128)S(1)}, s32[1,2]{1,0:T(1,128)}, u32[]{:S(2)}) copy-start(s32[1,2]{1,0:T(1,128)} %param.18) | copy-start | bytes 28
  61.1 8.8 %copy-start.9 = (bf16[528,1024]{1,0:T(8,128)(2,1)}, bf16[528,1024]{1,0:T(8,128)(2,1)S(1)}, u32[]{:S(2)}) copy-start(bf16[528,1024]{1,0:T(8,128)(2,1)S(1)} %add_convert_fusion.3.refs_2_.refs_4_.refs_3_.refs_5_) | copy-start | bytes 3244036
  61.1 31.8 %collective-permute-start = (bf16[528,1024]{1,0:T(8,128)(2,1)S(1)}, bf16[528,1024]{1,0:T(8,128)(2,1)}, u32[]{:S(2)}, u32[]{:S(2)}) collective-permute-start(bf16[528,1024]{1,0:T(8,128)(2,1)S(1)} %add_convert_fusion.3.refs_2_.refs_4_.refs_3_.refs_5_), channel_id=1, source_target_pairs={{0,2},{2,0},{1,3},{3,1},{4,6},{6,4},{5,7},{7,5},{8,10},{10,8},{9,1... | collective-permute-start | bytes 3244040 | tf_op jit(solution)/shard_map/ppermute | solution.py:95
  64.4 2.0 collective-permute-start.4
  66.6 38.9 %copy-start.12 = (bf16[1024,512]{1,0:T(8,128)(2,1)}, bf16[1024,512]{1,0:T(8,128)(2,1)S(1)}, u32[]{:S(2)}) copy-start(bf16[1024,512]{1,0:T(8,128)(2,1)S(1)} %bitcast_select_fusion) | copy-start | bytes 3145732
  108.5 25.5 %collective-permute-start.5 = (bf16[528,1024]{1,0:T(8,128)(2,1)}, bf16[528,1024]{1,0:T(8,128)(2,1)}, u32[]{:S(2)}, u32[]{:S(2)}) collective-permute-start(bf16[528,1024]{1,0:T(8,128)(2,1)} %convolution_convert_fusion.4), channel_id=1, source_target_pairs={{0,1},{1,0},{2,3},{3,2},{4,5},{5,4},{6,7},{7,6},{8,9},{9,8},{10,11... | collective-permute-start | bytes 3244040 | tf_op jit(solution)/shard_map/ppermute | solution.py:46
  137.6 6.6 %copy-start.18 = (bf16[528,1024]{1,0:T(8,128)(2,1)S(1)}, bf16[528,1024]{1,0:T(8,128)(2,1)}, u32[]{:S(2)}) copy-start(bf16[528,1024]{1,0:T(8,128)(2,1)} %multiply_convert_fusion.2) | copy-start | bytes 3244036
  137.6 6.6 %copy-start.38 = (bf16[1024,4096]{1,0:T(8,128)(2,1)S(1)}, bf16[1024,4096]{1,0:T(8,128)(2,1)}, u32[]{:S(2)}) copy-start(bf16[1024,4096]{1,0:T(8,128)(2,1)} %all-gather.7.cloned.1.call-done) | copy-start | bytes 25165828
  152.0 26.3 %collective-permute-start.7 = (bf16[528,1024]{1,0:T(8,128)(2,1)}, bf16[528,1024]{1,0:T(8,128)(2,1)}, u32[]{:S(2)}, u32[]{:S(2)}) collective-permute-start(bf16[528,1024]{1,0:T(8,128)(2,1)} %fusion.38), channel_id=1, source_target_pairs={{0,1},{1,0},{2,3},{3,2},{4,5},{5,4},{6,7},{7,6},{8,9},{9,8},{10,11... | collective-permute-start | bytes 3244040 | tf_op jit(solution)/shard_map/ppermute | solution.py:46
  158.3 47.8 %collective-permute-start.14 = (bf16[1024,1024]{1,0:T(8,128)(2,1)}, bf16[1024,1024]{1,0:T(8,128)(2,1)}, u32[]{:S(2)}, u32[]{:S(2)}) collective-permute-start(bf16[1024,1024]{1,0:T(8,128)(2,1)} %convolution_convert_fusion.2), channel_id=1, source_target_pairs={{0,2},{2,0},{1,3},{3,1},{4,6},{6,4},{5,7},{7,5},{8,10},{10,8},{9,1... | collective-permute-start | bytes 6291464 | tf_op jit(solution)/shard_map/ppermute | solution.py:46
  162.3 18.7 %copy-start.5 = (f32[1,528,1024]{2,1,0:T(8,128)S(1)}, f32[1,528,1024]{2,1,0:T(8,128)}, u32[]{:S(2)}) copy-start(f32[1,528,1024]{2,1,0:T(8,128)} %param.33) | copy-start | bytes 6488068
  210.6 101.5 %reduce-scatter.6.cloned.1.call-start = ((), (), s32[]{:S(2)}) async-start(), calls=%async_computation.7 | async-start | bytes 4718592 | tf_op jit(solution)/shard_map/reduce_scatter | solution.py:343
  217.6 124.0 %reduce-scatter.4.cloned.1.call-start = ((), (), s32[]{:S(2)}) async-start(), calls=%async_computation.6 | async-start | bytes 3538944 | tf_op jit(solution)/shard_map/reduce_scatter | solution.py:343
  217.7 7.0 %copy-start.7 = (f32[528,1024]{1,0:T(8,128)S(1)}, f32[528,1024]{1,0:T(8,128)}, u32[]{:S(2)}) copy-start(f32[528,1024]{1,0:T(8,128)} %copy-done.6) | copy-start | bytes 6488068
  217.7 7.0 %copy-start.13 = (bf16[1024,512]{1,0:T(8,128)(2,1)S(1)}, bf16[1024,512]{1,0:T(8,128)(2,1)}, u32[]{:S(2)}) copy-start(bf16[1024,512]{1,0:T(8,128)(2,1)} %copy-done.12) | copy-start | bytes 3145732
  224.1 52.3 %collective-permute-start.6 = (bf16[528,1024]{1,0:T(8,128)(2,1)}, bf16[528,1024]{1,0:T(8,128)(2,1)}, u32[]{:S(2)}, u32[]{:S(2)}) collective-permute-start(bf16[528,1024]{1,0:T(8,128)(2,1)} %fusion.41), channel_id=1, source_target_pairs={{0,1},{1,0},{2,3},{3,2},{4,5},{5,4},{6,7},{7,6},{8,9},{9,8},{10,11... | collective-permute-start | bytes 3244040 | tf_op jit(solution)/shard_map/ppermute | solution.py:46
  241.2 16.9 %copy-start.23 = (bf16[528,256]{1,0:T(8,128)(2,1)S(1)}, bf16[528,256]{1,0:T(8,128)(2,1)}, u32[]{:S(2)}) copy-start(bf16[528,256]{1,0:T(8,128)(2,1)} %get-tuple-element.26) | copy-start | bytes 811012
  241.2 18.1 %copy-start.20 = (f32[2,528,256]{2,1,0:T(8,128)S(1)}, f32[2,528,256]{2,1,0:T(8,128)}, u32[]{:S(2)}) copy-start(f32[2,528,256]{2,1,0:T(8,128)} %get-tuple-element.27) | copy-start | bytes 3244036
  241.2 18.1 %collective-permute-start.8 = (bf16[2,528,256]{2,1,0:T(8,128)(2,1)}, bf16[2,528,256]{2,1,0:T(8,128)(2,1)S(1)}, u32[]{:S(2)}, u32[]{:S(2)}) collective-permute-start(bf16[2,528,256]{2,1,0:T(8,128)(2,1)} %get-tuple-element.28), channel_id=1, source_target_pairs={{0,2},{2,0},{1,3},{3,1},{4,6},{6,4},{5,7},{7,5},{8,10},{10,8},{9,1... | collective-permute-start | bytes 1622024 | tf_op jit(solution)/shard_map/ppermute | solution.py:95
  256.6 13.1 %copy-start.19 = (f32[2,528,256]{2,1,0:T(8,128)S(1)}, f32[2,528,256]{2,1,0:T(8,128)}, u32[]{:S(2)}) copy-start(f32[2,528,256]{2,1,0:T(8,128)} %get-tuple-element.29) | copy-start | bytes 3244036
  256.6 13.1 %collective-permute-start.9 = (bf16[2,528,256]{2,1,0:T(8,128)(2,1)}, bf16[2,528,256]{2,1,0:T(8,128)(2,1)S(1)}, u32[]{:S(2)}, u32[]{:S(2)}) collective-permute-start(bf16[2,528,256]{2,1,0:T(8,128)(2,1)} %get-tuple-element.30), channel_id=1, source_target_pairs={{0,2},{2,0},{1,3},{3,1},{4,6},{6,4},{5,7},{7,5},{8,10},{10,8},{9,1... | collective-permute-start | bytes 1622024 | tf_op jit(solution)/shard_map/ppermute | solution.py:95
  259.4 10.4 %copy-start.14 = (bf16[2,528,256]{2,1,0:T(8,128)(2,1)}, bf16[2,528,256]{2,1,0:T(8,128)(2,1)S(1)}, u32[]{:S(2)}) copy-start(bf16[2,528,256]{2,1,0:T(8,128)(2,1)S(1)} %add_convert_fusion.5) | copy-start | bytes 1622020
  285.5 27.3 %copy-start.10 = (bf16[528,1024]{1,0:T(8,128)(2,1)}, bf16[528,1024]{1,0:T(8,128)(2,1)S(1)}, u32[]{:S(2)}) copy-start(bf16[528,1024]{1,0:T(8,128)(2,1)S(1)} %get-tuple-element.112) | copy-start | bytes 3244036
  285.5 24.3 %collective-permute-start.10 = (bf16[528,1024]{1,0:T(8,128)(2,1)S(1)}, bf16[528,1024]{1,0:T(8,128)(2,1)S(1)}, u32[]{:S(2)}, u32[]{:S(2)}) collective-permute-start(bf16[528,1024]{1,0:T(8,128)(2,1)S(1)} %get-tuple-element.112), channel_id=1, source_target_pairs={{0,1},{1,0},{2,3},{3,2},{4,5},{5,4},{6,7},{7,6},{8,9},{9,8},{10,11... | collective-permute-start | bytes 3244040 | tf_op jit(solution)/shard_map/ppermute | solution.py:46
  297.7 3.7 %collective-permute-start.11 = (bf16[1408]{0:T(1024)(128)(2,1)S(1)}, bf16[1408]{0:T(1024)(128)(2,1)S(1)}, u32[]{:S(2)}, u32[]{:S(2)}) collective-permute-start(bf16[1408]{0:T(1024)(128)(2,1)S(1)} %reduce_sum.222), channel_id=1, source_target_pairs={{0,2},{2,0},{1,3},{3,1},{4,6},{6,4},{5,7},{7,5},{8,10},{10,8},{9,1... | collective-permute-start | bytes 8456 | tf_op jit(solution)/shard_map/ppermute | solution.py:46
  301.4 7.9 %collective-permute-start.12 = (bf16[256]{0:T(256)(128)(2,1)S(1)}, bf16[256]{0:T(256)(128)(2,1)S(1)}, u32[]{:S(2)}, u32[]{:S(2)}) collective-permute-start(bf16[256]{0:T(256)(128)(2,1)S(1)} %slice.276), channel_id=1, source_target_pairs={{0,1},{1,0},{2,3},{3,2},{4,5},{5,4},{6,7},{7,6},{8,9},{9,8},{10,11... | collective-permute-start | bytes 1544 | tf_op jit(solution)/shard_map/ppermute | solution.py:46
  310.6 12.4 %collective-permute-start.15 = (bf16[128,1536]{1,0:T(8,128)(2,1)}, bf16[128,1536]{1,0:T(8,128)(2,1)}, u32[]{:S(2)}, u32[]{:S(2)}) collective-permute-start(bf16[128,1536]{1,0:T(8,128)(2,1)} %reduce-scatter.8.cloned.1.call-done), channel_id=1, source_target_pairs={{0,2},{2,0},{1,3},{3,1},{4,6},{6,4},{5,7},{7,5},{8,10},{10,8},{9,1... | collective-permute-start | bytes 1179656 | tf_op jit(solution)/shard_map/ppermute | solution.py:46
  312.1 18.0 %copy-start.21 = (bf16[128,2048]{1,0:T(8,128)(2,1)S(1)}, bf16[128,2048]{1,0:T(8,128)(2,1)}, u32[]{:S(2)}) copy-start(bf16[128,2048]{1,0:T(8,128)(2,1)} %reduce-scatter.6.cloned.1.call-done) | copy-start | bytes 1572868
  312.1 18.0 %collective-permute-start.13 = (bf16[128,2048]{1,0:T(8,128)(2,1)}, bf16[128,2048]{1,0:T(8,128)(2,1)S(1)}, u32[]{:S(2)}, u32[]{:S(2)}) collective-permute-start(bf16[128,2048]{1,0:T(8,128)(2,1)} %reduce-scatter.6.cloned.1.call-done), channel_id=1, source_target_pairs={{0,2},{2,0},{1,3},{3,1},{4,6},{6,4},{5,7},{7,5},{8,10},{10,8},{9,1... | collective-permute-start | bytes 1572872 | tf_op jit(solution)/shard_map/ppermute | solution.py:46
  312.8 30.3 %copy-start.8 = (f32[528,1024]{1,0:T(8,128)S(1)}, f32[528,1024]{1,0:T(8,128)}, u32[]{:S(2)}) copy-start(f32[528,1024]{1,0:T(8,128)} %copy-done.6) | copy-start | bytes 6488068
  341.6 9.4 %collective-permute-start.16 = (bf16[128,1536]{1,0:T(8,128)(2,1)}, bf16[128,1536]{1,0:T(8,128)(2,1)}, u32[]{:S(2)}, u32[]{:S(2)}) collective-permute-start(bf16[128,1536]{1,0:T(8,128)(2,1)} %reduce-scatter.4.cloned.1.call-done), channel_id=1, source_target_pairs={{0,2},{2,0},{1,3},{3,1},{4,6},{6,4},{5,7},{7,5},{8,10},{10,8},{9,1... | collective-permute-start | bytes 1179656 | tf_op jit(solution)/shard_map/ppermute | solution.py:46
  (15 other events, 47.1 us)
Sparse Core Ops, SparseCore 0:
  10.2 47.8 all-gather.4
  60.3 77.1 all-gather.6
  210.7 38.0 reduce-scatter.7
  251.0 49.5 reduce-scatter.5
  302.7 38.8 reduce-scatter.3

commit v7 on v6

--- a/solution.py
+++ b/solution.py
@@ -55,6 +55,16 @@
 
 def exchange_sum(part, axis):
     return pair_sum(part, swap_pair(part, axis), axis)
+
+
+def interleave_kernel(place_ref, same_ref, other_ref, out_ref, *, steps, rows):
+    step, odd = place_ref[0], place_ref[1]
+    for member in range(steps):
+        piece = (step - member + steps) % steps
+        mine, yours = same_ref[piece], other_ref[piece]
+        first = 2 * member * rows
+        out_ref[first : first + rows] = jnp.where(odd == 0, mine, yours)
+        out_ref[first + rows : first + 2 * rows] = jnp.where(odd == 0, yours, mine)
 
 
 def gather_by_permutes(shard, axis):
@@ -67,17 +77,16 @@
         pieces.append(
             lax.ppermute(shard, axis, [(i, (i + 2 * k) % size) for i in range(size)])
         )
-    backward = jnp.concatenate(pieces[::-1] * 2, axis=0)
-    start = (steps - 1 - index // 2) * rows
-    same = lax.dynamic_slice_in_dim(backward, start, steps * rows, 0)
+    same = jnp.stack(pieces)
     other = lax.ppermute(same, axis, [(i, i ^ 1) for i in range(size)])
-    same = same.reshape(steps, 1, rows, columns)
-    other = other.reshape(steps, 1, rows, columns)
-    even = (index % 2 == 0) == (
-        lax.broadcasted_iota(jnp.int32, (1, 2, 1, 1), 1) == 0
-    )
-    full = jnp.where(even, same, other)
-    return full.reshape(size * rows, columns)
+    whole = pl.BlockSpec((steps, rows, columns), lambda: (0, 0, 0))
+    full = pl.pallas_call(
+        lambda *refs: interleave_kernel(*refs, steps=steps, rows=rows),
+        in_specs=[pl.BlockSpec(memory_space=pltpu.SMEM), whole, whole],
+        out_specs=pl.BlockSpec((size * rows, columns), lambda: (0, 0)),
+        out_shape=jax.ShapeDtypeStruct((size * rows, columns), shard.dtype),
+    )(jnp.stack([index // 2, index % 2]).astype(jnp.int32), same, other)
+    return full
 
 
 def rows_major(matrix):
@@ -138,7 +147,6 @@
     def one_head(head, carry):
         mask = head_mask(rows, width, head_size, head)
         query = query_ref[...].astype(f32)
-        head_query = (query * mask).astype(bf16)
         scaled_query = (query * (mask * scaling)).astype(bf16)
         head_grads = (grad_ref[...].astype(f32) * mask).astype(bf16)
         scores = [
@@ -164,10 +172,12 @@
         for i, ref in enumerate(grad_refs):
             value_grad = dot(probabilities[i].astype(bf16), head_grads, ((1,), (0,)))
             ref[1] = (ref[1].astype(f32) + value_grad).astype(ref.dtype)
-            dscores = (probabilities[i] * (dprobs[i] - row_total) * scaling).astype(bf16)
-            key_grad = dot(dscores, head_query, ((1,), (0,)))
+            dscores = (probabilities[i] * (dprobs[i] - row_total)).astype(bf16)
+            key_grad = dot(dscores, scaled_query, ((1,), (0,)))
             ref[0] = (ref[0].astype(f32) + key_grad).astype(ref.dtype)
-            query_grad = query_grad + dot(dscores, key_refs[i][...], ((0,), (0,))) * mask
+            query_grad = query_grad + dot(dscores, key_refs[i][...], ((0,), (0,))) * (
+                mask * scaling
+            )
         query_grad_ref[...] = query_grad.astype(bf16)
         return carry
 
@@ -276,8 +286,9 @@
         mlp_scale,
     ]
     sizes = [math.prod(item.shape) for item in small]
-    packed = jnp.concatenate([item.reshape(-1) for item in small])
-    gathered = lax.all_gather(packed, "fsdp", axis=0)
+    base = first_gain.shape[0]
+    packed = jnp.concatenate([item.reshape(-1, base) for item in small], axis=0)
+    gathered = lax.all_gather(packed, "fsdp", axis=0).reshape(shards, -1)
     full = []
     offset = 0
     for size in sizes:
@@ -296,9 +307,10 @@
     )
     bias_up = bias_up.reshape(shards, up_bias.shape[0], -1).transpose(1, 0, 2).reshape(1, inner)
 
-    qkv_matrix = lax.all_gather(
-        qkv_weight.reshape(qkv_weight.shape[0], 3 * width), "fsdp", axis=0, tiled=True
-    )
+    kv_full = lax.all_gather(
+        qkv_weight[:, 1:].reshape(qkv_weight.shape[0], 2 * width), "fsdp", axis=0, tiled=True
+    )
+    query_full = gather_by_permutes(qkv_weight[:, 0], "fsdp")
     proj_back = gather_by_permutes(proj_weight.T, "fsdp")
     piece = up_weight.shape[0] // groups
     up_piece = lax.dynamic_slice_in_dim(up_weight, place * piece, piece, 0)
@@ -313,15 +325,17 @@
     normed_one, unit_one, inverse_one = normalize(source, gain_one, shift_one)
     low_one = normed_one.astype(bf16)
     bias_kv = jnp.concatenate([jnp.zeros((width,), f32), bias_pair[1]])
-    own = (dot(low_one, qkv_matrix[:, width:], ((1,), (0,))) + bias_kv).astype(bf16)
+    own = (dot(low_one, kv_full, ((1,), (0,))) + bias_kv).astype(bf16)
     others = [ring_shift(own, "ctx", step) for step in range(1, groups)]
-    queries = (dot(low_one, qkv_matrix[:, :width], ((1,), (0,))) + bias_pair[0]).astype(bf16)
+    queries = (dot(low_one, query_full, ((1,), (0,))) + bias_pair[0]).astype(bf16)
     order = (place - jnp.arange(groups, dtype=jnp.int32)) % groups
     live = jnp.take(lengths[0], order)
     mixed = attend(live, queries, own, others, head_size)
 
     proj_part = dot(mixed, proj_back, ((1,), (1,))).astype(bf16)
-    projected = exchange_sum(proj_part, "tp") + bias_proj
+    proj_other = swap_pair(proj_part, "tp")
+    qkv_matrix = jnp.concatenate([query_full, kv_full], axis=1)
+    projected = pair_sum(proj_part, proj_other, "tp") + bias_proj
     resid = source + scale_one * projected
     normed_two, unit_two, inverse_two = normalize(resid, gain_two, shift_two)
     low_two = normed_two.astype(bf16)

time: 364 us -> 368 us (1.011)
  waiting for transfers between devices: 128 us -> 115 us
  blocking collectives: 38.4 us -> 46.5 us
  other arithmetic: 32.9 us -> 38.3 us
  Pallas kernels: 42.4 us -> 46.8 us
    ppermute x3, waiting for transfers between devices: 33.2 us -> 23.4 us  [ring_shift(): lax.ppermute(value, axis, [(i, (i + step) % size) for i in range(size)])]
    all_gather x1, blocking collectives: 29.1 us -> 36.2 us  [body(): gathered = lax.all_gather(packed, 'fsdp', axis=0).reshape(shards, -1)]
    unnamed x122 -> x131, local copies, waits for them, and re-layouts: 18 us -> 11.6 us
    ppermute x10, waiting for transfers between devices: 80.2 us -> 75.6 us  [swap_pair(): return lax.ppermute(part, axis, [(0, 1), (1, 0)])]
    pallas_call x0 -> x2, Pallas kernels: none -> 4.51 us  [gather_by_permutes(): pl.pallas_call(lambda *refs: interleave_kernel(*refs, steps=steps, rows=r...]
    another operation x0 -> x3, other arithmetic: none -> 4.31 us  [the longest x2 3.72 us: gather_by_permutes(): same = jnp.stack(pieces)]
    ppermute x3 -> x6, starting transfers between devices: 7.04 us -> 9.77 us  [gather_by_permutes(): lax.ppermute(shard, axis, [(i, (i + 2 * k) % size) for i in range(size)])]
  transfers between devices with their start and end apart: 22 -> 26, of which waited for: 13 -> 11; matrix products, arithmetic and copies ran while one was open for 24% -> 24% of each run, Pallas kernels for 12% -> 13%
where the time goes in v7:
time: 368 us; the launch traced here: 364 us
  waiting for transfers between devices  115 us (31%)
  matrix products  55.8 us (15%)
  Pallas kernels  46.8 us (13%)
  blocking collectives  46.5 us (13%)
  other arithmetic  38.3 us (10%)
  starting transfers between devices  25.2 us (7%)
  local copies, waits for them, and re-layouts  22 us (6%)
  between operations  15 us (4%)
    ppermute x10, waiting for transfers between devices, swap_pair(): return lax.ppermute(part, axis, [(0, 1), (1, 0)])  75.6 us
    dot_general x14, matrix products, dot(): lax.dot_general(left, right, (dims, ((), ())), preferred_element_type=f32)  55.8 us
    all_gather x1, blocking collectives, body(): gathered = lax.all_gather(packed, 'fsdp', axis=0).reshape(shards, -1)  36.2 us
    pallas_call x2, Pallas kernels, attend_back(): pl.pallas_call(lambda *refs: backward_kernel(*refs, head_size=head_size,...  29.6 us
    ppermute x3, waiting for transfers between devices, ring_shift(): lax.ppermute(value, axis, [(i, (i + step) % size) for i in range(size)])  23.4 us
    reduce_scatter x3, waiting for transfers between devices, reduce_shards(): return lax.psum_scatter(matrix, 'fsdp', scatter_dimension=0, tiled=True)  12.6 us
    pallas_call x1, Pallas kernels, attend(): pl.pallas_call(lambda *refs: forward_kernel(*refs, head_size=head_size, b...  12.6 us
    unnamed x131, local copies, waits for them, and re-layouts  11.6 us
  transfers between devices with their start and end apart: 26, of which 11 were waited for; matrix products, arithmetic and copies ran while one was open for 24% of the time, Pallas kernels for 13%

profile of v7, /device:TPU:0, one launch (start us, length us, event | category | flops | bytes accessed | tf_op | source)
XLA Modules:
  0.0 364.5 jit_solution(878185137209487799)
XLA Ops:
  10.9 4.1 %collective-permute-start.6 = (bf16[128,512]{1,0:T(8,128)(2,1)S(1)}, bf16[128,512]{1,0:T(8,128)(2,1)}, u32[]{:S(2)}, u32[]{:S(2)}) collective-permute-start(bf16[128,512]{1,0:T(8,128)(2,1)S(1)} %bitcast.196), channel_id=1, source_target_pairs={{0,16},{4,20},{8,24},{12,28},{16,0},{20,4},{24,8},{28,12},{1,17},{... | collective-permute-start | bytes 393224 | tf_op jit(solution)/shard_map/ppermute | solution.py:78
  15.1 1.6 collective-permute-start.5
  16.6 2.2 collective-permute-start.7
  18.9 1.6 slice_bitcast_fusion.3
  22.2 36.2 %all-gather.1 = bf16[8,11,128]{2,1,0:T(8,128)(2,1)S(1)} all-gather(bf16[1,11,128]{2,1,0:T(8,128)(2,1)S(1)} %bitcast.207), channel_id=2, replica_groups=mesh['fsdp'=8,'ctx'=2,'tp'=2] {'fsdp'}, dimensions={0}, use_global_device_ids=true | all-gather | bytes 25344 | tf_op jit(solution)/shard_map/all_gather | solution.py:291
  61.3 3.0 add_convert_fusion.3.refs_2_.refs_4_.refs_3_.refs_5_
  65.8 3.3 collective-permute-done
  69.1 1.8 pad_maximum_fusion.1.refs_1_
  70.9 1.9 pad_maximum_fusion.2.refs_1_
  75.1 2.3 shard_map.288
  77.4 2.3 shard_map.289
  79.7 2.8 fusion.46.refs_1_
  82.5 13.6 %collective-permute-done.4.refs_3_.refs_5_.refs_4_.refs_6_ = bf16[528,1024]{1,0:T(8,128)(2,1)S(1)} collective-permute-done((bf16[528,1024]{1,0:T(8,128)(2,1)S(1)}, bf16[528,1024]{1,0:T(8,128)(2,1)S(1)}, u32[]{:S(2)}, u32[]{:S(2)}) %collective-permute-start.4) | collective-permute-done | bytes 1081376 | tf_op jit(solution)/shard_map/ppermute | solution.py:104
  97.1 12.6 %attend.1 = bf16[528,512]{1,0:T(8,128)(2,1)} custom-call(s32[2]{0:T(128)} %and_select_fusion.1.refs_0_, bf16[528,512]{1,0:T(8,128)(2,1)} %fusion.46.refs_1_, bf16[528,1024]{1,0:T(8,128)(2,1)} %copy-done.9, bf16[528,1024]{1,0:T(8,128)(2,1)} %copy-done.10, bf16[528,1024]{1,0:T(8,128)(2,1)} %copy-done.9, bf16[528,1024]{1,0:T(8,128)(2,1)} %copy-done.10), custom_call_target="tpu_custom_call" | custom-call | flops 1141899264 | bytes 3244032 | tf_op jit(solution)/shard_map/attend/pallas_call | solution.py:197
  109.8 3.0 convolution_convert_fusion.4
  116.3 21.9 %collective-permute-done.9 = bf16[528,1024]{1,0:T(8,128)(2,1)} collective-permute-done((bf16[528,1024]{1,0:T(8,128)(2,1)}, bf16[528,1024]{1,0:T(8,128)(2,1)}, u32[]{:S(2)}, u32[]{:S(2)}) %collective-permute-start.9) | collective-permute-done | bytes 1081376 | tf_op jit(solution)/shard_map/ppermute | solution.py:46
  138.3 2.2 fusion.74
  141.2 6.6 %multiply_convert_fusion = (bf16[528,2048]{1,0:T(8,128)(2,1)}, f32[528,2048]{1,0:T(8,128)S(1)}) fusion(f32[2048]{0:T(1024)S(1)} %reshape.433, bf16[1024,4096]{1,0:T(8,128)(2,1)} %all-gather.7.cloned.1.call-done, f32[528,1024]{1,0:T(8,128)S(1)} %get-tuple-element.110, f32[1024]{0:T(1024)S(1)} %copy-done.39, f32[1024]{0:T(1024)S(1)} %get-tuple-element.125, ...), kind=kOutput, calls=%fused_computation.7 | convolution fusion | flops 2223783936 | bytes 12865664 | tf_op jit(solution)/shard_map/dot_general | solution.py:41
  147.8 4.4 %fusion.81 = (bf16[2048]{0:T(1024)(128)(2,1)S(1)}, bf16[528,2048]{1,0:T(8,128)(2,1)S(1)}) fusion(f32[528,2048]{1,0:T(8,128)S(1)} %get-tuple-element.145, f32[2048]{0:T(1024)S(1)} %reshape.433, bf16[528,1024]{1,0:T(8,128)(2,1)S(1)} %copy-done.19, bf16[1024,4096]{1,0:T(8,128)(2,1)S(1)} %copy-done.51), kind=kOutput, calls=%fused_computation.175 | convolution fusion | flops 2227566592 | bytes 11776000 | tf_op jit(solution)/shard_map/dot_general | solution.py:41
  152.2 3.4 fusion.40
  155.6 1.5 collective-permute-start.11
  157.1 4.8 %convolution_convert_fusion.2 = bf16[1024,1024]{1,0:T(8,128)(2,1)} fusion(bf16[528,1024]{1,0:T(8,128)(2,1)} %multiply_convert_fusion.2, bf16[528,2048]{1,0:T(8,128)(2,1)} %get-tuple-element.144, s32[]{:T(128)S(6)} %select_n.83), kind=kOutput, calls=%fused_computation.65 | convolution fusion | flops 1108344832 | bytes 4259844 | tf_op jit(solution)/shard_map/dot_general | solution.py:41
  163.4 3.4 convolution_convert_fusion.3
  166.8 13.5 %collective-permute-done.11 = bf16[528,1024]{1,0:T(8,128)(2,1)} collective-permute-done((bf16[528,1024]{1,0:T(8,128)(2,1)}, bf16[528,1024]{1,0:T(8,128)(2,1)}, u32[]{:S(2)}, u32[]{:S(2)}) %collective-permute-start.11) | collective-permute-done | bytes 1081376 | tf_op jit(solution)/shard_map/ppermute | solution.py:46
  180.3 2.7 multiply_reduce_fusion.1
  183.0 3.4 multiply_reduce_fusion.2
  188.8 19.5 %collective-permute-done.18 = bf16[1024,1024]{1,0:T(8,128)(2,1)} collective-permute-done((bf16[1024,1024]{1,0:T(8,128)(2,1)}, bf16[1024,1024]{1,0:T(8,128)(2,1)}, u32[]{:S(2)}, u32[]{:S(2)}) %collective-permute-start.18) | collective-permute-done | bytes 2097184 | tf_op jit(solution)/shard_map/ppermute | solution.py:46
  208.2 2.5 add_convert_fusion
  210.8 1.9 pad_maximum_fusion
  212.7 6.9 %convolution_convert_fusion = bf16[1024,2048]{1,0:T(8,128)(2,1)} fusion(bf16[528,2048]{1,0:T(8,128)(2,1)} %copy-done.53, f32[528,1024]{1,0:T(8,128)S(1)} %get-tuple-element.110, f32[1024]{0:T(1024)S(1)} %copy-done.39, f32[1024]{0:T(1024)S(1)} %get-tuple-element.125, f32[528]{0:T(1024)S(1)} %add_rsqrt_fusion, f32[528]{0:T(1024)S(1)} %broadcast_multiply_fusion.4), kind=kOutput, calls=%fused_computation.10 | convolution fusion | flops 2219393024 | bytes 8532096 | tf_op jit(solution)/shard_map/dot_general | solution.py:41
  219.7 6.4 %fusion.43 = bf16[528,1024]{1,0:T(8,128)(2,1)} fusion(bf16[528,2048]{1,0:T(8,128)(2,1)} %get-tuple-element.144, bf16[1024,4096]{1,0:T(8,128)(2,1)} %all-gather.7.cloned.1.call-done), kind=kOutput, calls=%fused_computation.71 | convolution fusion | flops 2215133184 | bytes 7438336 | tf_op jit(solution)/shard_map/dot_general | solution.py:41
  228.1 14.9 %shard_map.291 = (bf16[528,256]{1,0:T(8,128)(2,1)}, f32[2,528,256]{2,1,0:T(8,128)}, bf16[2,528,256]{2,1,0:T(8,128)(2,1)}) custom-call(s32[2]{0:T(128)} %and_select_fusion.1.refs_0_, bf16[528,512]{1,0:T(8,128)(2,1)} %fusion.46.refs_1_, bf16[528,512]{1,0:T(8,128)(2,1)} %convolution_convert_fusion.6.refs_2_, bf16[528,1024]{1,0:T(8,128)(2,1)} %copy-done.9, ...), custom_call_target="tpu_custom_call" | custom-call | flops 1427374080 | bytes 4055040 | tf_op jit(solution)/shard_map/pallas_call | solution.py:224
  243.0 1.7 collective-permute-start.12
  244.7 14.7 %shard_map.290 = (bf16[528,256]{1,0:T(8,128)(2,1)}, f32[2,528,256]{2,1,0:T(8,128)}, bf16[2,528,256]{2,1,0:T(8,128)(2,1)}) custom-call(s32[2]{0:T(128)} %and_select_fusion.1.refs_0_, bf16[528,512]{1,0:T(8,128)(2,1)} %fusion.46.refs_1_, bf16[528,512]{1,0:T(8,128)(2,1)} %convolution_convert_fusion.6.refs_2_, bf16[528,1024]{1,0:T(8,128)(2,1)} %copy-done.9, ...), custom_call_target="tpu_custom_call" | custom-call | flops 1427374080 | bytes 4055040 | tf_op jit(solution)/shard_map/pallas_call | solution.py:224
  261.3 9.8 %collective-permute-done.13 = bf16[2,528,256]{2,1,0:T(8,128)(2,1)S(1)} collective-permute-done((bf16[2,528,256]{2,1,0:T(8,128)(2,1)}, bf16[2,528,256]{2,1,0:T(8,128)(2,1)S(1)}, u32[]{:S(2)}, u32[]{:S(2)}) %collective-permute-start.13) | collective-permute-done | bytes 540704 | tf_op jit(solution)/shard_map/ppermute | solution.py:104
  273.2 4.3 %convolution_convert_fusion.1 = bf16[1024,1536]{1,0:T(8,128)(2,1)} fusion(bf16[528,1536]{1,0:T(8,128)(2,1)S(1)} %bitcast_dynamic-update-slice_fusion, bf16[1,528,1024]{2,1,0:T(8,128)(2,1)S(1)} %copy-done.3, f32[1024]{0:T(1024)S(1)} %copy-done.38, f32[1024]{0:T(1024)S(1)} %copy-done.31, f32[528]{0:T(1024)S(1)} %copy-done.34, ...), kind=kOutput, calls=%fused_computation.11 | convolution fusion | flops 1665761280 | bytes 5861504 | tf_op jit(solution)/shard_map/dot_general | solution.py:41
  277.5 2.3 copy.74
  280.1 4.3 %multiply_reduce_fusion = (bf16[1024]{0:T(1024)(128)(2,1)S(1)}, bf16[1024]{0:T(1024)(128)(2,1)S(1)}, bf16[1,528,1024]{2,1,0:T(8,128)(2,1)}) fusion(bf16[528,1024]{1,0:T(8,128)(2,1)} %collective-permute-done.10, bf16[528,1024]{1,0:T(8,128)(2,1)} %fusion.43, f32[1,528,1024]{2,1,0:T(8,128)} %param.33, f32[1024]{0:T(1024)S(1)} %copy-done.35, ...), kind=kLoop, calls=%fused_computation.45 | loop fusion | flops 6486016 | bytes 7583808 | tf_op jit(solution)/shard_map/reduce_sum | solution.py:411
  284.8 4.4 %fusion.73 = (bf16[1024]{0:T(1024)(128)(2,1)S(1)}, bf16[1024]{0:T(1024)(128)(2,1)S(1)}, bf16[528,1024]{1,0:T(8,128)(2,1)S(1)}) fusion(f32[528]{0:T(1024)S(1)} %copy-done.34, f32[528]{0:T(1024)S(1)} %broadcast_multiply_fusion.5, bf16[1,528,1024]{2,1,0:T(8,128)(2,1)S(1)} %copy-done.3, bf16[528,1536]{1,0:T(8,128)(2,1)} %copy-done.29, ...), kind=kOutput, calls=%fused_computation.168 | convolution fusion | flops 1671018496 | bytes 6938752 | tf_op jit(solution)/shard_map/dot_general | solution.py:41
  289.1 1.6 collective-permute-start.14
  292.1 10.3 %all_to_all.6 = bf16[8,2,704]{2,1,0:T(2,128)(2,1)S(1)} all-to-all(bf16[8,2,704]{2,1,0:T(2,128)(2,1)S(1)} %reshape.450), channel_id=1, replica_groups=mesh['fsdp'=8,'ctx'=2,'tp'=2] {'fsdp'}, dimensions={0} | all-to-all | bytes 45056 | tf_op jit(solution)/shard_map/all_to_all | solution.py:465
  303.3 2.9 collective-permute-done.15
  308.6 2.9 collective-permute-done.16
  315.0 10.3 %collective-permute-done.19 = bf16[128,1536]{1,0:T(8,128)(2,1)} collective-permute-done((bf16[128,1536]{1,0:T(8,128)(2,1)}, bf16[128,1536]{1,0:T(8,128)(2,1)}, u32[]{:S(2)}, u32[]{:S(2)}) %collective-permute-start.19) | collective-permute-done | bytes 393248 | tf_op jit(solution)/shard_map/ppermute | solution.py:46
  327.4 4.6 %collective-permute-done.17 = bf16[128,2048]{1,0:T(8,128)(2,1)S(1)} collective-permute-done((bf16[128,2048]{1,0:T(8,128)(2,1)}, bf16[128,2048]{1,0:T(8,128)(2,1)S(1)}, u32[]{:S(2)}, u32[]{:S(2)}) %collective-permute-start.17) | collective-permute-done | bytes 524320 | tf_op jit(solution)/shard_map/ppermute | solution.py:46
  333.1 12.6 %reduce-scatter.4.cloned.1.call-done = bf16[128,1536]{1,0:T(8,128)(2,1)} async-done(((bf16[1024,1536]{1,0:T(8,128)(2,1)}), bf16[128,1536]{1,0:T(8,128)(2,1)}) %reduce-scatter.4.cloned.1.call-update) | async-done | bytes 393232 | tf_op jit(solution)/shard_map/reduce_scatter | solution.py:357
  347.3 3.5 fusion.52
  350.7 2.6 copy.83
  (240 shorter events, 44.8 us)
Async XLA Ops:
  7.2 54.1 %all-gather.5.cloned.1.call-start = ((), (), s32[]{:S(2)}) async-start(), calls=%async_computation.4 | async-start | bytes 2359296 | tf_op jit(solution)/shard_map/all_gather | solution.py:310
  9.2 131.7 %all-gather.7.cloned.1.call-start = ((), (), s32[]{:S(2)}) async-start(), calls=%async_computation.5 | async-start | bytes 8912896 | tf_op jit(solution)/shard_map/all_gather | solution.py:318
  9.2 12.5 %copy-start.40 = (bf16[2,8,8]{2,1,0:T(8,128)(2,1)S(1)}, bf16[2,8,8]{2,1,0:T(8,128)(2,1)}, u32[]{:S(2)}) copy-start(bf16[2,8,8]{2,1,0:T(8,128)(2,1)} %param.22) | copy-start | bytes 772
  9.2 12.5 %copy-start.41 = (bf16[32,8]{0,1:T(8,128)(2,1)S(1)}, bf16[32,8]{0,1:T(8,128)(2,1)}, u32[]{:S(2)}) copy-start(bf16[32,8]{0,1:T(8,128)(2,1)} %param.29) | copy-start | bytes 1540
  9.3 12.7 %copy-start.43 = (bf16[128]{0:T(256)(128)(2,1)S(1)}, bf16[128]{0:T(256)(128)(2,1)}, u32[]{:S(2)}) copy-start(bf16[128]{0:T(256)(128)(2,1)} %param.19) | copy-start | bytes 772
  9.3 12.7 %copy-start.44 = (bf16[128]{0:T(256)(128)(2,1)S(1)}, bf16[128]{0:T(256)(128)(2,1)}, u32[]{:S(2)}) copy-start(bf16[128]{0:T(256)(128)(2,1)} %param.20) | copy-start | bytes 772
  9.3 12.7 %copy-start.45 = (bf16[128]{0:T(256)(128)(2,1)S(1)}, bf16[128]{0:T(256)(128)(2,1)}, u32[]{:S(2)}) copy-start(bf16[128]{0:T(256)(128)(2,1)} %param.24) | copy-start | bytes 772
  9.3 12.7 %copy-start.46 = (bf16[128]{0:T(256)(128)(2,1)S(1)}, bf16[128]{0:T(256)(128)(2,1)}, u32[]{:S(2)}) copy-start(bf16[128]{0:T(256)(128)(2,1)} %param.25) | copy-start | bytes 772
  9.3 12.7 %copy-start.47 = (bf16[128]{0:T(256)(128)(2,1)S(1)}, bf16[128]{0:T(256)(128)(2,1)}, u32[]{:S(2)}) copy-start(bf16[128]{0:T(256)(128)(2,1)} %param.26) | copy-start | bytes 772
  9.3 12.7 %copy-start.48 = (bf16[128]{0:T(256)(128)(2,1)S(1)}, bf16[128]{0:T(256)(128)(2,1)}, u32[]{:S(2)}) copy-start(bf16[128]{0:T(256)(128)(2,1)} %param.27) | copy-start | bytes 772
  9.3 12.7 %copy-start.49 = (bf16[128]{0:T(256)(128)(2,1)S(1)}, bf16[128]{0:T(256)(128)(2,1)}, u32[]{:S(2)}) copy-start(bf16[128]{0:T(256)(128)(2,1)} %param.31) | copy-start | bytes 772
  9.3 12.7 %copy-start.50 = (bf16[128]{0:T(256)(128)(2,1)S(1)}, bf16[128]{0:T(256)(128)(2,1)}, u32[]{:S(2)}) copy-start(bf16[128]{0:T(256)(128)(2,1)} %param.32) | copy-start | bytes 772
  9.6 50.4 %copy-start.3 = (bf16[1,528,1024]{2,1,0:T(8,128)(2,1)S(1)}, bf16[1,528,1024]{2,1,0:T(8,128)(2,1)}, u32[]{:S(2)}) copy-start(bf16[1,528,1024]{2,1,0:T(8,128)(2,1)} %param.17) | copy-start | bytes 3244036
  10.7 302.1 %reduce-scatter.8.cloned.1.call-start = ((), (), s32[]{:S(2)}) async-start(), calls=%async_computation.8 | async-start | bytes 3538944 | tf_op jit(solution)/shard_map/reduce_scatter | solution.py:357
  10.9 60.0 %collective-permute-start.6 = (bf16[128,512]{1,0:T(8,128)(2,1)S(1)}, bf16[128,512]{1,0:T(8,128)(2,1)}, u32[]{:S(2)}, u32[]{:S(2)}) collective-permute-start(bf16[128,512]{1,0:T(8,128)(2,1)S(1)} %bitcast.196), channel_id=1, source_target_pairs={{0,16},{4,20},{8,24},{12,28},{16,0},{20,4},{24,8},{28,12},{1,17},{... | collective-permute-start | bytes 393224 | tf_op jit(solution)/shard_map/ppermute | solution.py:78
  15.1 55.9 %collective-permute-start.5 = (bf16[128,512]{1,0:T(8,128)(2,1)S(1)}, bf16[128,512]{1,0:T(8,128)(2,1)}, u32[]{:S(2)}, u32[]{:S(2)}) collective-permute-start(bf16[128,512]{1,0:T(8,128)(2,1)S(1)} %bitcast.197), channel_id=1, source_target_pairs={{0,8},{4,12},{8,16},{12,20},{16,24},{20,28},{24,0},{28,4},{1,9},{5... | collective-permute-start | bytes 393224 | tf_op jit(solution)/shard_map/ppermute | solution.py:78
  16.6 54.3 %collective-permute-start.7 = (bf16[128,512]{1,0:T(8,128)(2,1)S(1)}, bf16[128,512]{1,0:T(8,128)(2,1)}, u32[]{:S(2)}, u32[]{:S(2)}) collective-permute-start(bf16[128,512]{1,0:T(8,128)(2,1)S(1)} %bitcast.198), channel_id=1, source_target_pairs={{0,24},{4,28},{8,0},{12,4},{16,8},{20,12},{24,16},{28,20},{1,25},{... | collective-permute-start | bytes 393224 | tf_op jit(solution)/shard_map/ppermute | solution.py:78
  20.5 40.2 %collective-permute-start.2 = (bf16[128,512]{1,0:T(8,128)(2,1)}, bf16[128,512]{1,0:T(8,128)(2,1)S(1)}, u32[]{:S(2)}, u32[]{:S(2)}) collective-permute-start(bf16[128,512]{1,0:T(8,128)(2,1)} %get-tuple-element.116), channel_id=1, source_target_pairs={{0,24},{4,28},{8,0},{12,4},{16,8},{20,12},{24,16},{28,20},{1,25},{... | collective-permute-start | bytes 393224 | tf_op jit(solution)/shard_map/ppermute | solution.py:78
  20.5 43.9 %collective-permute-start.1 = (bf16[128,512]{1,0:T(8,128)(2,1)}, bf16[128,512]{1,0:T(8,128)(2,1)}, u32[]{:S(2)}, u32[]{:S(2)}) collective-permute-start(bf16[128,512]{1,0:T(8,128)(2,1)} %get-tuple-element.116), channel_id=1, source_target_pairs={{0,16},{4,20},{8,24},{12,28},{16,0},{20,4},{24,8},{28,12},{1,17},{... | collective-permute-start | bytes 393224 | tf_op jit(solution)/shard_map/ppermute | solution.py:78
  60.6 8.4 %collective-permute-start = (bf16[128,512]{1,0:T(8,128)(2,1)}, bf16[128,512]{1,0:T(8,128)(2,1)}, u32[]{:S(2)}, u32[]{:S(2)}) collective-permute-start(bf16[128,512]{1,0:T(8,128)(2,1)} %get-tuple-element.116), channel_id=1, source_target_pairs={{0,8},{4,12},{8,16},{12,20},{16,24},{20,28},{24,0},{28,4},{1,9},{5... | collective-permute-start | bytes 393224 | tf_op jit(solution)/shard_map/ppermute | solution.py:78
  64.3 13.1 %copy-start.9 = (bf16[528,1024]{1,0:T(8,128)(2,1)}, bf16[528,1024]{1,0:T(8,128)(2,1)S(1)}, u32[]{:S(2)}) copy-start(bf16[528,1024]{1,0:T(8,128)(2,1)S(1)} %add_convert_fusion.3.refs_2_.refs_4_.refs_3_.refs_5_) | copy-start | bytes 3244036
  64.3 31.8 %collective-permute-start.4 = (bf16[528,1024]{1,0:T(8,128)(2,1)S(1)}, bf16[528,1024]{1,0:T(8,128)(2,1)S(1)}, u32[]{:S(2)}, u32[]{:S(2)}) collective-permute-start(bf16[528,1024]{1,0:T(8,128)(2,1)S(1)} %add_convert_fusion.3.refs_2_.refs_4_.refs_3_.refs_5_), channel_id=1, source_target_pairs={{0,2},{2,0},{1,3},{3,1},{4,6},{6,4},{5,7},{7,5},{8,10},{10,8},{9,1... | collective-permute-start | bytes 3244040 | tf_op jit(solution)/shard_map/ppermute | solution.py:104
  70.9 4.2 %collective-permute-start.3 = (bf16[4,128,512]{2,1,0:T(8,128)(2,1)}, bf16[4,128,512]{2,1,0:T(8,128)(2,1)}, u32[]{:S(2)}, u32[]{:S(2)}) collective-permute-start(bf16[4,128,512]{2,1,0:T(8,128)(2,1)} %pad_maximum_fusion.1.refs_1_), channel_id=1, source_target_pairs={{0,4},{4,0},{8,12},{12,8},{16,20},{20,16},{24,28},{28,24},{1,5},{5... | collective-permute-start | bytes 1572872 | tf_op jit(solution)/shard_map/ppermute | solution.py:81
  72.8 4.6 %collective-permute-start.8 = (bf16[4,128,512]{2,1,0:T(8,128)(2,1)}, bf16[4,128,512]{2,1,0:T(8,128)(2,1)}, u32[]{:S(2)}, u32[]{:S(2)}) collective-permute-start(bf16[4,128,512]{2,1,0:T(8,128)(2,1)} %pad_maximum_fusion.2.refs_1_), channel_id=1, source_target_pairs={{0,4},{4,0},{8,12},{12,8},{16,20},{20,16},{24,28},{28,24},{1,5},{5... | collective-permute-start | bytes 1572872 | tf_op jit(solution)/shard_map/ppermute | solution.py:81
  82.5 27.2 %copy-start.13 = (bf16[1024,512]{1,0:T(8,128)(2,1)S(1)}, bf16[1024,512]{1,0:T(8,128)(2,1)}, u32[]{:S(2)}) copy-start(bf16[1024,512]{1,0:T(8,128)(2,1)} %shard_map.289) | copy-start | bytes 3145732
  112.7 25.6 %collective-permute-start.9 = (bf16[528,1024]{1,0:T(8,128)(2,1)}, bf16[528,1024]{1,0:T(8,128)(2,1)}, u32[]{:S(2)}, u32[]{:S(2)}) collective-permute-start(bf16[528,1024]{1,0:T(8,128)(2,1)} %convolution_convert_fusion.4), channel_id=1, source_target_pairs={{0,1},{1,0},{2,3},{3,2},{4,5},{5,4},{6,7},{7,6},{8,9},{9,8},{10,11... | collective-permute-start | bytes 3244040 | tf_op jit(solution)/shard_map/ppermute | solution.py:46
  155.6 24.7 %collective-permute-start.11 = (bf16[528,1024]{1,0:T(8,128)(2,1)}, bf16[528,1024]{1,0:T(8,128)(2,1)}, u32[]{:S(2)}, u32[]{:S(2)}) collective-permute-start(bf16[528,1024]{1,0:T(8,128)(2,1)} %fusion.40), channel_id=1, source_target_pairs={{0,1},{1,0},{2,3},{3,2},{4,5},{5,4},{6,7},{7,6},{8,9},{9,8},{10,11... | collective-permute-start | bytes 3244040 | tf_op jit(solution)/shard_map/ppermute | solution.py:46
  161.9 46.3 %collective-permute-start.18 = (bf16[1024,1024]{1,0:T(8,128)(2,1)}, bf16[1024,1024]{1,0:T(8,128)(2,1)}, u32[]{:S(2)}, u32[]{:S(2)}) collective-permute-start(bf16[1024,1024]{1,0:T(8,128)(2,1)} %convolution_convert_fusion.2), channel_id=1, source_target_pairs={{0,2},{2,0},{1,3},{3,1},{4,6},{6,4},{5,7},{7,5},{8,10},{10,8},{9,1... | collective-permute-start | bytes 6291464 | tf_op jit(solution)/shard_map/ppermute | solution.py:46
  166.8 16.3 %copy-start.5 = (f32[1,528,1024]{2,1,0:T(8,128)S(1)}, f32[1,528,1024]{2,1,0:T(8,128)}, u32[]{:S(2)}) copy-start(f32[1,528,1024]{2,1,0:T(8,128)} %param.33) | copy-start | bytes 6488068
  212.7 101.1 %reduce-scatter.6.cloned.1.call-start = ((), (), s32[]{:S(2)}) async-start(), calls=%async_computation.7 | async-start | bytes 4718592 | tf_op jit(solution)/shard_map/reduce_scatter | solution.py:357
  219.7 126.1 %reduce-scatter.4.cloned.1.call-start = ((), (), s32[]{:S(2)}) async-start(), calls=%async_computation.6 | async-start | bytes 3538944 | tf_op jit(solution)/shard_map/reduce_scatter | solution.py:357
  226.2 53.9 %collective-permute-start.10 = (bf16[528,1024]{1,0:T(8,128)(2,1)}, bf16[528,1024]{1,0:T(8,128)(2,1)}, u32[]{:S(2)}, u32[]{:S(2)}) collective-permute-start(bf16[528,1024]{1,0:T(8,128)(2,1)} %fusion.43), channel_id=1, source_target_pairs={{0,1},{1,0},{2,3},{3,2},{4,5},{5,4},{6,7},{7,6},{8,9},{9,8},{10,11... | collective-permute-start | bytes 3244040 | tf_op jit(solution)/shard_map/ppermute | solution.py:46
  243.0 16.9 %copy-start.24 = (bf16[528,256]{1,0:T(8,128)(2,1)S(1)}, bf16[528,256]{1,0:T(8,128)(2,1)}, u32[]{:S(2)}) copy-start(bf16[528,256]{1,0:T(8,128)(2,1)} %get-tuple-element.26) | copy-start | bytes 811012
  243.0 18.1 %copy-start.21 = (f32[2,528,256]{2,1,0:T(8,128)S(1)}, f32[2,528,256]{2,1,0:T(8,128)}, u32[]{:S(2)}) copy-start(f32[2,528,256]{2,1,0:T(8,128)} %get-tuple-element.27) | copy-start | bytes 3244036
  243.0 18.1 %collective-permute-start.12 = (bf16[2,528,256]{2,1,0:T(8,128)(2,1)}, bf16[2,528,256]{2,1,0:T(8,128)(2,1)S(1)}, u32[]{:S(2)}, u32[]{:S(2)}) collective-permute-start(bf16[2,528,256]{2,1,0:T(8,128)(2,1)} %get-tuple-element.28), channel_id=1, source_target_pairs={{0,2},{2,0},{1,3},{3,1},{4,6},{6,4},{5,7},{7,5},{8,10},{10,8},{9,1... | collective-permute-start | bytes 1622024 | tf_op jit(solution)/shard_map/ppermute | solution.py:104
  259.4 11.6 %copy-start.20 = (f32[2,528,256]{2,1,0:T(8,128)S(1)}, f32[2,528,256]{2,1,0:T(8,128)}, u32[]{:S(2)}) copy-start(f32[2,528,256]{2,1,0:T(8,128)} %get-tuple-element.29) | copy-start | bytes 3244036
  259.4 11.6 %collective-permute-start.13 = (bf16[2,528,256]{2,1,0:T(8,128)(2,1)}, bf16[2,528,256]{2,1,0:T(8,128)(2,1)S(1)}, u32[]{:S(2)}, u32[]{:S(2)}) collective-permute-start(bf16[2,528,256]{2,1,0:T(8,128)(2,1)} %get-tuple-element.30), channel_id=1, source_target_pairs={{0,2},{2,0},{1,3},{3,1},{4,6},{6,4},{5,7},{7,5},{8,10},{10,8},{9,1... | collective-permute-start | bytes 1622024 | tf_op jit(solution)/shard_map/ppermute | solution.py:104
  261.2 12.0 %copy-start.34 = (f32[528]{0:T(1024)S(1)}, f32[528]{0:T(1024)}, u32[]{:S(2)}) copy-start(f32[528]{0:T(1024)} %copy-done.32) | copy-start | bytes 6340
  261.2 11.9 %copy-start.38 = (f32[1024]{0:T(1024)S(1)}, f32[1024]{0:T(1024)}, u32[]{:S(2)}) copy-start(f32[1024]{0:T(1024)} %copy-done.36) | copy-start | bytes 12292
  289.1 25.8 %copy-start.11 = (bf16[528,1024]{1,0:T(8,128)(2,1)}, bf16[528,1024]{1,0:T(8,128)(2,1)S(1)}, u32[]{:S(2)}) copy-start(bf16[528,1024]{1,0:T(8,128)(2,1)S(1)} %get-tuple-element.112) | copy-start | bytes 3244036
  289.1 22.9 %collective-permute-start.14 = (bf16[528,1024]{1,0:T(8,128)(2,1)S(1)}, bf16[528,1024]{1,0:T(8,128)(2,1)S(1)}, u32[]{:S(2)}, u32[]{:S(2)}) collective-permute-start(bf16[528,1024]{1,0:T(8,128)(2,1)S(1)} %get-tuple-element.112), channel_id=1, source_target_pairs={{0,1},{1,0},{2,3},{3,2},{4,5},{5,4},{6,7},{7,6},{8,9},{9,8},{10,11... | collective-permute-start | bytes 3244040 | tf_op jit(solution)/shard_map/ppermute | solution.py:46
  302.6 3.7 %collective-permute-start.15 = (bf16[1408]{0:T(1024)(128)(2,1)S(1)}, bf16[1408]{0:T(1024)(128)(2,1)S(1)}, u32[]{:S(2)}, u32[]{:S(2)}) collective-permute-start(bf16[1408]{0:T(1024)(128)(2,1)S(1)} %reduce_sum.222), channel_id=1, source_target_pairs={{0,2},{2,0},{1,3},{3,1},{4,6},{6,4},{5,7},{7,5},{8,10},{10,8},{9,1... | collective-permute-start | bytes 8456 | tf_op jit(solution)/shard_map/ppermute | solution.py:46
  306.2 5.2 %collective-permute-start.16 = (bf16[256]{0:T(256)(128)(2,1)S(1)}, bf16[256]{0:T(256)(128)(2,1)S(1)}, u32[]{:S(2)}, u32[]{:S(2)}) collective-permute-start(bf16[256]{0:T(256)(128)(2,1)S(1)} %slice.270), channel_id=1, source_target_pairs={{0,1},{1,0},{2,3},{3,2},{4,5},{5,4},{6,7},{7,6},{8,9},{9,8},{10,11... | collective-permute-start | bytes 1544 | tf_op jit(solution)/shard_map/ppermute | solution.py:46
  312.8 12.4 %collective-permute-start.19 = (bf16[128,1536]{1,0:T(8,128)(2,1)}, bf16[128,1536]{1,0:T(8,128)(2,1)}, u32[]{:S(2)}, u32[]{:S(2)}) collective-permute-start(bf16[128,1536]{1,0:T(8,128)(2,1)} %reduce-scatter.8.cloned.1.call-done), channel_id=1, source_target_pairs={{0,2},{2,0},{1,3},{3,1},{4,6},{6,4},{5,7},{7,5},{8,10},{10,8},{9,1... | collective-permute-start | bytes 1179656 | tf_op jit(solution)/shard_map/ppermute | solution.py:46
  313.8 18.3 %copy-start.22 = (bf16[128,2048]{1,0:T(8,128)(2,1)S(1)}, bf16[128,2048]{1,0:T(8,128)(2,1)}, u32[]{:S(2)}) copy-start(bf16[128,2048]{1,0:T(8,128)(2,1)} %reduce-scatter.6.cloned.1.call-done) | copy-start | bytes 1572868
  313.8 18.3 %collective-permute-start.17 = (bf16[128,2048]{1,0:T(8,128)(2,1)}, bf16[128,2048]{1,0:T(8,128)(2,1)S(1)}, u32[]{:S(2)}, u32[]{:S(2)}) collective-permute-start(bf16[128,2048]{1,0:T(8,128)(2,1)} %reduce-scatter.6.cloned.1.call-done), channel_id=1, source_target_pairs={{0,2},{2,0},{1,3},{3,1},{4,6},{6,4},{5,7},{7,5},{8,10},{10,8},{9,1... | collective-permute-start | bytes 1572872 | tf_op jit(solution)/shard_map/ppermute | solution.py:46
  315.0 32.3 %copy-start.8 = (f32[528,1024]{1,0:T(8,128)S(1)}, f32[528,1024]{1,0:T(8,128)}, u32[]{:S(2)}) copy-start(f32[528,1024]{1,0:T(8,128)} %copy-done.6) | copy-start | bytes 6488068
  345.8 9.4 %collective-permute-start.20 = (bf16[128,1536]{1,0:T(8,128)(2,1)}, bf16[128,1536]{1,0:T(8,128)(2,1)}, u32[]{:S(2)}, u32[]{:S(2)}) collective-permute-start(bf16[128,1536]{1,0:T(8,128)(2,1)} %reduce-scatter.4.cloned.1.call-done), channel_id=1, source_target_pairs={{0,2},{2,0},{1,3},{3,1},{4,6},{6,4},{5,7},{7,5},{8,10},{10,8},{9,1... | collective-permute-start | bytes 1179656 | tf_op jit(solution)/shard_map/ppermute | solution.py:46
  (32 other events, 138.1 us)
Sparse Core Ops, SparseCore 0:
  10.2 45.4 all-gather.4
  57.9 78.3 all-gather.6
  212.8 40.1 reduce-scatter.7
  255.2 49.5 reduce-scatter.5
  306.9 38.8 reduce-scatter.3
